TPU v7x, 512 devices: a whole 4x8x8 slice. The times are simulated.
512 devices in a mesh: gx: 16 (over z, x_lo), gy: 8 (over y), gz: 4 (over x_hi, core).
Axes of the slice: x: 4 (x_hi: 2, x_lo: 2; x = x_hi * 2 + x_lo), y: 8, z: 8, core: 2. Of those that a mesh axis runs over, the one named last changes fastest.
Arguments:
- block_input: bfloat16 [64, 64, 4096], P('gx', 'gy', 'gz'), may hold values from -6 to 6
- pre_act: bfloat16 [64, 64, 4096], P('gx', 'gy', 'gz'), may hold values from -6 to 6
- skip_grad: bfloat16 [64, 64, 4096], P('gx', 'gy', 'gz'), may hold values from -6 to 6
- pool_grad: bfloat16 [32, 32, 2048], P('gx', 'gy', 'gz'), may hold values from -6 to 6
- conv1_weight: bfloat16 [64, 1728], P('gx'), may hold values from -0.15625 to 0.15625
- conv2_weight: bfloat16 [64, 1728], P('gx'), may hold values from -0.15625 to 0.15625
Outputs:
- input_grad: bfloat16 [64, 64, 4096], P('gx', 'gy', 'gz')
- conv1_grad: float32 [64, 1728], P('gx')
- conv2_grad: float32 [64, 1728], P('gx')
All inputs are finite; a program needn't handle non-finite values.
Results may differ from a plain program's by a relative error of at most 0.0053.
Values may be sent and summed in bfloat16 or wider, within the bound.
No kernel may reach another device: no remote copies, remote signals or barrier semaphores. Data moves between devices by JAX's collectives and lax.ppermute only.
A program may use at most 64 MiB of HBM per device.

v0:
```python
import math

import jax
import jax.numpy as jnp
from jax import lax
from jax.sharding import PartitionSpec as P


def padded_2(block, sides, width):
    for axis, dim in sides:
        count = lax.axis_size(axis)
        forward = [(i, i + 1) for i in range(count - 1)]
        forward.append((count - 1, 0))
        backward = [(target, source) for source, target in forward]
        low = lax.ppermute(
            lax.slice_in_dim(block, block.shape[dim] - width, None, axis=dim), axis, forward
        )
        high = lax.ppermute(lax.slice_in_dim(block, 0, width, axis=dim), axis, backward)
        block = jnp.concatenate([low, block, high], axis=dim)
    return block


def offset_of(k):
    return (k // 9 - 1, k // 3 % 3 - 1, k % 3 - 1)


def silu_slope(v):
    g = jax.nn.sigmoid(v)
    return g * (1.0 + v * (1.0 - g))


def window(padded, start, shape):
    lower = (start[0], start[1], start[2], 0)
    upper = (start[0] + shape[0], start[1] + shape[1], start[2] + shape[2], padded.shape[3])
    return lax.slice(padded, lower, upper).reshape(-1, padded.shape[3])


def transpose_conv(weight, padded, margin, shape):
    chans = weight.shape[0]
    total = None
    for k in range(27):
        d = offset_of(k)
        behind = window(padded, (margin - d[0], margin - d[1], margin - d[2]), shape)
        block = weight[:, k * chans : (k + 1) * chans]
        term = lax.dot_general(
            behind, block, (((1,), (0,)), ((), ())), preferred_element_type=jnp.float32
        )
        total = term if total is None else total + term
    return total


def weight_grad(left_flat, padded, margin, shape):
    pieces = []
    for k in range(27):
        d = offset_of(k)
        ahead = window(padded, (margin + d[0], margin + d[1], margin + d[2]), shape)
        pieces.append(
            lax.dot_general(
                left_flat, ahead, (((0,), (0,)), ((), ())), preferred_element_type=jnp.float32
            )
        )
    return jnp.concatenate(pieces, axis=1)


def body(block_input, pre_act, skip_grad, pool_grad, conv1_weight, conv2_weight):
    chans = conv1_weight.shape[1] // 27
    size_x, size_y, merged = block_input.shape
    size_z = merged // chans
    inner = (size_x, size_y, size_z)
    four_shape = (size_x, size_y, size_z, chans)
    weight_one, weight_two = (
        lax.all_gather(conv1_weight, "gx", axis=0, tiled=True),
        lax.all_gather(conv2_weight, "gx", axis=0, tiled=True),
    )
    pool_four = pool_grad.reshape(size_x // 2, size_y // 2, size_z // 2, chans).astype(jnp.float32)
    upsampled = jnp.repeat(jnp.repeat(jnp.repeat(pool_four, 2, axis=0), 2, axis=1), 2, axis=2)
    out_grad = (skip_grad.reshape(four_shape).astype(jnp.float32) + 0.125 * upsampled).astype(
        jnp.bfloat16
    )
    out_flat = out_grad.reshape(-1, chans)
    input_four = block_input.reshape(four_shape)
    pre_four = pre_act.reshape(four_shape)
    stacked = jnp.concatenate([input_four, pre_four, out_grad], axis=3)
    padded = padded_2(stacked, (("gx", 0), ("gy", 1), ("gz", 2)), 1)
    input_pad = padded[..., :chans]
    act_pad = jax.nn.silu(padded[..., chans : 2 * chans].astype(jnp.float32)).astype(jnp.bfloat16)
    grad_pad = padded[..., 2 * chans :]
    grads_two = weight_grad(out_flat, act_pad, 1, inner)
    act_grad = transpose_conv(weight_two, grad_pad, 1, inner)
    slope = silu_slope(pre_four.astype(jnp.float32)).reshape(-1, chans)
    pre_grad = (act_grad * slope).astype(jnp.bfloat16).reshape(four_shape)
    pre_pad = padded_2(pre_grad, (("gx", 0), ("gy", 1), ("gz", 2)), 1)
    pre_flat = pre_grad.reshape(-1, chans)
    grads_one = weight_grad(pre_flat, input_pad, 1, inner)
    total = out_grad.astype(jnp.float32).reshape(-1, chans) + transpose_conv(
        weight_one, pre_pad, 1, inner
    )
    input_grad = total.reshape(size_x, size_y, merged).astype(jnp.bfloat16)
    cells_all = (
        inner[0]
        * inner[1]
        * inner[2]
        * lax.axis_size("gx")
        * lax.axis_size("gy")
        * lax.axis_size("gz")
    )
    scale_all = 1.0 / math.sqrt(cells_all)
    grads_one = grads_one * scale_all
    grads_two = grads_two * scale_all
    owned = chans // lax.axis_size("gx")
    summed_one, summed_two = lax.psum((grads_one, grads_two), ("gx", "gy", "gz"))
    first = lax.axis_index("gx") * owned
    conv1_grad = lax.dynamic_slice_in_dim(summed_one, first, owned, 0)
    conv2_grad = lax.dynamic_slice_in_dim(summed_two, first, owned, 0)
    return (input_grad, conv1_grad, conv2_grad)


def solution(mesh):
    in_specs = (
        P("gx", "gy", "gz"),
        P("gx", "gy", "gz"),
        P("gx", "gy", "gz"),
        P("gx", "gy", "gz"),
        P("gx", None),
        P("gx", None),
    )
    out_specs = (P("gx", "gy", "gz"), P("gx", None), P("gx", None))
    return jax.shard_map(body, mesh=mesh, in_specs=in_specs, out_specs=out_specs, check_vma=False)
```

profile of v0, /device:TPU:1, one launch (start us, length us, event | category | flops | bytes accessed | tf_op | source)
XLA Modules:
  0.0 442.2 jit_solution(9441771854849640452)
XLA Ops:
  9.0 1.0 reshape.322
  10.0 1.0 reshape.321
  11.3 12.4 %collective-permute-start.1 = (bf16[1,8,16,192]{3,2,1,0:T(8,128)(2,1)S(1)}, bf16[1,8,16,192]{3,2,1,0:T(8,128)(2,1)S(1)}, u32[]{:S(2)}, u32[]{:S(2)}) collective-permute-start(bf16[1,8,16,192]{3,2,1,0:T(8,128)(2,1)S(1)} %get-tuple-element.68), channel_id=1, source_target_pairs={{32,0},{64,32},{96,64},{128,96},{160,128},{192,160},{224,192},{256... | collective-permute-start | bytes 147464 | tf_op jit(solution)/shard_map/ppermute | solution.py:18
  23.7 1.9 collective-permute-start
  26.1 27.4 %all-gather = bf16[16,4,1728]{2,1,0:T(4,128)(2,1)S(1)} all-gather(bf16[1,4,1728]{2,1,0:T(4,128)(2,1)S(1)} %bitcast.417), channel_id=1, replica_groups=mesh['gx'=16,'gy'=8,'gz'=4] {'gx'}, dimensions={0}, use_global_device_ids=true | all-gather | bytes 235008 | tf_op jit(solution)/shard_map/all_gather | solution.py:73
  54.9 24.1 %all-gather.1 = bf16[16,4,1728]{2,1,0:T(4,128)(2,1)S(1)} all-gather(bf16[1,4,1728]{2,1,0:T(4,128)(2,1)S(1)} %bitcast.418), channel_id=1, replica_groups=mesh['gx'=16,'gy'=8,'gz'=4] {'gx'}, dimensions={0}, use_global_device_ids=true | all-gather | bytes 235008 | tf_op jit(solution)/shard_map/all_gather | solution.py:72
  80.2 5.1 %collective-permute-start.3 = (bf16[6,1,16,192]{3,2,1,0:T(8,128)(2,1)S(1)}, bf16[6,1,16,192]{3,2,1,0:T(8,128)(2,1)S(1)}, u32[]{:S(2)}, u32[]{:S(2)}) collective-permute-start(bf16[6,1,16,192]{3,2,1,0:T(8,128)(2,1)S(1)} %get-tuple-element.48), channel_id=1, source_target_pairs={{4,0},{8,4},{12,8},{16,12},{20,16},{24,20},{28,24},{0,28},{5,1},{9... | collective-permute-start | bytes 110600 | tf_op jit(solution)/shard_map/ppermute | solution.py:18
  85.3 1.9 collective-permute-start.2
  88.2 3.5 collective-permute-done.2
  91.9 18.2 %collective-permute-start.4 = (bf16[6,10,1,192]{3,2,1,0:T(2,128)(2,1)S(1)}, bf16[6,10,1,192]{3,2,1,0:T(2,128)(2,1)S(1)}, u32[]{:S(2)}, u32[]{:S(2)}) collective-permute-start(bf16[6,10,1,192]{3,2,1,0:T(2,128)(2,1)S(1)} %get-tuple-element.43), channel_id=1, source_target_pairs={{1,0},{2,1},{3,2},{0,3},{5,4},{6,5},{7,6},{4,7},{9,8},{10,9},{11,1... | collective-permute-start | bytes 69128 | tf_op jit(solution)/shard_map/ppermute | solution.py:18
  110.1 4.3 collective-permute-start.5
  138.0 1.4 pad_maximum_fusion
  140.3 1.3 fusion.103
  148.1 2.9 collective-permute-start.7
  151.7 2.3 collective-permute-start.6
  154.7 1.1 fusion.116
  162.4 2.1 collective-permute-start.9
  164.5 3.4 collective-permute-start.8
  167.9 2.4 collective-permute-done.8
  170.3 5.3 %collective-permute-start.10 = (bf16[6,10,1,64]{3,2,1,0:T(2,128)(2,1)S(1)}, bf16[6,10,1,64]{3,2,1,0:T(2,128)(2,1)S(1)}, u32[]{:S(2)}, u32[]{:S(2)}) collective-permute-start(bf16[6,10,1,64]{3,2,1,0:T(2,128)(2,1)S(1)} %get-tuple-element.89), channel_id=1, source_target_pairs={{1,0},{2,1},{3,2},{0,3},{5,4},{6,5},{7,6},{4,7},{9,8},{10,9},{11,1... | collective-permute-start | bytes 23048 | tf_op jit(solution)/shard_map/ppermute | solution.py:18
  175.6 4.3 collective-permute-start.11
  188.4 244.0 %all-reduce.3.cloned.1.call-done = (f32[64,1728]{1,0:T(8,128)}, f32[64,1728]{1,0:T(8,128)}) async-done(((f32[64,1728]{1,0:T(8,128)}, f32[64,1728]{1,0:T(8,128)}), (f32[64,1728]{1,0:T(8,128)}, f32[64,1728]{1,0:T(8,128)})) %all-reduce.3.cloned.1.call-update) | async-done | bytes 884752 | tf_op jit(solution)/shard_map/psum | solution.py:111
  432.5 1.4 constant_dynamic-slice_fusion.1
  433.9 1.4 constant_dynamic-slice_fusion
  (239 shorter events, 53.0 us)
Async XLA Ops:
  7.2 425.3 %all-reduce.3.cloned.1.call-start = ((), (), s32[]{:S(2)}) async-start(), calls=%async_computation | async-start | bytes 1835008 | tf_op jit(solution)/shard_map/psum | solution.py:111
  11.0 14.6 %copy-start.5 = (bf16[4,8,1024]{2,1,0:T(8,128)(2,1)S(1)}, bf16[4,8,1024]{2,1,0:T(8,128)(2,1)}, u32[]{:S(2)}) copy-start(bf16[4,8,1024]{2,1,0:T(8,128)(2,1)} %param.8) | copy-start | bytes 196612
  11.3 14.8 %copy-start.36 = (bf16[4,1728]{1,0:T(4,128)(2,1)S(1)}, bf16[4,1728]{1,0:T(4,128)(2,1)}, u32[]{:S(2)}) copy-start(bf16[4,1728]{1,0:T(4,128)(2,1)} %param.11) | copy-start | bytes 41476
  11.3 68.8 %collective-permute-start.1 = (bf16[1,8,16,192]{3,2,1,0:T(8,128)(2,1)S(1)}, bf16[1,8,16,192]{3,2,1,0:T(8,128)(2,1)S(1)}, u32[]{:S(2)}, u32[]{:S(2)}) collective-permute-start(bf16[1,8,16,192]{3,2,1,0:T(8,128)(2,1)S(1)} %get-tuple-element.68), channel_id=1, source_target_pairs={{32,0},{64,32},{96,64},{128,96},{160,128},{192,160},{224,192},{256... | collective-permute-start | bytes 147464 | tf_op jit(solution)/shard_map/ppermute | solution.py:18
  23.7 56.4 %collective-permute-start = (bf16[1,8,16,192]{3,2,1,0:T(8,128)(2,1)S(1)}, bf16[1,8,16,192]{3,2,1,0:T(8,128)(2,1)S(1)}, u32[]{:S(2)}, u32[]{:S(2)}) collective-permute-start(bf16[1,8,16,192]{3,2,1,0:T(8,128)(2,1)S(1)} %get-tuple-element.67), channel_id=1, source_target_pairs={{0,32},{32,64},{64,96},{96,128},{128,160},{160,192},{192,224},{224... | collective-permute-start | bytes 147464 | tf_op jit(solution)/shard_map/ppermute | solution.py:15
  53.6 1.2 copy-start.37
  53.6 25.3 %copy-start.6 = (bf16[4,8,1024]{2,1,0:T(8,128)(2,1)S(1)}, bf16[4,8,1024]{2,1,0:T(8,128)(2,1)}, u32[]{:S(2)}) copy-start(bf16[4,8,1024]{2,1,0:T(8,128)(2,1)} %param.7) | copy-start | bytes 196612
  53.8 25.3 %copy-start.7 = (bf16[4,8,1024]{2,1,0:T(8,128)(2,1)S(1)}, bf16[4,8,1024]{2,1,0:T(8,128)(2,1)}, u32[]{:S(2)}) copy-start(bf16[4,8,1024]{2,1,0:T(8,128)(2,1)} %param.6) | copy-start | bytes 196612
  80.2 7.9 %collective-permute-start.3 = (bf16[6,1,16,192]{3,2,1,0:T(8,128)(2,1)S(1)}, bf16[6,1,16,192]{3,2,1,0:T(8,128)(2,1)S(1)}, u32[]{:S(2)}, u32[]{:S(2)}) collective-permute-start(bf16[6,1,16,192]{3,2,1,0:T(8,128)(2,1)S(1)} %get-tuple-element.48), channel_id=1, source_target_pairs={{4,0},{8,4},{12,8},{16,12},{20,16},{24,20},{28,24},{0,28},{5,1},{9... | collective-permute-start | bytes 110600 | tf_op jit(solution)/shard_map/ppermute | solution.py:18
  85.3 6.3 %collective-permute-start.2 = (bf16[6,1,16,192]{3,2,1,0:T(8,128)(2,1)S(1)}, bf16[6,1,16,192]{3,2,1,0:T(8,128)(2,1)S(1)}, u32[]{:S(2)}, u32[]{:S(2)}) collective-permute-start(bf16[6,1,16,192]{3,2,1,0:T(8,128)(2,1)S(1)} %get-tuple-element.47), channel_id=1, source_target_pairs={{0,4},{4,8},{8,12},{12,16},{16,20},{20,24},{24,28},{28,0},{1,5},{5... | collective-permute-start | bytes 110600 | tf_op jit(solution)/shard_map/ppermute | solution.py:15
  91.9 23.3 %collective-permute-start.4 = (bf16[6,10,1,192]{3,2,1,0:T(2,128)(2,1)S(1)}, bf16[6,10,1,192]{3,2,1,0:T(2,128)(2,1)S(1)}, u32[]{:S(2)}, u32[]{:S(2)}) collective-permute-start(bf16[6,10,1,192]{3,2,1,0:T(2,128)(2,1)S(1)} %get-tuple-element.43), channel_id=1, source_target_pairs={{1,0},{2,1},{3,2},{0,3},{5,4},{6,5},{7,6},{4,7},{9,8},{10,9},{11,1... | collective-permute-start | bytes 69128 | tf_op jit(solution)/shard_map/ppermute | solution.py:18
  110.1 5.5 %collective-permute-start.5 = (bf16[6,10,1,192]{3,2,1,0:T(2,128)(2,1)S(1)}, bf16[6,10,1,192]{3,2,1,0:T(2,128)(2,1)S(1)}, u32[]{:S(2)}, u32[]{:S(2)}) collective-permute-start(bf16[6,10,1,192]{3,2,1,0:T(2,128)(2,1)S(1)} %get-tuple-element.44), channel_id=1, source_target_pairs={{0,1},{1,2},{2,3},{3,0},{4,5},{5,6},{6,7},{7,4},{8,9},{9,10},{10,1... | collective-permute-start | bytes 69128 | tf_op jit(solution)/shard_map/ppermute | solution.py:15
  147.3 8.4 %copy-start.2 = (bf16[4,8,16,64]{3,2,1,0:T(8,128)(2,1)S(1)}, bf16[4,8,16,64]{3,2,1,0:T(8,128)(2,1)}, u32[]{:S(2)}) copy-start(bf16[4,8,16,64]{3,2,1,0:T(8,128)(2,1)} %get-tuple-element.12) | copy-start | bytes 196612
  148.1 14.2 %collective-permute-start.7 = (bf16[1,8,16,64]{3,2,1,0:T(8,128)(2,1)}, bf16[1,8,16,64]{3,2,1,0:T(8,128)(2,1)S(1)}, u32[]{:S(2)}, u32[]{:S(2)}) collective-permute-start(bf16[1,8,16,64]{3,2,1,0:T(8,128)(2,1)} %bitcast.33), channel_id=1, source_target_pairs={{32,0},{64,32},{96,64},{128,96},{160,128},{192,160},{224,192},{256... | collective-permute-start | bytes 49160 | tf_op jit(solution)/shard_map/ppermute | solution.py:18
  151.7 10.6 %collective-permute-start.6 = (bf16[1,8,16,64]{3,2,1,0:T(8,128)(2,1)}, bf16[1,8,16,64]{3,2,1,0:T(8,128)(2,1)S(1)}, u32[]{:S(2)}, u32[]{:S(2)}) collective-permute-start(bf16[1,8,16,64]{3,2,1,0:T(8,128)(2,1)} %bitcast.31), channel_id=1, source_target_pairs={{0,32},{32,64},{64,96},{96,128},{128,160},{160,192},{192,224},{224... | collective-permute-start | bytes 49160 | tf_op jit(solution)/shard_map/ppermute | solution.py:15
  154.4 1.9 copy-start.1
  159.5 1.1 copy-start.9
  159.5 1.1 copy-start.10
  159.5 1.1 copy-start.11
  159.5 1.1 copy-start.12
  162.4 5.5 %collective-permute-start.9 = (bf16[6,1,16,64]{3,2,1,0:T(8,128)(2,1)S(1)}, bf16[6,1,16,64]{3,2,1,0:T(8,128)(2,1)S(1)}, u32[]{:S(2)}, u32[]{:S(2)}) collective-permute-start(bf16[6,1,16,64]{3,2,1,0:T(8,128)(2,1)S(1)} %get-tuple-element.100), channel_id=1, source_target_pairs={{4,0},{8,4},{12,8},{16,12},{20,16},{24,20},{28,24},{0,28},{5,1},{9... | collective-permute-start | bytes 36872 | tf_op jit(solution)/shard_map/ppermute | solution.py:18
  164.5 5.8 %collective-permute-start.8 = (bf16[6,1,16,64]{3,2,1,0:T(8,128)(2,1)S(1)}, bf16[6,1,16,64]{3,2,1,0:T(8,128)(2,1)S(1)}, u32[]{:S(2)}, u32[]{:S(2)}) collective-permute-start(bf16[6,1,16,64]{3,2,1,0:T(8,128)(2,1)S(1)} %get-tuple-element.99), channel_id=1, source_target_pairs={{0,4},{4,8},{8,12},{12,16},{16,20},{20,24},{24,28},{28,0},{1,5},{5... | collective-permute-start | bytes 36872 | tf_op jit(solution)/shard_map/ppermute | solution.py:15
  170.3 10.0 %collective-permute-start.10 = (bf16[6,10,1,64]{3,2,1,0:T(2,128)(2,1)S(1)}, bf16[6,10,1,64]{3,2,1,0:T(2,128)(2,1)S(1)}, u32[]{:S(2)}, u32[]{:S(2)}) collective-permute-start(bf16[6,10,1,64]{3,2,1,0:T(2,128)(2,1)S(1)} %get-tuple-element.89), channel_id=1, source_target_pairs={{1,0},{2,1},{3,2},{0,3},{5,4},{6,5},{7,6},{4,7},{9,8},{10,9},{11,1... | collective-permute-start | bytes 23048 | tf_op jit(solution)/shard_map/ppermute | solution.py:18
  175.6 5.2 %collective-permute-start.11 = (bf16[6,10,1,64]{3,2,1,0:T(2,128)(2,1)S(1)}, bf16[6,10,1,64]{3,2,1,0:T(2,128)(2,1)S(1)}, u32[]{:S(2)}, u32[]{:S(2)}) collective-permute-start(bf16[6,10,1,64]{3,2,1,0:T(2,128)(2,1)S(1)} %get-tuple-element.90), channel_id=1, source_target_pairs={{0,1},{1,2},{2,3},{3,0},{4,5},{5,6},{6,7},{7,4},{8,9},{9,10},{10,1... | collective-permute-start | bytes 23048 | tf_op jit(solution)/shard_map/ppermute | solution.py:15
  (27 other events, 28.4 us)
Sparse Core Ops, SparseCore 0:
  162.4 269.9 all-reduce.2
where the time goes:
time: 443 us; the launch traced here: 442 us
  waiting for transfers between devices  251 us (57%)
  starting transfers between devices  64.1 us (14%)
  blocking collectives  51.5 us (12%)
  matrix products  40.7 us (9%)
  between operations  15 us (3%)
  local copies, waits for them, and re-layouts  13.2 us (3%)
  other arithmetic  6.58 us (1%)
    psum x1, waiting for transfers between devices, body(): lax.psum((grads_one, grads_two), ('gx', 'gy', 'gz'))  244 us
    ppermute x6, starting transfers between devices, padded_2(): lax.ppermute(lax.slice_in_dim(block, 0, width, axis=dim), axis, backward)  46.1 us
    all_gather x1, blocking collectives, body(): lax.all_gather(conv2_weight, 'gx', axis=0, tiled=True)  27.4 us
    dot_general x54, matrix products, weight_grad(): lax.dot_general(left_flat, ahead, (((0,), (0,)), ((), ())), preferred_ele...  26.9 us
    all_gather x1, blocking collectives, body(): lax.all_gather(conv1_weight, 'gx', axis=0, tiled=True)  24.1 us
    ppermute x6, starting transfers between devices, padded_2(): lax.ppermute(lax.slice_in_dim(block, block.shape[dim] - width, None, axis...  18.1 us
    dot_general x54, matrix products, transpose_conv(): lax.dot_general(behind, block, (((1,), (0,)), ((), ())), preferred_elemen...  13.8 us
  transfers between devices with their start and end apart: 13, of which 5 were waited for; matrix products, arithmetic and copies ran while one was open for 5% of the time, Pallas kernels for 0%

commit v1 on v0

--- a/solution.py
+++ b/solution.py
@@ -62,16 +62,26 @@
     return jnp.concatenate(pieces, axis=1)
 
 
+def reduced(grads):
+    count = lax.axis_size("gx")
+    rows = grads.shape[0] // count
+    slots = grads.astype(jnp.bfloat16).reshape(count, rows, grads.shape[1])
+    part = lax.all_to_all(slots, "gx", 0, 0, tiled=True).astype(jnp.float32).sum(0)
+    part = lax.all_gather(part, "gz", axis=0).sum(0)
+    spread = jnp.broadcast_to(part[None], (lax.axis_size("gy"),) + part.shape)
+    return lax.all_to_all(spread, "gy", 0, 0, tiled=True).sum(0)
+
+
 def body(block_input, pre_act, skip_grad, pool_grad, conv1_weight, conv2_weight):
     chans = conv1_weight.shape[1] // 27
     size_x, size_y, merged = block_input.shape
     size_z = merged // chans
     inner = (size_x, size_y, size_z)
     four_shape = (size_x, size_y, size_z, chans)
-    weight_one, weight_two = (
-        lax.all_gather(conv1_weight, "gx", axis=0, tiled=True),
-        lax.all_gather(conv2_weight, "gx", axis=0, tiled=True),
-    )
+    both = jnp.concatenate([conv1_weight, conv2_weight], axis=1)
+    spread = jnp.broadcast_to(both[None], (lax.axis_size("gx"),) + both.shape)
+    gathered = lax.all_to_all(spread, "gx", 0, 0, tiled=True).reshape(chans, -1)
+    weight_one, weight_two = gathered[:, : 27 * chans], gathered[:, 27 * chans :]
     pool_four = pool_grad.reshape(size_x // 2, size_y // 2, size_z // 2, chans).astype(jnp.float32)
     upsampled = jnp.repeat(jnp.repeat(jnp.repeat(pool_four, 2, axis=0), 2, axis=1), 2, axis=2)
     out_grad = (skip_grad.reshape(four_shape).astype(jnp.float32) + 0.125 * upsampled).astype(
@@ -107,11 +117,8 @@
     scale_all = 1.0 / math.sqrt(cells_all)
     grads_one = grads_one * scale_all
     grads_two = grads_two * scale_all
-    owned = chans // lax.axis_size("gx")
-    summed_one, summed_two = lax.psum((grads_one, grads_two), ("gx", "gy", "gz"))
-    first = lax.axis_index("gx") * owned
-    conv1_grad = lax.dynamic_slice_in_dim(summed_one, first, owned, 0)
-    conv2_grad = lax.dynamic_slice_in_dim(summed_two, first, owned, 0)
+    summed = reduced(jnp.concatenate([grads_one, grads_two], axis=1))
+    conv1_grad, conv2_grad = summed[:, : 27 * chans], summed[:, 27 * chans :]
     return (input_grad, conv1_grad, conv2_grad)
 
 

time: 443 us -> 173 us (0.39)
  waiting for transfers between devices: 251 us -> 17 us
  blocking collectives: 51.5 us -> 8.38 us
  between operations: 15 us -> 1.72 us
  local copies, waits for them, and re-layouts: 13.2 us -> 20.1 us
  matrix products: 40.7 us -> 47.6 us
  starting transfers between devices: 64.1 us -> 70.8 us
    psum x1 -> x0, waiting for transfers between devices: 244 us -> none  [body(): lax.psum((grads_one, grads_two), ('gx', 'gy', 'gz'))]
    all_gather x2 -> x1, blocking collectives: 51.5 us -> 8.38 us  [reduced(): part = lax.all_gather(part, 'gz', axis=0).sum(0)]
    all_to_all x0 -> x3, starting transfers between devices: none -> 17.1 us  [the longest x1 6.93 us: reduced(): lax.all_to_all(slots, 'gx', 0, 0, tiled=True).astype(jnp.float32).sum(0)]
    ppermute x6, starting transfers between devices: 46.1 us -> 30.9 us  [padded_2(): lax.ppermute(lax.slice_in_dim(block, 0, width, axis=dim), axis, backward)]
    all_to_all x0 -> x3, waiting for transfers between devices: none -> 14.4 us  [the longest x1 14.4 us: reduced(): return lax.all_to_all(spread, 'gy', 0, 0, tiled=True).sum(0)]
    dot_general x54, matrix products: 26.9 us -> 34.5 us  [weight_grad(): lax.dot_general(left_flat, ahead, (((0,), (0,)), ((), ())), preferred_ele...]
    ppermute x6, waiting for transfers between devices: 6.86 us -> 0.39 us  [padded_2(): lax.ppermute(lax.slice_in_dim(block, block.shape[dim] - width, None, axis...]
    ppermute x6, starting transfers between devices: 18.1 us -> 22.8 us  [padded_2(): lax.ppermute(lax.slice_in_dim(block, block.shape[dim] - width, None, axis...]
  transfers between devices with their start and end apart: 13 -> 15, of which waited for: 5 -> 4; matrix products, arithmetic and copies ran while one was open for 5% -> 31% of each run, Pallas kernels for 0% -> 0%
where the time goes in v1:
time: 173 us; the launch traced here: 171 us
  starting transfers between devices  70.8 us (41%)
  matrix products  47.6 us (28%)
  local copies, waits for them, and re-layouts  20.1 us (12%)
  waiting for transfers between devices  17 us (10%)
  blocking collectives  8.38 us (5%)
  other arithmetic  5.66 us (3%)
    dot_general x54, matrix products, weight_grad(): lax.dot_general(left_flat, ahead, (((0,), (0,)), ((), ())), preferred_ele...  34.5 us
    ppermute x6, starting transfers between devices, padded_2(): lax.ppermute(lax.slice_in_dim(block, 0, width, axis=dim), axis, backward)  30.9 us
    ppermute x6, starting transfers between devices, padded_2(): lax.ppermute(lax.slice_in_dim(block, block.shape[dim] - width, None, axis...  22.8 us
    all_to_all x1, waiting for transfers between devices, reduced(): return lax.all_to_all(spread, 'gy', 0, 0, tiled=True).sum(0)  14.4 us
    dot_general x54, matrix products, transpose_conv(): lax.dot_general(behind, block, (((1,), (0,)), ((), ())), preferred_elemen...  13.1 us
    all_gather x1, blocking collectives, reduced(): part = lax.all_gather(part, 'gz', axis=0).sum(0)  8.38 us
    all_to_all x1, starting transfers between devices, reduced(): lax.all_to_all(slots, 'gx', 0, 0, tiled=True).astype(jnp.float32).sum(0)  6.93 us
    all_to_all x1, starting transfers between devices, reduced(): return lax.all_to_all(spread, 'gy', 0, 0, tiled=True).sum(0)  6.15 us
  transfers between devices with their start and end apart: 15, of which 4 were waited for; matrix products, arithmetic and copies ran while one was open for 31% of the time, Pallas kernels for 0%

profile of v1, /device:TPU:1, one launch (start us, length us, event | category | flops | bytes accessed | tf_op | source)
XLA Modules:
  0.0 171.3 jit_solution(5892113954592458112)
XLA Ops:
  4.7 4.1 %collective-permute-start = (bf16[1,8,16,192]{3,2,1,0:T(8,128)(2,1)S(1)}, bf16[1,8,16,192]{3,2,1,0:T(8,128)(2,1)S(1)}, u32[]{:S(2)}, u32[]{:S(2)}) collective-permute-start(bf16[1,8,16,192]{3,2,1,0:T(8,128)(2,1)S(1)} %get-tuple-element.65), channel_id=1, source_target_pairs={{0,32},{32,64},{64,96},{96,128},{128,160},{160,192},{192,224},{224... | collective-permute-start | bytes 147464 | tf_op jit(solution)/shard_map/ppermute | solution.py:15
  8.8 10.4 %collective-permute-start.1 = (bf16[1,8,16,192]{3,2,1,0:T(8,128)(2,1)S(1)}, bf16[1,8,16,192]{3,2,1,0:T(8,128)(2,1)S(1)}, u32[]{:S(2)}, u32[]{:S(2)}) collective-permute-start(bf16[1,8,16,192]{3,2,1,0:T(8,128)(2,1)S(1)} %get-tuple-element.66), channel_id=1, source_target_pairs={{32,0},{64,32},{96,64},{128,96},{160,128},{192,160},{224,192},{256... | collective-permute-start | bytes 147464 | tf_op jit(solution)/shard_map/ppermute | solution.py:18
  20.2 4.0 %all-to-all-start = ((bf16[16,4,3456]{2,1,0:T(4,128)(2,1)}), bf16[16,4,3456]{2,1,0:T(4,128)(2,1)S(1)}, u32[]{:S(2)}, u32[]{:S(2)}) async-start(bf16[16,4,3456]{2,1,0:T(4,128)(2,1)} %broadcast_in_dim.24), calls=%async_computation | async-start | bytes 884736 | tf_op jit(solution)/shard_map/all_to_all | solution.py:83
  27.1 1.5 copy.429
  28.8 3.2 %collective-permute-start.2 = (bf16[6,1,16,192]{3,2,1,0:T(8,128)(2,1)S(1)}, bf16[6,1,16,192]{3,2,1,0:T(8,128)(2,1)S(1)}, u32[]{:S(2)}, u32[]{:S(2)}) collective-permute-start(bf16[6,1,16,192]{3,2,1,0:T(8,128)(2,1)S(1)} %get-tuple-element.45), channel_id=1, source_target_pairs={{0,4},{4,8},{8,12},{12,16},{16,20},{20,24},{24,28},{28,0},{1,5},{5... | collective-permute-start | bytes 110600 | tf_op jit(solution)/shard_map/ppermute | solution.py:15
  32.0 3.8 %collective-permute-start.3 = (bf16[6,1,16,192]{3,2,1,0:T(8,128)(2,1)S(1)}, bf16[6,1,16,192]{3,2,1,0:T(8,128)(2,1)S(1)}, u32[]{:S(2)}, u32[]{:S(2)}) collective-permute-start(bf16[6,1,16,192]{3,2,1,0:T(8,128)(2,1)S(1)} %get-tuple-element.46), channel_id=1, source_target_pairs={{4,0},{8,4},{12,8},{16,12},{20,16},{24,20},{28,24},{0,28},{5,1},{9... | collective-permute-start | bytes 110600 | tf_op jit(solution)/shard_map/ppermute | solution.py:18
  37.4 4.6 %collective-permute-start.4 = (bf16[6,10,1,192]{3,2,1,0:T(2,128)(2,1)S(1)}, bf16[6,10,1,192]{3,2,1,0:T(2,128)(2,1)S(1)}, u32[]{:S(2)}, u32[]{:S(2)}) collective-permute-start(bf16[6,10,1,192]{3,2,1,0:T(2,128)(2,1)S(1)} %get-tuple-element.41), channel_id=1, source_target_pairs={{1,0},{2,1},{3,2},{0,3},{5,4},{6,5},{7,6},{4,7},{9,8},{10,9},{11,1... | collective-permute-start | bytes 69128 | tf_op jit(solution)/shard_map/ppermute | solution.py:18
  41.9 4.7 %collective-permute-start.5 = (bf16[6,10,1,192]{3,2,1,0:T(2,128)(2,1)S(1)}, bf16[6,10,1,192]{3,2,1,0:T(2,128)(2,1)S(1)}, u32[]{:S(2)}, u32[]{:S(2)}) collective-permute-start(bf16[6,10,1,192]{3,2,1,0:T(2,128)(2,1)S(1)} %get-tuple-element.42), channel_id=1, source_target_pairs={{0,1},{1,2},{2,3},{3,0},{4,5},{5,6},{6,7},{7,4},{8,9},{9,10},{10,1... | collective-permute-start | bytes 69128 | tf_op jit(solution)/shard_map/ppermute | solution.py:15
  67.9 1.5 convolution_bitcast_fusion.25
  71.9 1.3 convolution_bitcast_fusion.4
  78.2 1.4 pad_maximum_fusion
  79.6 1.5 fusion.158
  83.7 1.5 fusion.159
  98.4 2.9 %collective-permute-start.6 = (bf16[1,8,16,64]{3,2,1,0:T(8,128)(2,1)S(1)}, bf16[1,8,16,64]{3,2,1,0:T(8,128)(2,1)S(1)}, u32[]{:S(2)}, u32[]{:S(2)}) collective-permute-start(bf16[1,8,16,64]{3,2,1,0:T(8,128)(2,1)S(1)} %bitcast.530), channel_id=1, source_target_pairs={{0,32},{32,64},{64,96},{96,128},{128,160},{160,192},{192,224},{224... | collective-permute-start | bytes 49160 | tf_op jit(solution)/shard_map/ppermute | solution.py:15
  101.4 4.5 %collective-permute-start.7 = (bf16[1,8,16,64]{3,2,1,0:T(8,128)(2,1)S(1)}, bf16[1,8,16,64]{3,2,1,0:T(8,128)(2,1)S(1)}, u32[]{:S(2)}, u32[]{:S(2)}) collective-permute-start(bf16[1,8,16,64]{3,2,1,0:T(8,128)(2,1)S(1)} %bitcast.531), channel_id=1, source_target_pairs={{32,0},{64,32},{96,64},{128,96},{160,128},{192,160},{224,192},{256... | collective-permute-start | bytes 49160 | tf_op jit(solution)/shard_map/ppermute | solution.py:18
  107.4 6.9 %all-to-all-start.1 = ((bf16[16,4,3456]{2,1,0:T(4,128)(2,1)}), bf16[16,4,3456]{2,1,0:T(4,128)(2,1)S(1)}, u32[]{:S(2)}, u32[]{:S(2)}) async-start(bf16[16,4,3456]{2,1,0:T(4,128)(2,1)} %copy.457), calls=%async_computation.1 | async-start | bytes 884736 | tf_op jit(solution)/shard_map/all_to_all | solution.py:69
  114.4 3.2 %collective-permute-start.8 = (bf16[6,1,16,64]{3,2,1,0:T(8,128)(2,1)S(1)}, bf16[6,1,16,64]{3,2,1,0:T(8,128)(2,1)S(1)}, u32[]{:S(2)}, u32[]{:S(2)}) collective-permute-start(bf16[6,1,16,64]{3,2,1,0:T(8,128)(2,1)S(1)} %get-tuple-element.97), channel_id=1, source_target_pairs={{0,4},{4,8},{8,12},{12,16},{16,20},{20,24},{24,28},{28,0},{1,5},{5... | collective-permute-start | bytes 36872 | tf_op jit(solution)/shard_map/ppermute | solution.py:15
  117.6 3.5 %collective-permute-start.9 = (bf16[6,1,16,64]{3,2,1,0:T(8,128)(2,1)S(1)}, bf16[6,1,16,64]{3,2,1,0:T(8,128)(2,1)S(1)}, u32[]{:S(2)}, u32[]{:S(2)}) collective-permute-start(bf16[6,1,16,64]{3,2,1,0:T(8,128)(2,1)S(1)} %get-tuple-element.98), channel_id=1, source_target_pairs={{4,0},{8,4},{12,8},{16,12},{20,16},{24,20},{28,24},{0,28},{5,1},{9... | collective-permute-start | bytes 36872 | tf_op jit(solution)/shard_map/ppermute | solution.py:18
  121.1 1.9 %collective-permute-done.9 = bf16[6,1,16,64]{3,2,1,0:T(8,128)(2,1)S(1)} collective-permute-done((bf16[6,1,16,64]{3,2,1,0:T(8,128)(2,1)S(1)}, bf16[6,1,16,64]{3,2,1,0:T(8,128)(2,1)S(1)}, u32[]{:S(2)}, u32[]{:S(2)}) %collective-permute-start.9) | collective-permute-done | bytes 12320 | tf_op jit(solution)/shard_map/ppermute | solution.py:18
  123.3 4.3 %collective-permute-start.10 = (bf16[6,10,1,64]{3,2,1,0:T(2,128)(2,1)S(1)}, bf16[6,10,1,64]{3,2,1,0:T(2,128)(2,1)S(1)}, u32[]{:S(2)}, u32[]{:S(2)}) collective-permute-start(bf16[6,10,1,64]{3,2,1,0:T(2,128)(2,1)S(1)} %get-tuple-element.87), channel_id=1, source_target_pairs={{1,0},{2,1},{3,2},{0,3},{5,4},{6,5},{7,6},{4,7},{9,8},{10,9},{11,1... | collective-permute-start | bytes 23048 | tf_op jit(solution)/shard_map/ppermute | solution.py:18
  127.6 4.6 %collective-permute-start.11 = (bf16[6,10,1,64]{3,2,1,0:T(2,128)(2,1)S(1)}, bf16[6,10,1,64]{3,2,1,0:T(2,128)(2,1)S(1)}, u32[]{:S(2)}, u32[]{:S(2)}) collective-permute-start(bf16[6,10,1,64]{3,2,1,0:T(2,128)(2,1)S(1)} %get-tuple-element.88), channel_id=1, source_target_pairs={{0,1},{1,2},{2,3},{3,0},{4,5},{5,6},{6,7},{7,4},{8,9},{9,10},{10,1... | collective-permute-start | bytes 23048 | tf_op jit(solution)/shard_map/ppermute | solution.py:15
  138.9 8.4 %all-gather.1 = f32[4,4,3456]{2,1,0:T(4,128)S(1)} all-gather(f32[1,4,3456]{2,1,0:T(4,128)S(1)} %bitcast.528), channel_id=2, replica_groups=mesh['gx'=16,'gy'=8,'gz'=4] {'gz'}, dimensions={0}, use_global_device_ids=true | all-gather | bytes 276480 | tf_op jit(solution)/shard_map/all_gather | solution.py:70
  148.2 6.1 %all-to-all-start.2 = ((f32[8,4,3456]{2,1,0:T(4,128)}), f32[8,4,3456]{2,1,0:T(4,128)S(1)}, u32[]{:S(2)}, u32[]{:S(2)}) async-start(f32[8,4,3456]{2,1,0:T(4,128)} %broadcast_in_dim.25), calls=%async_computation.2 | async-start | bytes 884736 | tf_op jit(solution)/shard_map/all_to_all | solution.py:72
  156.1 14.4 %all-to-all-done.2 = f32[8,4,3456]{2,1,0:T(4,128)S(1)} async-done(((f32[8,4,3456]{2,1,0:T(4,128)}), f32[8,4,3456]{2,1,0:T(4,128)S(1)}, u32[]{:S(2)}, u32[]{:S(2)}) %all-to-all-start.2) | async-done | bytes 442400 | tf_op jit(solution)/shard_map/all_to_all | solution.py:72
  (281 shorter events, 65.4 us)
Async XLA Ops:
  4.4 14.8 %copy-start.52 = (bf16[4,1728]{1,0:T(4,128)(2,1)S(1)}, bf16[4,1728]{1,0:T(4,128)(2,1)}, u32[]{:S(2)}) copy-start(bf16[4,1728]{1,0:T(4,128)(2,1)} %param.11) | copy-start | bytes 41476
  4.4 14.8 %copy-start.53 = (bf16[4,1728]{1,0:T(4,128)(2,1)S(1)}, bf16[4,1728]{1,0:T(4,128)(2,1)}, u32[]{:S(2)}) copy-start(bf16[4,1728]{1,0:T(4,128)(2,1)} %param.10) | copy-start | bytes 41476
  4.7 19.5 %copy-start.42 = (bf16[4,8,1024]{2,1,0:T(8,128)(2,1)S(1)}, bf16[4,8,1024]{2,1,0:T(8,128)(2,1)}, u32[]{:S(2)}) copy-start(bf16[4,8,1024]{2,1,0:T(8,128)(2,1)} %param.8) | copy-start | bytes 196612
  4.7 24.0 %collective-permute-start = (bf16[1,8,16,192]{3,2,1,0:T(8,128)(2,1)S(1)}, bf16[1,8,16,192]{3,2,1,0:T(8,128)(2,1)S(1)}, u32[]{:S(2)}, u32[]{:S(2)}) collective-permute-start(bf16[1,8,16,192]{3,2,1,0:T(8,128)(2,1)S(1)} %get-tuple-element.65), channel_id=1, source_target_pairs={{0,32},{32,64},{64,96},{96,128},{128,160},{160,192},{192,224},{224... | collective-permute-start | bytes 147464 | tf_op jit(solution)/shard_map/ppermute | solution.py:15
  8.8 19.9 %collective-permute-start.1 = (bf16[1,8,16,192]{3,2,1,0:T(8,128)(2,1)S(1)}, bf16[1,8,16,192]{3,2,1,0:T(8,128)(2,1)S(1)}, u32[]{:S(2)}, u32[]{:S(2)}) collective-permute-start(bf16[1,8,16,192]{3,2,1,0:T(8,128)(2,1)S(1)} %get-tuple-element.66), channel_id=1, source_target_pairs={{32,0},{64,32},{96,64},{128,96},{160,128},{192,160},{224,192},{256... | collective-permute-start | bytes 147464 | tf_op jit(solution)/shard_map/ppermute | solution.py:18
  20.2 65.0 %all-to-all-start = ((bf16[16,4,3456]{2,1,0:T(4,128)(2,1)}), bf16[16,4,3456]{2,1,0:T(4,128)(2,1)S(1)}, u32[]{:S(2)}, u32[]{:S(2)}) async-start(bf16[16,4,3456]{2,1,0:T(4,128)(2,1)} %broadcast_in_dim.24), calls=%async_computation | async-start | bytes 884736 | tf_op jit(solution)/shard_map/all_to_all | solution.py:83
  28.8 8.0 %collective-permute-start.2 = (bf16[6,1,16,192]{3,2,1,0:T(8,128)(2,1)S(1)}, bf16[6,1,16,192]{3,2,1,0:T(8,128)(2,1)S(1)}, u32[]{:S(2)}, u32[]{:S(2)}) collective-permute-start(bf16[6,1,16,192]{3,2,1,0:T(8,128)(2,1)S(1)} %get-tuple-element.45), channel_id=1, source_target_pairs={{0,4},{4,8},{8,12},{12,16},{16,20},{20,24},{24,28},{28,0},{1,5},{5... | collective-permute-start | bytes 110600 | tf_op jit(solution)/shard_map/ppermute | solution.py:15
  32.0 5.1 %collective-permute-start.3 = (bf16[6,1,16,192]{3,2,1,0:T(8,128)(2,1)S(1)}, bf16[6,1,16,192]{3,2,1,0:T(8,128)(2,1)S(1)}, u32[]{:S(2)}, u32[]{:S(2)}) collective-permute-start(bf16[6,1,16,192]{3,2,1,0:T(8,128)(2,1)S(1)} %get-tuple-element.46), channel_id=1, source_target_pairs={{4,0},{8,4},{12,8},{16,12},{20,16},{24,20},{28,24},{0,28},{5,1},{9... | collective-permute-start | bytes 110600 | tf_op jit(solution)/shard_map/ppermute | solution.py:18
  37.4 10.7 %collective-permute-start.4 = (bf16[6,10,1,192]{3,2,1,0:T(2,128)(2,1)S(1)}, bf16[6,10,1,192]{3,2,1,0:T(2,128)(2,1)S(1)}, u32[]{:S(2)}, u32[]{:S(2)}) collective-permute-start(bf16[6,10,1,192]{3,2,1,0:T(2,128)(2,1)S(1)} %get-tuple-element.41), channel_id=1, source_target_pairs={{1,0},{2,1},{3,2},{0,3},{5,4},{6,5},{7,6},{4,7},{9,8},{10,9},{11,1... | collective-permute-start | bytes 69128 | tf_op jit(solution)/shard_map/ppermute | solution.py:18
  41.9 6.1 %collective-permute-start.5 = (bf16[6,10,1,192]{3,2,1,0:T(2,128)(2,1)S(1)}, bf16[6,10,1,192]{3,2,1,0:T(2,128)(2,1)S(1)}, u32[]{:S(2)}, u32[]{:S(2)}) collective-permute-start(bf16[6,10,1,192]{3,2,1,0:T(2,128)(2,1)S(1)} %get-tuple-element.42), channel_id=1, source_target_pairs={{0,1},{1,2},{2,3},{3,0},{4,5},{5,6},{6,7},{7,4},{8,9},{9,10},{10,1... | collective-permute-start | bytes 69128 | tf_op jit(solution)/shard_map/ppermute | solution.py:15
  81.2 1.3 copy-start.47
  81.2 1.3 copy-start.48
  81.2 1.3 copy-start.49
  81.2 1.3 copy-start.50
  85.2 1.5 copy-start.35
  85.4 1.6 copy-start.25
  98.4 16.0 %collective-permute-start.6 = (bf16[1,8,16,64]{3,2,1,0:T(8,128)(2,1)S(1)}, bf16[1,8,16,64]{3,2,1,0:T(8,128)(2,1)S(1)}, u32[]{:S(2)}, u32[]{:S(2)}) collective-permute-start(bf16[1,8,16,64]{3,2,1,0:T(8,128)(2,1)S(1)} %bitcast.530), channel_id=1, source_target_pairs={{0,32},{32,64},{64,96},{96,128},{128,160},{160,192},{192,224},{224... | collective-permute-start | bytes 49160 | tf_op jit(solution)/shard_map/ppermute | solution.py:15
  101.4 12.9 %collective-permute-start.7 = (bf16[1,8,16,64]{3,2,1,0:T(8,128)(2,1)S(1)}, bf16[1,8,16,64]{3,2,1,0:T(8,128)(2,1)S(1)}, u32[]{:S(2)}, u32[]{:S(2)}) collective-permute-start(bf16[1,8,16,64]{3,2,1,0:T(8,128)(2,1)S(1)} %bitcast.531), channel_id=1, source_target_pairs={{32,0},{64,32},{96,64},{128,96},{160,128},{192,160},{224,192},{256... | collective-permute-start | bytes 49160 | tf_op jit(solution)/shard_map/ppermute | solution.py:18
  107.4 31.3 %all-to-all-start.1 = ((bf16[16,4,3456]{2,1,0:T(4,128)(2,1)}), bf16[16,4,3456]{2,1,0:T(4,128)(2,1)S(1)}, u32[]{:S(2)}, u32[]{:S(2)}) async-start(bf16[16,4,3456]{2,1,0:T(4,128)(2,1)} %copy.457), calls=%async_computation.1 | async-start | bytes 884736 | tf_op jit(solution)/shard_map/all_to_all | solution.py:69
  114.4 6.7 %collective-permute-start.8 = (bf16[6,1,16,64]{3,2,1,0:T(8,128)(2,1)S(1)}, bf16[6,1,16,64]{3,2,1,0:T(8,128)(2,1)S(1)}, u32[]{:S(2)}, u32[]{:S(2)}) collective-permute-start(bf16[6,1,16,64]{3,2,1,0:T(8,128)(2,1)S(1)} %get-tuple-element.97), channel_id=1, source_target_pairs={{0,4},{4,8},{8,12},{12,16},{16,20},{20,24},{24,28},{28,0},{1,5},{5... | collective-permute-start | bytes 36872 | tf_op jit(solution)/shard_map/ppermute | solution.py:15
  117.6 5.5 %collective-permute-start.9 = (bf16[6,1,16,64]{3,2,1,0:T(8,128)(2,1)S(1)}, bf16[6,1,16,64]{3,2,1,0:T(8,128)(2,1)S(1)}, u32[]{:S(2)}, u32[]{:S(2)}) collective-permute-start(bf16[6,1,16,64]{3,2,1,0:T(8,128)(2,1)S(1)} %get-tuple-element.98), channel_id=1, source_target_pairs={{4,0},{8,4},{12,8},{16,12},{20,16},{24,20},{28,24},{0,28},{5,1},{9... | collective-permute-start | bytes 36872 | tf_op jit(solution)/shard_map/ppermute | solution.py:18
  123.3 9.2 %collective-permute-start.10 = (bf16[6,10,1,64]{3,2,1,0:T(2,128)(2,1)S(1)}, bf16[6,10,1,64]{3,2,1,0:T(2,128)(2,1)S(1)}, u32[]{:S(2)}, u32[]{:S(2)}) collective-permute-start(bf16[6,10,1,64]{3,2,1,0:T(2,128)(2,1)S(1)} %get-tuple-element.87), channel_id=1, source_target_pairs={{1,0},{2,1},{3,2},{0,3},{5,4},{6,5},{7,6},{4,7},{9,8},{10,9},{11,1... | collective-permute-start | bytes 23048 | tf_op jit(solution)/shard_map/ppermute | solution.py:18
  127.6 5.4 %collective-permute-start.11 = (bf16[6,10,1,64]{3,2,1,0:T(2,128)(2,1)S(1)}, bf16[6,10,1,64]{3,2,1,0:T(2,128)(2,1)S(1)}, u32[]{:S(2)}, u32[]{:S(2)}) collective-permute-start(bf16[6,10,1,64]{3,2,1,0:T(2,128)(2,1)S(1)} %get-tuple-element.88), channel_id=1, source_target_pairs={{0,1},{1,2},{2,3},{3,0},{4,5},{5,6},{6,7},{7,4},{8,9},{9,10},{10,1... | collective-permute-start | bytes 23048 | tf_op jit(solution)/shard_map/ppermute | solution.py:15
  148.2 22.4 %all-to-all-start.2 = ((f32[8,4,3456]{2,1,0:T(4,128)}), f32[8,4,3456]{2,1,0:T(4,128)S(1)}, u32[]{:S(2)}, u32[]{:S(2)}) async-start(f32[8,4,3456]{2,1,0:T(4,128)} %broadcast_in_dim.25), calls=%async_computation.2 | async-start | bytes 884736 | tf_op jit(solution)/shard_map/all_to_all | solution.py:72
  (45 other events, 45.5 us)

commit v2 on v0

v2 whole, which is shorter than its diff:
```python
import functools
import math

import jax
import jax.numpy as jnp
from jax import lax
from jax.experimental import pallas as pl
from jax.experimental.pallas import tpu as pltpu
from jax.sharding import PartitionSpec as P

F32, B16 = jnp.float32, jnp.bfloat16
SX, SY, SZ, CH = 4, 8, 16, 64
LANES = SZ * CH
ROWS = 16 * (SX + 5)
WIDE = LANES + 6 * CH
BAND = 6 * CH
DEPTH = 9 * BAND
OWN = 16 * 3
HALO_ROWS = 16 * (SX + 3)
LAYERS = 20


def vmem():
    return pl.BlockSpec(memory_space=pltpu.VMEM)


def call(kernel, outs, scratch, flops, moved, *args):
    return pl.pallas_call(
        kernel,
        out_shape=[jax.ShapeDtypeStruct(shape, dtype) for shape, dtype in outs],
        in_specs=[vmem()] * len(args),
        out_specs=[vmem()] * len(outs),
        scratch_shapes=[pltpu.VMEM(shape, dtype) for shape, dtype in scratch],
        compiler_params=pltpu.CompilerParams(vmem_limit_bytes=48 * 1024 * 1024),
        cost_estimate=pl.CostEstimate(flops=flops, bytes_accessed=moved, transcendentals=0),
    )(*args)


def low_half(shape):
    return lax.broadcasted_iota(jnp.int32, shape, len(shape) - 1) % 128 < 64


def prep_kernel(skip, pool, pre, inp, grad, low, high, up):
    for px in range(SX // 2):
        pieces = []
        for j in range(LANES // 256):
            v = pool[px, :, 128 * j : 128 * (j + 1)].astype(F32)
            turned = pltpu.roll(v, 64, 1)
            first = low_half(v.shape)
            pieces += [jnp.where(first, v, turned), jnp.where(first, turned, v)]
        for y in range(SY):
            for j, piece in enumerate(pieces):
                up[px, y : y + 1, 128 * j : 128 * (j + 1)] = piece[y // 2 : y // 2 + 1, :]
    for x in range(SX):
        value = (skip[x].astype(F32) + 0.125 * up[x // 2]).astype(B16)
        grad[x] = value
        if x < 2:
            low[x] = value
        else:
            high[x - 2] = value
    low[2], low[3] = pre[0], inp[0]
    high[2], high[3] = pre[SX - 1], inp[SX - 1]


def layer_list(grad, pre, inp, xlo, xhi):
    def own(ref):
        return [(ref, x) for x in range(SX)]

    return (
        [(xlo, 0), (xlo, 1)] + own(grad) + [(xhi, 0), (xhi, 1)]
        + [(xlo, 2)] + own(pre) + [(xhi, 2)]
        + [(xlo, 3)] + own(inp) + [(xhi, 3)]
    )


def ypack_kernel(grad, pre, inp, xlo, xhi, low, high):
    for at, (ref, x) in enumerate(layer_list(grad, pre, inp, xlo, xhi)):
        value = ref[x].astype(F32)
        low[at] = value[0:2].astype(B16)
        high[at] = value[SY - 2 : SY].astype(B16)


def zpack_kernel(grad, pre, inp, xlo, xhi, ylo, yhi, low, high, held):
    for out, lane in ((low, 0), (high, LANES - 128)):
        for at, (ref, x) in enumerate(layer_list(grad, pre, inp, xlo, xhi)):
            held[at, 0:2] = ylo[at, :, lane : lane + 128].astype(F32)
            held[at, 2:10] = ref[x, :, lane : lane + 128].astype(F32)
            held[at, 10:12] = yhi[at, :, lane : lane + 128].astype(F32)
        out[...] = held[...].astype(B16)


def bands_kernel(weights, one, two, flat, turned):
    count, rows = weights.shape[0], weights.shape[1]
    flat[...] = jnp.zeros_like(flat)
    for g in range(count):
        flat[g * rows : (g + 1) * rows, 256 : 256 + 54 * CH] = weights[g].astype(F32)
    turned[...] = pltpu.roll(flat[...], flat.shape[1] - 64, 1)
    block = lax.broadcasted_iota(jnp.int32, (CH, 256), 1) // CH
    for which, out in enumerate((one, two)):
        for m in range(9):
            for a in range(6):
                at = 4 + 27 * which + 3 * m + 2 - a
                source = turned if at % 2 else flat
                lane = at // 2 * 128
                valid = (block + 2 - a >= 0) & (block - a <= 0)
                value = jnp.where(valid, source[:, lane : lane + 256], 0.0)
                out[m * BAND + a * CH : m * BAND + (a + 1) * CH, :] = value.astype(B16)


def fill(field, layers, first, x0, ylo, yhi, zlo, zhi):
    field[...] = jnp.zeros_like(field)
    for j, (ref, x) in enumerate(layers):
        at, row = first + j, 16 * (x0 + j + 1)
        field[row : row + 8, 128 : 128 + LANES] = ref[x].astype(F32)
        field[row - 2 : row, 128 : 128 + LANES] = ylo[at].astype(F32)
        field[row + 8 : row + 10, 128 : 128 + LANES] = yhi[at].astype(F32)
        for side, lane in ((zlo, 0), (zhi, 128 + LANES)):
            value = side[at].astype(F32)
            field[row - 2 : row, lane : lane + 128] = value[0:2]
            field[row : row + 8, lane : lane + 128] = value[2:10]
            field[row + 8 : row + 10, lane : lane + 128] = value[10:12]


def spread(value, steps, sign):
    moved = pltpu.roll(value, 64, 1)
    for i, dy in enumerate((-1, 0, 1)):
        by = (-sign * dy) % ROWS
        steps[i] = (pltpu.roll(moved, by, 0) if by else moved).astype(B16)


def own_columns(steps, columns, sign):
    for m in range(9):
        dx, dy = m // 3 - 1, m % 3
        row = OWN + sign * 16 * dx
        for h in range(4):
            columns[64 * h : 64 * (h + 1), BAND * m : BAND * (m + 1)] = steps[
                dy, row : row + 64, 256 * h + 128 : 256 * h + 128 + BAND
            ]


def main_kernel(scale, grad, pre, inp, xlo, xhi, ylo, yhi, zlo, zhi, band,
                slots, pre_out, fg, fa, fi, steps, columns, many, left, left_f, grads_one, grads_two, held):
    layers = layer_list(grad, pre, inp, xlo, xhi)
    halos = (ylo, yhi, zlo, zhi)
    fill(fg, layers[0:8], 0, 0, *halos)
    fill(fa, layers[8:14], 8, 1, *halos)
    fill(fi, layers[14:20], 14, 1, *halos)
    contract = (((0,), (0,)), ((), ()))

    v = fa[...]
    spread((v * jax.nn.sigmoid(v)).astype(B16).astype(F32), steps, 1)
    own_columns(steps, columns, 1)
    left_f[...] = jnp.zeros_like(left_f)
    for h in range(4):
        for x in range(SX):
            row = 64 * h + 16 * x
            left_f[row : row + 8, :] = grad[x, :, 256 * h : 256 * (h + 1)].astype(F32)
    left[...] = left_f[...].astype(B16)
    grads_two[...] = lax.dot_general(left[...], columns[...], contract, preferred_element_type=F32)

    spread(fg[...], steps, -1)
    for m in range(9):
        dx, dy = m // 3 - 1, m % 3
        row = 16 - 16 * dx
        for h in range(5):
            many[HALO_ROWS * h : HALO_ROWS * (h + 1), BAND * m : BAND * (m + 1)] = steps[
                dy, row : row + HALO_ROWS, 256 * h : 256 * h + BAND
            ]
    held[...] = jnp.dot(many[...], band[...], preferred_element_type=F32)
    fg[...] = jnp.zeros_like(fg)
    for h in range(5):
        v = fa[16 : 16 + HALO_ROWS, 256 * h : 256 * (h + 1)]
        g = jax.nn.sigmoid(v)
        value = held[HALO_ROWS * h : HALO_ROWS * (h + 1), :] * (g * (1.0 + v * (1.0 - g)))
        fg[16 : 16 + HALO_ROWS, 256 * h : 256 * (h + 1)] = value.astype(B16).astype(F32)
    pre_out[...] = pltpu.roll(fg[...], 64, 1).astype(B16)

    spread(fi[...], steps, 1)
    own_columns(steps, columns, 1)
    inside = lax.broadcasted_iota(jnp.int32, (64, 256), 0) % 16 < 8
    for h in range(4):
        value = fg[OWN : OWN + 64, 256 * h + 128 : 256 * h + 384]
        left[64 * h : 64 * (h + 1), :] = jnp.where(inside, value, 0.0).astype(B16)
    grads_one[...] = lax.dot_general(left[...], columns[...], contract, preferred_element_type=F32)

    count, rows = slots.shape[0], slots.shape[1]

    def block(kk):
        k, source = (kk, grads_one) if kk < 27 else (kk - 27, grads_two)
        m, t = k // 3, k % 3
        same, other = [], []
        for b in range(4):
            lane = (6 * m + b + t) // 2 * 128
            piece = source[64 * b : 64 * (b + 1), lane : lane + 128]
            (same if (b + t) % 2 == kk % 2 else other).append(piece)
        return (same[0] + same[1]) + pltpu.roll(other[0] + other[1], 64, 1)

    for j in range(27):
        first, second = block(2 * j), block(2 * j + 1)
        value = jnp.where(low_half(first.shape), first, second) * scale
        for g in range(count):
            slots[g, :, 128 * j : 128 * (j + 1)] = value[g * rows : (g + 1) * rows, :].astype(B16)


def last_kernel(pre_grad, grad, band, out, steps, columns, held):
    value = pre_grad[...].astype(F32)
    for i, dy in enumerate((-1, 0, 1)):
        steps[i] = (pltpu.roll(value, dy % ROWS, 0) if dy else value).astype(B16)
    own_columns(steps, columns, -1)
    held[...] = jnp.dot(columns[...], band[...], preferred_element_type=F32)
    for h in range(4):
        for x in range(SX):
            row, lanes = 64 * h + 16 * x, slice(256 * h, 256 * (h + 1))
            out[x, :, lanes] = (held[row : row + 8, :] + grad[x, :, lanes].astype(F32)).astype(B16)


def swapped(low, high, axis):
    count = lax.axis_size(axis)
    up = [(i, (i + 1) % count) for i in range(count)]
    down = [(target, source) for source, target in up]
    return lax.ppermute(high, axis, up), lax.ppermute(low, axis, down)


def reduced(slots):
    part = lax.all_to_all(slots, "gx", 0, 0, tiled=True).astype(F32).sum(0)
    part = lax.all_gather(part, "gz", axis=0).sum(0)
    copies = jnp.broadcast_to(part[None].astype(B16), (lax.axis_size("gy"),) + part.shape)
    return lax.all_to_all(copies, "gy", 0, 0, tiled=True).astype(F32).sum(0)


def body(block_input, pre_act, skip_grad, pool_grad, conv1_weight, conv2_weight):
    count = lax.axis_size("gx")
    rows = CH // count
    cells = SX * SY * SZ * count * lax.axis_size("gy") * lax.axis_size("gz")
    message = ((4, SY, LANES), B16)
    grad, low, high = call(
        prep_kernel,
        [((SX, SY, LANES), B16), message, message],
        [((SX // 2, SY, LANES), F32)],
        100000, 400000,
        skip_grad, pool_grad, pre_act, block_input,
    )
    xlo, xhi = swapped(low, high, "gx")
    both = jnp.concatenate([conv1_weight, conv2_weight], axis=1)
    copies = jnp.broadcast_to(both[None], (count,) + both.shape)
    gathered = lax.all_to_all(copies, "gx", 0, 0, tiled=True)
    fields = (grad, pre_act, block_input, xlo, xhi)
    message = ((LAYERS, 2, LANES), B16)
    ylo, yhi = swapped(*call(ypack_kernel, [message, message], [], 100000, 600000, *fields), "gy")
    message = ((LAYERS, 12, 128), B16)
    zlo, zhi = swapped(
        *call(zpack_kernel, [message, message], [((LAYERS, 12, 128), F32)], 100000, 700000, *fields, ylo, yhi),
        "gz",
    )
    matrix = ((DEPTH, 256), B16)
    flat = ((CH, 54 * CH + 512), F32)
    band_one, band_two = call(bands_kernel, [matrix, matrix], [flat, flat], 1000000, 4000000, gathered)
    field = ((ROWS, WIDE), F32)
    steps = ((3, ROWS, WIDE), B16)
    columns = ((256, DEPTH), B16)
    slots, pre_grad = call(
        functools.partial(main_kernel, 1.0 / math.sqrt(cells)),
        [((count, rows, 54 * CH), B16), ((ROWS, WIDE), B16)],
        [
            field, field, field, steps, columns,
            ((5 * HALO_ROWS, DEPTH), B16), ((256, 256), B16), ((256, 256), F32),
            ((256, DEPTH), F32), ((256, DEPTH), F32), ((5 * HALO_ROWS, 256), F32),
        ],
        2 * 900 * 1000 * 1000, 8000000,
        *fields, ylo, yhi, zlo, zhi, band_two,
    )
    (input_grad,) = call(
        last_kernel,
        [((SX, SY, LANES), B16)],
        [steps, columns, ((256, 256), F32)],
        500000000, 4000000,
        pre_grad, grad, band_one,
    )
    summed = reduced(slots)
    return input_grad, summed[:, : 27 * CH], summed[:, 27 * CH :]


def solution(mesh):
    in_specs = (
        P("gx", "gy", "gz"),
        P("gx", "gy", "gz"),
        P("gx", "gy", "gz"),
        P("gx", "gy", "gz"),
        P("gx", None),
        P("gx", None),
    )
    out_specs = (P("gx", "gy", "gz"), P("gx", None), P("gx", None))
    return jax.shard_map(body, mesh=mesh, in_specs=in_specs, out_specs=out_specs, check_vma=False)
```

time: 443 us -> 106 us (0.24)
  waiting for transfers between devices: 251 us -> 19.2 us
  matrix products: 40.7 us -> 0 us
  blocking collectives: 51.5 us -> 28.1 us
  starting transfers between devices: 64.1 us -> 42.6 us
  between operations: 15 us -> 0.77 us
  Pallas kernels: 0 us -> 6.44 us
  local copies, waits for them, and re-layouts: 13.2 us -> 7.21 us
  other arithmetic: 6.58 us -> 1.23 us
    psum x1 -> x0, waiting for transfers between devices: 244 us -> none  [body(): lax.psum((grads_one, grads_two), ('gx', 'gy', 'gz'))]
    all_gather x2 -> x1, blocking collectives: 51.5 us -> 7.14 us  [reduced(): part = lax.all_gather(part, 'gz', axis=0).sum(0)]
    dot_general x108 -> x0, matrix products: 40.7 us -> none  [the longest x54 26.9 us: weight_grad(): lax.dot_general(left_flat, ahead, (((0,), (0,)), ((), ())), preferred_ele...]
    ppermute x12 -> x6, starting transfers between devices: 64.1 us -> 23.7 us  [swapped(): return (lax.ppermute(high, axis, up), lax.ppermute(low, axis, down))]
    all_to_all x0 -> x1, blocking collectives: none -> 20.9 us  [reduced(): part = lax.all_to_all(slots, 'gx', 0, 0, tiled=True).astype(F32).sum(0)]
    all_to_all x0 -> x2, starting transfers between devices: none -> 18.9 us  [the longest x1 11.9 us: body(): gathered = lax.all_to_all(copies, 'gx', 0, 0, tiled=True)]
    all_to_all x0 -> x2, waiting for transfers between devices: none -> 9.28 us  [the longest x1 9.28 us: reduced(): return lax.all_to_all(copies, 'gy', 0, 0, tiled=True).astype(F32).sum(0)]
    pallas_call x0 -> x6, Pallas kernels: none -> 6.44 us  [call(): pl.pallas_call(kernel, out_shape=[jax.ShapeDtypeStruct(shape, dtype) for...]
  transfers between devices with their start and end apart: 13 -> 8, of which waited for: 5 -> 5; matrix products, arithmetic and copies ran while one was open for 5% -> 0% of each run, Pallas kernels for 0% -> 2%
where the time goes in v2:
time: 106 us
  starting transfers between devices  42.6 us (40%)
  blocking collectives  28.1 us (27%)
  waiting for transfers between devices  19.2 us (18%)
  local copies, waits for them, and re-layouts  7.21 us (7%)
  Pallas kernels  6.44 us (6%)
  other arithmetic  1.23 us (1%)
    ppermute x6, starting transfers between devices, swapped(): return (lax.ppermute(high, axis, up), lax.ppermute(low, axis, down))  23.7 us
    all_to_all x1, blocking collectives, reduced(): part = lax.all_to_all(slots, 'gx', 0, 0, tiled=True).astype(F32).sum(0)  20.9 us
    all_to_all x1, starting transfers between devices, body(): gathered = lax.all_to_all(copies, 'gx', 0, 0, tiled=True)  11.9 us
    ppermute x6, waiting for transfers between devices, swapped(): return (lax.ppermute(high, axis, up), lax.ppermute(low, axis, down))  9.91 us
    all_to_all x1, waiting for transfers between devices, reduced(): return lax.all_to_all(copies, 'gy', 0, 0, tiled=True).astype(F32).sum(0)  9.28 us
    all_gather x1, blocking collectives, reduced(): part = lax.all_gather(part, 'gz', axis=0).sum(0)  7.14 us
    all_to_all x1, starting transfers between devices, reduced(): return lax.all_to_all(copies, 'gy', 0, 0, tiled=True).astype(F32).sum(0)  7.02 us
    pallas_call x6, Pallas kernels, call(): pl.pallas_call(kernel, out_shape=[jax.ShapeDtypeStruct(shape, dtype) for...  6.44 us
  transfers between devices with their start and end apart: 8, of which 5 were waited for; matrix products, arithmetic and copies ran while one was open for 0% of the time, Pallas kernels for 2%

profile of v2, /device:TPU:1, one launch (start us, length us, event | category | flops | bytes accessed | tf_op | source)
XLA Modules:
  0.0 105.5 jit_solution(5953414333704035365)
XLA Ops:
  0.7 0.8 pad_maximum_fusion
  1.5 0.9 broadcast_in_dim.4
  2.4 11.9 %all-to-all-start = ((bf16[16,4,3456]{2,1,0:T(4,128)(2,1)}), bf16[16,4,3456]{2,1,0:T(4,128)(2,1)S(1)}, u32[]{:S(2)}, u32[]{:S(2)}) async-start(bf16[16,4,3456]{2,1,0:T(4,128)(2,1)} %broadcast_in_dim.4), calls=%async_computation | async-start | bytes 884736 | tf_op jit(solution)/shard_map/all_to_all | solution.py:246
  14.3 0.8 copy-done
  15.1 0.8 copy-done.3
  16.0 0.8 copy-done.6
  17.6 3.3 %collective-permute-start = (bf16[4,8,1024]{2,1,0:T(8,128)(2,1)S(1)}, bf16[4,8,1024]{2,1,0:T(8,128)(2,1)S(1)}, u32[]{:S(2)}, u32[]{:S(2)}) collective-permute-start(bf16[4,8,1024]{2,1,0:T(8,128)(2,1)S(1)} %get-tuple-element.15), channel_id=1, source_target_pairs={{0,32},{32,64},{64,96},{96,128},{128,160},{160,192},{192,224},{224... | collective-permute-start | bytes 196616 | tf_op jit(solution)/shard_map/ppermute | solution.py:221
  20.9 4.1 %collective-permute-start.1 = (bf16[4,8,1024]{2,1,0:T(8,128)(2,1)S(1)}, bf16[4,8,1024]{2,1,0:T(8,128)(2,1)S(1)}, u32[]{:S(2)}, u32[]{:S(2)}) collective-permute-start(bf16[4,8,1024]{2,1,0:T(8,128)(2,1)S(1)} %get-tuple-element.16), channel_id=1, source_target_pairs={{32,0},{64,32},{96,64},{128,96},{160,128},{192,160},{224,192},{256... | collective-permute-start | bytes 196616 | tf_op jit(solution)/shard_map/ppermute | solution.py:221
  25.0 2.6 %collective-permute-done.xlo = bf16[4,8,1024]{2,1,0:T(8,128)(2,1)S(1)} collective-permute-done((bf16[4,8,1024]{2,1,0:T(8,128)(2,1)S(1)}, bf16[4,8,1024]{2,1,0:T(8,128)(2,1)S(1)}, u32[]{:S(2)}, u32[]{:S(2)}) %collective-permute-start) | collective-permute-done | bytes 65568 | tf_op jit(solution)/shard_map/ppermute | solution.py:221
  27.6 1.0 collective-permute-done.1.xhi
  28.6 0.8 copy-done.1
  29.5 0.8 copy-done.4
  30.3 3.2 %collective-permute-start.2 = (bf16[20,2,1024]{2,1,0:T(2,128)(2,1)S(1)}, bf16[20,2,1024]{2,1,0:T(2,128)(2,1)S(1)}, u32[]{:S(2)}, u32[]{:S(2)}) collective-permute-start(bf16[20,2,1024]{2,1,0:T(2,128)(2,1)S(1)} %get-tuple-element.17), channel_id=1, source_target_pairs={{0,4},{4,8},{8,12},{12,16},{16,20},{20,24},{24,28},{28,0},{1,5},{5... | collective-permute-start | bytes 245768 | tf_op jit(solution)/shard_map/ppermute | solution.py:221
  33.5 3.8 %collective-permute-start.3 = (bf16[20,2,1024]{2,1,0:T(2,128)(2,1)S(1)}, bf16[20,2,1024]{2,1,0:T(2,128)(2,1)S(1)}, u32[]{:S(2)}, u32[]{:S(2)}) collective-permute-start(bf16[20,2,1024]{2,1,0:T(2,128)(2,1)S(1)} %get-tuple-element.18), channel_id=1, source_target_pairs={{4,0},{8,4},{12,8},{16,12},{20,16},{24,20},{28,24},{0,28},{5,1},{9... | collective-permute-start | bytes 245768 | tf_op jit(solution)/shard_map/ppermute | solution.py:221
  37.4 1.6 %collective-permute-done.3.yhi = bf16[20,2,1024]{2,1,0:T(2,128)(2,1)S(1)} collective-permute-done((bf16[20,2,1024]{2,1,0:T(2,128)(2,1)S(1)}, bf16[20,2,1024]{2,1,0:T(2,128)(2,1)S(1)}, u32[]{:S(2)}, u32[]{:S(2)}) %collective-permute-start.3) | collective-permute-done | bytes 81952 | tf_op jit(solution)/shard_map/ppermute | solution.py:221
  39.1 7.4 %collective-permute-start.4 = (bf16[20,12,128]{2,1,0:T(8,128)(2,1)S(1)}, bf16[20,12,128]{2,1,0:T(8,128)(2,1)S(1)}, u32[]{:S(2)}, u32[]{:S(2)}) collective-permute-start(bf16[20,12,128]{2,1,0:T(8,128)(2,1)S(1)} %get-tuple-element.19), channel_id=1, source_target_pairs={{0,1},{1,2},{2,3},{3,0},{4,5},{5,6},{6,7},{7,4},{8,9},{9,10},{10,1... | collective-permute-start | bytes 184328 | tf_op jit(solution)/shard_map/ppermute | solution.py:221
  46.5 1.9 %collective-permute-start.5 = (bf16[20,12,128]{2,1,0:T(8,128)(2,1)S(1)}, bf16[20,12,128]{2,1,0:T(8,128)(2,1)S(1)}, u32[]{:S(2)}, u32[]{:S(2)}) collective-permute-start(bf16[20,12,128]{2,1,0:T(8,128)(2,1)S(1)} %get-tuple-element.20), channel_id=1, source_target_pairs={{1,0},{2,1},{3,2},{0,3},{5,4},{6,5},{7,6},{4,7},{9,8},{10,9},{11,1... | collective-permute-start | bytes 184328 | tf_op jit(solution)/shard_map/ppermute | solution.py:221
  49.1 4.7 %collective-permute-done.5.zhi = bf16[20,12,128]{2,1,0:T(8,128)(2,1)S(1)} collective-permute-done((bf16[20,12,128]{2,1,0:T(8,128)(2,1)S(1)}, bf16[20,12,128]{2,1,0:T(8,128)(2,1)S(1)}, u32[]{:S(2)}, u32[]{:S(2)}) %collective-permute-start.5) | collective-permute-done | bytes 61472 | tf_op jit(solution)/shard_map/ppermute | solution.py:221
  53.7 4.3 %shard_map.89 = (bf16[16,4,3456]{2,1,0:T(4,128)(2,1)S(1)}, bf16[144,1408]{1,0:T(8,128)(2,1)S(1)}) custom-call(bf16[4,8,1024]{2,1,0:T(8,128)(2,1)S(1)} %get-tuple-element.14.grad, bf16[4,8,1024]{2,1,0:T(8,128)(2,1)S(1)} %copy-done.2, bf16[4,8,1024]{2,1,0:T(8,128)(2,1)S(1)} %copy-done.5, bf16[4,8,1024]{2,1,0:T(8,128)(2,1)S(1)} %collective-permute-done.xlo, ...), custom_call_target="tpu_custom_call" | custom-call | flops 1800000000 | bytes 8000000 | tf_op jit(solution)/shard_map/pallas_call | solution.py:28
  58.0 20.9 %all_to_all.15 = bf16[16,4,3456]{2,1,0:T(4,128)(2,1)S(1)} all-to-all(bf16[16,4,3456]{2,1,0:T(4,128)(2,1)S(1)} %get-tuple-element.24), channel_id=1, replica_groups=mesh['gx'=16,'gy'=8,'gz'=4] {'gx'}, dimensions={0} | all-to-all | bytes 884736 | tf_op jit(solution)/shard_map/all_to_all | solution.py:225
  79.1 7.1 %all-gather.1 = f32[4,4,3456]{2,1,0:T(4,128)S(1)} all-gather(f32[1,4,3456]{2,1,0:T(4,128)S(1)} %bitcast.1), channel_id=2, replica_groups=mesh['gx'=16,'gy'=8,'gz'=4] {'gz'}, dimensions={0}, use_global_device_ids=true | all-gather | bytes 276480 | tf_op jit(solution)/shard_map/all_gather | solution.py:226
  87.0 7.0 %all-to-all-start.2 = ((bf16[8,4,3456]{2,1,0:T(4,128)(2,1)}), bf16[8,4,3456]{2,1,0:T(4,128)(2,1)S(1)}, u32[]{:S(2)}, u32[]{:S(2)}) async-start(bf16[8,4,3456]{2,1,0:T(4,128)(2,1)} %broadcast_in_dim.5), calls=%async_computation.2 | async-start | bytes 442368 | tf_op jit(solution)/shard_map/all_to_all | solution.py:228
  94.1 1.3 %shard_map.90 = bf16[4,8,1024]{2,1,0:T(8,128)(2,1)} custom-call(bf16[144,1408]{1,0:T(8,128)(2,1)S(1)} %get-tuple-element.22.pre_grad, bf16[4,8,1024]{2,1,0:T(8,128)(2,1)S(1)} %get-tuple-element.14.grad, bf16[3456,256]{1,0:T(8,128)(2,1)S(1)} %get-tuple-element.23.band), custom_call_target="tpu_custom_call" | custom-call | flops 500000000 | bytes 4000000 | tf_op jit(solution)/shard_map/pallas_call | solution.py:28
  95.4 9.3 %all-to-all-done.2 = bf16[8,4,3456]{2,1,0:T(4,128)(2,1)S(1)} async-done(((bf16[8,4,3456]{2,1,0:T(4,128)(2,1)}), bf16[8,4,3456]{2,1,0:T(4,128)(2,1)S(1)}, u32[]{:S(2)}, u32[]{:S(2)}) %all-to-all-start.2) | async-done | bytes 221216 | tf_op jit(solution)/shard_map/all_to_all | solution.py:228
  (23 shorter events, 3.4 us)
Async XLA Ops:
  0.6 53.1 %copy-start.2 = (bf16[4,8,1024]{2,1,0:T(8,128)(2,1)S(1)}, bf16[4,8,1024]{2,1,0:T(8,128)(2,1)}, u32[]{:S(2)}) copy-start(bf16[4,8,1024]{2,1,0:T(8,128)(2,1)} %pre.7) | copy-start | bytes 196612
  0.6 53.1 %copy-start.5 = (bf16[4,8,1024]{2,1,0:T(8,128)(2,1)S(1)}, bf16[4,8,1024]{2,1,0:T(8,128)(2,1)}, u32[]{:S(2)}) copy-start(bf16[4,8,1024]{2,1,0:T(8,128)(2,1)} %inp.7) | copy-start | bytes 196612
  2.4 46.0 %all-to-all-start = ((bf16[16,4,3456]{2,1,0:T(4,128)(2,1)}), bf16[16,4,3456]{2,1,0:T(4,128)(2,1)S(1)}, u32[]{:S(2)}, u32[]{:S(2)}) async-start(bf16[16,4,3456]{2,1,0:T(4,128)(2,1)} %broadcast_in_dim.4), calls=%async_computation | async-start | bytes 884736 | tf_op jit(solution)/shard_map/all_to_all | solution.py:246
  14.3 0.8 copy-start
  15.1 0.8 copy-start.3
  16.0 0.8 copy-start.6
  16.8 0.7 copy-start.7
  17.6 10.0 %collective-permute-start = (bf16[4,8,1024]{2,1,0:T(8,128)(2,1)S(1)}, bf16[4,8,1024]{2,1,0:T(8,128)(2,1)S(1)}, u32[]{:S(2)}, u32[]{:S(2)}) collective-permute-start(bf16[4,8,1024]{2,1,0:T(8,128)(2,1)S(1)} %get-tuple-element.15), channel_id=1, source_target_pairs={{0,32},{32,64},{64,96},{96,128},{128,160},{160,192},{192,224},{224... | collective-permute-start | bytes 196616 | tf_op jit(solution)/shard_map/ppermute | solution.py:221
  20.9 7.7 %collective-permute-start.1 = (bf16[4,8,1024]{2,1,0:T(8,128)(2,1)S(1)}, bf16[4,8,1024]{2,1,0:T(8,128)(2,1)S(1)}, u32[]{:S(2)}, u32[]{:S(2)}) collective-permute-start(bf16[4,8,1024]{2,1,0:T(8,128)(2,1)S(1)} %get-tuple-element.16), channel_id=1, source_target_pairs={{32,0},{64,32},{96,64},{128,96},{160,128},{192,160},{224,192},{256... | collective-permute-start | bytes 196616 | tf_op jit(solution)/shard_map/ppermute | solution.py:221
  28.6 0.8 copy-start.1
  29.5 0.8 copy-start.4
  30.3 7.0 %collective-permute-start.2 = (bf16[20,2,1024]{2,1,0:T(2,128)(2,1)S(1)}, bf16[20,2,1024]{2,1,0:T(2,128)(2,1)S(1)}, u32[]{:S(2)}, u32[]{:S(2)}) collective-permute-start(bf16[20,2,1024]{2,1,0:T(2,128)(2,1)S(1)} %get-tuple-element.17), channel_id=1, source_target_pairs={{0,4},{4,8},{8,12},{12,16},{16,20},{20,24},{24,28},{28,0},{1,5},{5... | collective-permute-start | bytes 245768 | tf_op jit(solution)/shard_map/ppermute | solution.py:221
  33.5 5.5 %collective-permute-start.3 = (bf16[20,2,1024]{2,1,0:T(2,128)(2,1)S(1)}, bf16[20,2,1024]{2,1,0:T(2,128)(2,1)S(1)}, u32[]{:S(2)}, u32[]{:S(2)}) collective-permute-start(bf16[20,2,1024]{2,1,0:T(2,128)(2,1)S(1)} %get-tuple-element.18), channel_id=1, source_target_pairs={{4,0},{8,4},{12,8},{16,12},{20,16},{24,20},{28,24},{0,28},{5,1},{9... | collective-permute-start | bytes 245768 | tf_op jit(solution)/shard_map/ppermute | solution.py:221
  39.1 10.0 %collective-permute-start.4 = (bf16[20,12,128]{2,1,0:T(8,128)(2,1)S(1)}, bf16[20,12,128]{2,1,0:T(8,128)(2,1)S(1)}, u32[]{:S(2)}, u32[]{:S(2)}) collective-permute-start(bf16[20,12,128]{2,1,0:T(8,128)(2,1)S(1)} %get-tuple-element.19), channel_id=1, source_target_pairs={{0,1},{1,2},{2,3},{3,0},{4,5},{5,6},{6,7},{7,4},{8,9},{9,10},{10,1... | collective-permute-start | bytes 184328 | tf_op jit(solution)/shard_map/ppermute | solution.py:221
  46.5 7.3 %collective-permute-start.5 = (bf16[20,12,128]{2,1,0:T(8,128)(2,1)S(1)}, bf16[20,12,128]{2,1,0:T(8,128)(2,1)S(1)}, u32[]{:S(2)}, u32[]{:S(2)}) collective-permute-start(bf16[20,12,128]{2,1,0:T(8,128)(2,1)S(1)} %get-tuple-element.20), channel_id=1, source_target_pairs={{1,0},{2,1},{3,2},{0,3},{5,4},{6,5},{7,6},{4,7},{9,8},{10,9},{11,1... | collective-permute-start | bytes 184328 | tf_op jit(solution)/shard_map/ppermute | solution.py:221
  87.0 17.6 %all-to-all-start.2 = ((bf16[8,4,3456]{2,1,0:T(4,128)(2,1)}), bf16[8,4,3456]{2,1,0:T(4,128)(2,1)S(1)}, u32[]{:S(2)}, u32[]{:S(2)}) async-start(bf16[8,4,3456]{2,1,0:T(4,128)(2,1)} %broadcast_in_dim.5), calls=%async_computation.2 | async-start | bytes 442368 | tf_op jit(solution)/shard_map/all_to_all | solution.py:228

commit v3 on v2

--- a/solution.py
+++ b/solution.py
@@ -17,21 +17,19 @@
 DEPTH = 9 * BAND
 OWN = 16 * 3
 HALO_ROWS = 16 * (SX + 3)
-LAYERS = 20
-
-
-def vmem():
-    return pl.BlockSpec(memory_space=pltpu.VMEM)
-
-
-def call(kernel, outs, scratch, flops, moved, *args):
+LAYERS = 14
+SPLIT = 4
+PART = 7 * 128
+
+
+def call(kernel, outs, scratch, flops, moved, *args, space=pltpu.VMEM, grant=48):
     return pl.pallas_call(
         kernel,
         out_shape=[jax.ShapeDtypeStruct(shape, dtype) for shape, dtype in outs],
-        in_specs=[vmem()] * len(args),
-        out_specs=[vmem()] * len(outs),
-        scratch_shapes=[pltpu.VMEM(shape, dtype) for shape, dtype in scratch],
-        compiler_params=pltpu.CompilerParams(vmem_limit_bytes=48 * 1024 * 1024),
+        in_specs=[pl.BlockSpec(memory_space=space)] * len(args),
+        out_specs=[pl.BlockSpec(memory_space=pltpu.VMEM)] * len(outs),
+        scratch_shapes=[pltpu.VMEM(*held) if isinstance(held, tuple) else held for held in scratch],
+        compiler_params=pltpu.CompilerParams(vmem_limit_bytes=grant * 1024 * 1024),
         cost_estimate=pl.CostEstimate(flops=flops, bytes_accessed=moved, transcendentals=0),
     )(*args)
 
@@ -40,7 +38,23 @@
     return lax.broadcasted_iota(jnp.int32, shape, len(shape) - 1) % 128 < 64
 
 
-def prep_kernel(skip, pool, pre, inp, grad, low, high, up):
+def prep_kernel(skip_in, pool_in, pre_in, inp_in, one_in, two_in,
+                grad, pre, inp, low, high, copies, skip, pool, one, two, up, rows, sems):
+    moves = [
+        pltpu.make_async_copy(source, target, sems.at[i])
+        for i, (source, target) in enumerate(
+            ((skip_in, skip), (pool_in, pool), (pre_in, pre), (inp_in, inp), (one_in, one), (two_in, two))
+        )
+    ]
+    for move in moves:
+        move.start()
+    for move in moves:
+        move.wait()
+    each = one.shape[0]
+    rows[0:each], rows[each : 2 * each] = one[...].astype(F32), two[...].astype(F32)
+    both = rows[...].astype(B16)
+    for g in range(copies.shape[0]):
+        copies[g] = both
     for px in range(SX // 2):
         pieces = []
         for j in range(LANES // 256):
@@ -62,44 +76,66 @@
     high[2], high[3] = pre[SX - 1], inp[SX - 1]
 
 
-def layer_list(grad, pre, inp, xlo, xhi):
+def fields_of(grad, pre, inp, xlo, xhi):
     def own(ref):
         return [(ref, x) for x in range(SX)]
 
     return (
-        [(xlo, 0), (xlo, 1)] + own(grad) + [(xhi, 0), (xhi, 1)]
-        + [(xlo, 2)] + own(pre) + [(xhi, 2)]
-        + [(xlo, 3)] + own(inp) + [(xhi, 3)]
-    )
-
-
-def ypack_kernel(grad, pre, inp, xlo, xhi, low, high):
-    for at, (ref, x) in enumerate(layer_list(grad, pre, inp, xlo, xhi)):
+        [(xlo, 0), (xlo, 1)] + own(grad) + [(xhi, 0), (xhi, 1)],
+        [(xlo, 2)] + own(pre) + [(xhi, 2)],
+        [(xlo, 3)] + own(inp) + [(xhi, 3)],
+    )
+
+
+def ypack_kernel(grad, pre, inp, xlo, xhi, low, high, held):
+    wide, acts, inputs = fields_of(grad, pre, inp, xlo, xhi)
+    for at, (ref, x) in enumerate(wide):
         value = ref[x].astype(F32)
         low[at] = value[0:2].astype(B16)
         high[at] = value[SY - 2 : SY].astype(B16)
-
-
-def zpack_kernel(grad, pre, inp, xlo, xhi, ylo, yhi, low, high, held):
-    for out, lane in ((low, 0), (high, LANES - 128)):
-        for at, (ref, x) in enumerate(layer_list(grad, pre, inp, xlo, xhi)):
-            held[at, 0:2] = ylo[at, :, lane : lane + 128].astype(F32)
-            held[at, 2:10] = ref[x, :, lane : lane + 128].astype(F32)
-            held[at, 10:12] = yhi[at, :, lane : lane + 128].astype(F32)
+    for out, row in ((low, 0), (high, SY - 1)):
+        for at, ((a, ax), (i, ix)) in enumerate(zip(acts, inputs)):
+            held[0:1] = a[ax].astype(F32)[row : row + 1]
+            held[1:2] = i[ix].astype(F32)[row : row + 1]
+            out[8 + at] = held[...].astype(B16)
+
+
+def zpack_kernel(grad, pre, inp, xlo, xhi, ylo, yhi, low, high, held, second):
+    wide, acts, inputs = fields_of(grad, pre, inp, xlo, xhi)
+    for out, lane, half in ((low, 0, True), (high, LANES - 128, False)):
+        cut = slice(lane, lane + 128)
+        for at, (ref, x) in enumerate(wide):
+            held[at, 0:2] = ylo[at, :, cut].astype(F32)
+            held[at, 2:10] = ref[x, :, cut].astype(F32)
+            held[at, 10:12] = yhi[at, :, cut].astype(F32)
+        for j, ((a, ax), (i, ix)) in enumerate(zip(acts, inputs)):
+            at = 8 + j
+            below, above = ylo[at, :, cut].astype(F32), yhi[at, :, cut].astype(F32)
+            for to, ref, x, row in ((held.at[at], a, ax, 0), (second, i, ix, 1)):
+                to[1:2] = below[row : row + 1]
+                to[2:10] = ref[x, :, cut].astype(F32)
+                to[10:11] = above[row : row + 1]
+            v, w = held[at], second[...]
+            if half:
+                w = pltpu.roll(w, 64, 1)
+            else:
+                v = pltpu.roll(v, 64, 1)
+            held[at] = jnp.where(low_half(v.shape), v, w)
         out[...] = held[...].astype(B16)
 
 
 def bands_kernel(weights, one, two, flat, turned):
-    count, rows = weights.shape[0], weights.shape[1]
-    flat[...] = jnp.zeros_like(flat)
-    for g in range(count):
-        flat[g * rows : (g + 1) * rows, 256 : 256 + 54 * CH] = weights[g].astype(F32)
-    turned[...] = pltpu.roll(flat[...], flat.shape[1] - 64, 1)
+    count, rows = weights.shape[0], weights.shape[1] // 2
     block = lax.broadcasted_iota(jnp.int32, (CH, 256), 1) // CH
     for which, out in enumerate((one, two)):
+        flat[...] = jnp.zeros_like(flat)
+        for g in range(count):
+            value = weights[g].astype(F32)[which * rows : (which + 1) * rows]
+            flat[g * rows : (g + 1) * rows, 256 : 256 + 27 * CH] = value
+        turned[...] = pltpu.roll(flat[...], flat.shape[1] - 64, 1)
         for m in range(9):
             for a in range(6):
-                at = 4 + 27 * which + 3 * m + 2 - a
+                at = 4 + 3 * m + 2 - a
                 source = turned if at % 2 else flat
                 lane = at // 2 * 128
                 valid = (block + 2 - a >= 0) & (block - a <= 0)
@@ -107,10 +143,10 @@
                 out[m * BAND + a * CH : m * BAND + (a + 1) * CH, :] = value.astype(B16)
 
 
-def fill(field, layers, first, x0, ylo, yhi, zlo, zhi):
+def fill_wide(field, layers, ylo, yhi, zlo, zhi):
     field[...] = jnp.zeros_like(field)
-    for j, (ref, x) in enumerate(layers):
-        at, row = first + j, 16 * (x0 + j + 1)
+    for at, (ref, x) in enumerate(layers):
+        row = 16 * (at + 1)
         field[row : row + 8, 128 : 128 + LANES] = ref[x].astype(F32)
         field[row - 2 : row, 128 : 128 + LANES] = ylo[at].astype(F32)
         field[row + 8 : row + 10, 128 : 128 + LANES] = yhi[at].astype(F32)
@@ -121,6 +157,23 @@
             field[row + 8 : row + 10, lane : lane + 128] = value[10:12]
 
 
+def fill_thin(field, layers, second, ylo, yhi, zlo, zhi):
+    field[...] = jnp.zeros_like(field)
+    for j, (ref, x) in enumerate(layers):
+        at, row = 8 + j, 16 * (j + 2)
+        field[row : row + 8, 128 : 128 + LANES] = ref[x].astype(F32)
+        field[row - 1 : row, 128 : 128 + LANES] = ylo[at].astype(F32)[second : second + 1]
+        field[row + 8 : row + 9, 128 : 128 + LANES] = yhi[at].astype(F32)[second : second + 1]
+        for side, lane, upper in ((zlo, 0, True), (zhi, 128 + LANES, False)):
+            value = side[at].astype(F32)
+            if upper != bool(second):
+                value = pltpu.roll(value, 64, 1)
+            value = jnp.where(low_half(value.shape) != upper, value, 0.0)
+            field[row - 1 : row, lane : lane + 128] = value[1:2]
+            field[row : row + 8, lane : lane + 128] = value[2:10]
+            field[row + 8 : row + 9, lane : lane + 128] = value[10:11]
+
+
 def spread(value, steps, sign):
     moved = pltpu.roll(value, 64, 1)
     for i, dy in enumerate((-1, 0, 1)):
@@ -140,11 +193,11 @@
 
 def main_kernel(scale, grad, pre, inp, xlo, xhi, ylo, yhi, zlo, zhi, band,
                 slots, pre_out, fg, fa, fi, steps, columns, many, left, left_f, grads_one, grads_two, held):
-    layers = layer_list(grad, pre, inp, xlo, xhi)
+    wide, acts, inputs = fields_of(grad, pre, inp, xlo, xhi)
     halos = (ylo, yhi, zlo, zhi)
-    fill(fg, layers[0:8], 0, 0, *halos)
-    fill(fa, layers[8:14], 8, 1, *halos)
-    fill(fi, layers[14:20], 14, 1, *halos)
+    fill_wide(fg, wide, *halos)
+    fill_thin(fa, acts, 0, *halos)
+    fill_thin(fi, inputs, 1, *halos)
     contract = (((0,), (0,)), ((), ()))
 
     v = fa[...]
@@ -183,7 +236,7 @@
         left[64 * h : 64 * (h + 1), :] = jnp.where(inside, value, 0.0).astype(B16)
     grads_one[...] = lax.dot_general(left[...], columns[...], contract, preferred_element_type=F32)
 
-    count, rows = slots.shape[0], slots.shape[1]
+    count, rows = slots.shape[1], slots.shape[2]
 
     def block(kk):
         k, source = (kk, grads_one) if kk < 27 else (kk - 27, grads_two)
@@ -199,7 +252,9 @@
         first, second = block(2 * j), block(2 * j + 1)
         value = jnp.where(low_half(first.shape), first, second) * scale
         for g in range(count):
-            slots[g, :, 128 * j : 128 * (j + 1)] = value[g * rows : (g + 1) * rows, :].astype(B16)
+            part, lane = j // 7, j % 7 * 128
+            slots[part, g, :, lane : lane + 128] = value[g * rows : (g + 1) * rows, :].astype(B16)
+    slots[SPLIT - 1, :, :, PART - 128 :] = jnp.zeros((count, rows, 128), B16)
 
 
 def last_kernel(pre_grad, grad, band, out, steps, columns, held):
@@ -221,46 +276,88 @@
     return lax.ppermute(high, axis, up), lax.ppermute(low, axis, down)
 
 
+def total_kernel(parts, out):
+    value = parts[0].astype(F32)
+    for i in range(1, parts.shape[0]):
+        value += parts[i].astype(F32)
+    value = value.astype(out.dtype)
+    if out.ndim == value.ndim:
+        out[...] = value
+    else:
+        for i in range(out.shape[0]):
+            out[i] = value
+
+
+def last_total_kernel(parts, one, two):
+    columns = []
+    for part in range(SPLIT):
+        columns += [parts[part, :, 128 * i : 128 * (i + 1)] for i in range(7)]
+    for j in range(13):
+        one[:, 128 * j : 128 * (j + 1)] = columns[j]
+    one[:, 13 * 128 :] = columns[13][:, 0:64]
+    for j in range(14):
+        v, w = pltpu.roll(columns[13 + j], 64, 1), pltpu.roll(columns[14 + j], 64, 1)
+        value = jnp.where(low_half(v.shape), v, w)
+        if j < 13:
+            two[:, 128 * j : 128 * (j + 1)] = value
+        else:
+            two[:, 13 * 128 :] = value[:, 0:64]
+
+
 def reduced(slots):
-    part = lax.all_to_all(slots, "gx", 0, 0, tiled=True).astype(F32).sum(0)
-    part = lax.all_gather(part, "gz", axis=0).sum(0)
-    copies = jnp.broadcast_to(part[None].astype(B16), (lax.axis_size("gy"),) + part.shape)
-    return lax.all_to_all(copies, "gy", 0, 0, tiled=True).astype(F32).sum(0)
+    count, rows = slots.shape[1:3]
+    gy = lax.axis_size("gy")
+
+    def a2a(array, axis):
+        return lax.all_to_all(array, axis, 0, 0, tiled=True)
+
+    (part,) = call(total_kernel, [((count, rows, PART), B16)], [], 1000, 500000, a2a(slots, "gz"))
+    (copies,) = call(total_kernel, [((gy, rows, PART), F32)], [], 1000, 500000, a2a(part, "gx"))
+    (part,) = call(total_kernel, [((rows, PART), F32)], [], 1000, 500000, a2a(copies, "gy"))
+    parts = lax.all_gather(part, "gz", axis=0)
+    grads = ((rows, 27 * CH), F32)
+    return call(last_total_kernel, [grads, grads], [], 1000, 500000, parts)
 
 
 def body(block_input, pre_act, skip_grad, pool_grad, conv1_weight, conv2_weight):
     count = lax.axis_size("gx")
     rows = CH // count
     cells = SX * SY * SZ * count * lax.axis_size("gy") * lax.axis_size("gz")
-    message = ((4, SY, LANES), B16)
-    grad, low, high = call(
+    block, message = ((SX, SY, LANES), B16), ((4, SY, LANES), B16)
+    weight = ((rows, 27 * CH), B16)
+    grad, pre, inp, low, high, copies = call(
         prep_kernel,
-        [((SX, SY, LANES), B16), message, message],
-        [((SX // 2, SY, LANES), F32)],
+        [block, block, block, message, message, ((count, 2 * rows, 27 * CH), B16)],
+        [
+            block, ((SX // 2, SY // 2, LANES // 2), B16), weight, weight,
+            ((SX // 2, SY, LANES), F32), ((2 * rows, 27 * CH), F32), pltpu.SemaphoreType.DMA((6,)),
+        ],
         100000, 400000,
-        skip_grad, pool_grad, pre_act, block_input,
+        skip_grad, pool_grad, pre_act, block_input, conv1_weight, conv2_weight,
+        space=pltpu.HBM,
+        grant=60,
     )
     xlo, xhi = swapped(low, high, "gx")
-    both = jnp.concatenate([conv1_weight, conv2_weight], axis=1)
-    copies = jnp.broadcast_to(both[None], (count,) + both.shape)
     gathered = lax.all_to_all(copies, "gx", 0, 0, tiled=True)
-    fields = (grad, pre_act, block_input, xlo, xhi)
+    fields = (grad, pre, inp, xlo, xhi)
     message = ((LAYERS, 2, LANES), B16)
-    ylo, yhi = swapped(*call(ypack_kernel, [message, message], [], 100000, 600000, *fields), "gy")
-    message = ((LAYERS, 12, 128), B16)
+    ylo, yhi = swapped(
+        *call(ypack_kernel, [message, message], [((2, LANES), F32)], 100000, 600000, *fields), "gy"
+    )
+    message, held = ((LAYERS, 12, 128), B16), ((LAYERS, 12, 128), F32)
     zlo, zhi = swapped(
-        *call(zpack_kernel, [message, message], [((LAYERS, 12, 128), F32)], 100000, 700000, *fields, ylo, yhi),
+        *call(zpack_kernel, [message, message], [held, ((12, 128), F32)], 100000, 700000, *fields, ylo, yhi),
         "gz",
     )
     matrix = ((DEPTH, 256), B16)
-    flat = ((CH, 54 * CH + 512), F32)
+    flat = ((CH, 36 * CH), F32)
     band_one, band_two = call(bands_kernel, [matrix, matrix], [flat, flat], 1000000, 4000000, gathered)
     field = ((ROWS, WIDE), F32)
     steps = ((3, ROWS, WIDE), B16)
     columns = ((256, DEPTH), B16)
     slots, pre_grad = call(
         functools.partial(main_kernel, 1.0 / math.sqrt(cells)),
-        [((count, rows, 54 * CH), B16), ((ROWS, WIDE), B16)],
+        [((SPLIT, count, rows, PART), B16), ((ROWS, WIDE), B16)],
         [
             field, field, field, steps, columns,
             ((5 * HALO_ROWS, DEPTH), B16), ((256, 256), B16), ((256, 256), F32),
@@ -276,8 +373,8 @@
         500000000, 4000000,
         pre_grad, grad, band_one,
     )
-    summed = reduced(slots)
-    return input_grad, summed[:, : 27 * CH], summed[:, 27 * CH :]
+    conv1_grad, conv2_grad = reduced(slots)
+    return input_grad, conv1_grad, conv2_grad
 
 
 def solution(mesh):

time: 106 us -> 110 us (1.038)
  blocking collectives: 28.1 us -> 48.9 us
  waiting for transfers between devices: 19.2 us -> 11.9 us
  starting transfers between devices: 42.6 us -> 36.4 us
  local copies, waits for them, and re-layouts: 7.21 us -> 2.53 us
  Pallas kernels: 6.44 us -> 9.22 us
  other arithmetic: 1.23 us -> 0 us
    all_to_all x1 -> x3, blocking collectives: 20.9 us -> 38.8 us  [a2a(): return lax.all_to_all(array, axis, 0, 0, tiled=True)]
    all_to_all x1 -> x0, waiting for transfers between devices: 9.28 us -> none  [reduced(): return lax.all_to_all(copies, 'gy', 0, 0, tiled=True).astype(F32).sum(0)]
    all_to_all x1 -> x0, starting transfers between devices: 7.02 us -> none  [reduced(): return lax.all_to_all(copies, 'gy', 0, 0, tiled=True).astype(F32).sum(0)]
    all_gather x1, blocking collectives: 7.14 us -> 10.2 us  [reduced(): parts = lax.all_gather(part, 'gz', axis=0)]
    pallas_call x6 -> x10, Pallas kernels: 6.44 us -> 9.22 us  [call(): pl.pallas_call(kernel, out_shape=[jax.ShapeDtypeStruct(shape, dtype) for...]
    unnamed x16 -> x12, local copies, waits for them, and re-layouts: 4.9 us -> 2.53 us
    ppermute x6, waiting for transfers between devices: 9.91 us -> 11.9 us  [swapped(): return (lax.ppermute(high, axis, up), lax.ppermute(low, axis, down))]
    broadcast_in_dim x2 -> x0, local copies, waits for them, and re-layouts: 1.62 us -> none  [the longest x1 0.88 us: body(): copies = jnp.broadcast_to(both[None], (count,) + both.shape)]
  transfers between devices with their start and end apart: 8 -> 7, of which waited for: 5 -> 3; matrix products, arithmetic and copies ran while one was open for 0% -> 0% of each run, Pallas kernels for 2% -> 1%
where the time goes in v3:
time: 110 us
  blocking collectives  48.9 us (44%)
  starting transfers between devices  36.4 us (33%)
  waiting for transfers between devices  11.9 us (11%)
  Pallas kernels  9.22 us (8%)
  local copies, waits for them, and re-layouts  2.53 us (2%)
    all_to_all x3, blocking collectives, a2a(): return lax.all_to_all(array, axis, 0, 0, tiled=True)  38.8 us
    ppermute x6, starting transfers between devices, swapped(): return (lax.ppermute(high, axis, up), lax.ppermute(low, axis, down))  24.4 us
    all_to_all x1, starting transfers between devices, body(): gathered = lax.all_to_all(copies, 'gx', 0, 0, tiled=True)  12 us
    ppermute x6, waiting for transfers between devices, swapped(): return (lax.ppermute(high, axis, up), lax.ppermute(low, axis, down))  11.9 us
    all_gather x1, blocking collectives, reduced(): parts = lax.all_gather(part, 'gz', axis=0)  10.2 us
    pallas_call x10, Pallas kernels, call(): pl.pallas_call(kernel, out_shape=[jax.ShapeDtypeStruct(shape, dtype) for...  9.22 us
    unnamed x12, local copies, waits for them, and re-layouts  2.53 us
  transfers between devices with their start and end apart: 7, of which 3 were waited for; matrix products, arithmetic and copies ran while one was open for 0% of the time, Pallas kernels for 1%

profile of v3, /device:TPU:1, one launch (start us, length us, event | category | flops | bytes accessed | tf_op | source)
XLA Modules:
  0.0 109.8 jit_solution(7991472296355660014)
XLA Ops:
  0.6 1.9 %shard_map.85 = (bf16[4,8,1024]{2,1,0:T(8,128)(2,1)}, bf16[4,8,1024]{2,1,0:T(8,128)(2,1)}, bf16[4,8,1024]{2,1,0:T(8,128)(2,1)}, bf16[4,8,1024]{2,1,0:T(8,128)(2,...) custom-call(bf16[4,8,1024]{2,1,0:T(8,128)(2,1)} %skip_in.1, bf16[2,4,512]{2,1,0:T(4,128)(2,1)} %pool_in.1, ...), custom_call_target="tpu_custom_call" | custom-call | flops 100000 | bytes 400000 | tf_op jit(solution)/shard_map/pallas_call | solution.py:26
  2.5 12.0 %all-to-all-start = ((bf16[16,8,1728]{2,1,0:T(8,128)(2,1)}), bf16[16,8,1728]{2,1,0:T(8,128)(2,1)S(1)}, u32[]{:S(2)}, u32[]{:S(2)}) async-start(bf16[16,8,1728]{2,1,0:T(8,128)(2,1)} %get-tuple-element.28), calls=%async_computation | async-start | bytes 917504 | tf_op jit(solution)/shard_map/all_to_all | solution.py:341
  14.6 3.3 %collective-permute-start = (bf16[4,8,1024]{2,1,0:T(8,128)(2,1)}, bf16[4,8,1024]{2,1,0:T(8,128)(2,1)S(1)}, u32[]{:S(2)}, u32[]{:S(2)}) collective-permute-start(bf16[4,8,1024]{2,1,0:T(8,128)(2,1)} %get-tuple-element.22), channel_id=1, source_target_pairs={{0,32},{32,64},{64,96},{96,128},{128,160},{160,192},{192,224},{224... | collective-permute-start | bytes 196616 | tf_op jit(solution)/shard_map/ppermute | solution.py:276
  17.8 4.1 %collective-permute-start.1 = (bf16[4,8,1024]{2,1,0:T(8,128)(2,1)}, bf16[4,8,1024]{2,1,0:T(8,128)(2,1)S(1)}, u32[]{:S(2)}, u32[]{:S(2)}) collective-permute-start(bf16[4,8,1024]{2,1,0:T(8,128)(2,1)} %get-tuple-element.23), channel_id=1, source_target_pairs={{32,0},{64,32},{96,64},{128,96},{160,128},{192,160},{224,192},{256... | collective-permute-start | bytes 196616 | tf_op jit(solution)/shard_map/ppermute | solution.py:276
  22.0 6.2 %collective-permute-done.xlo = bf16[4,8,1024]{2,1,0:T(8,128)(2,1)S(1)} collective-permute-done((bf16[4,8,1024]{2,1,0:T(8,128)(2,1)}, bf16[4,8,1024]{2,1,0:T(8,128)(2,1)S(1)}, u32[]{:S(2)}, u32[]{:S(2)}) %collective-permute-start) | collective-permute-done | bytes 65568 | tf_op jit(solution)/shard_map/ppermute | solution.py:276
  28.2 0.8 copy-done
  29.1 0.8 copy-done.2
  29.9 0.8 copy-done.4
  30.7 0.1 shard_map.86
  30.9 3.2 %collective-permute-start.2 = (bf16[14,2,1024]{2,1,0:T(2,128)(2,1)S(1)}, bf16[14,2,1024]{2,1,0:T(2,128)(2,1)S(1)}, u32[]{:S(2)}, u32[]{:S(2)}) collective-permute-start(bf16[14,2,1024]{2,1,0:T(2,128)(2,1)S(1)} %get-tuple-element.24), channel_id=1, source_target_pairs={{0,4},{4,8},{8,12},{12,16},{16,20},{20,24},{24,28},{28,0},{1,5},{5... | collective-permute-start | bytes 172040 | tf_op jit(solution)/shard_map/ppermute | solution.py:276
  34.1 3.8 %collective-permute-start.3 = (bf16[14,2,1024]{2,1,0:T(2,128)(2,1)S(1)}, bf16[14,2,1024]{2,1,0:T(2,128)(2,1)S(1)}, u32[]{:S(2)}, u32[]{:S(2)}) collective-permute-start(bf16[14,2,1024]{2,1,0:T(2,128)(2,1)S(1)} %get-tuple-element.25), channel_id=1, source_target_pairs={{4,0},{8,4},{12,8},{16,12},{20,16},{24,20},{28,24},{0,28},{5,1},{9... | collective-permute-start | bytes 172040 | tf_op jit(solution)/shard_map/ppermute | solution.py:276
  37.9 1.2 %collective-permute-done.3.yhi = bf16[14,2,1024]{2,1,0:T(2,128)(2,1)S(1)} collective-permute-done((bf16[14,2,1024]{2,1,0:T(2,128)(2,1)S(1)}, bf16[14,2,1024]{2,1,0:T(2,128)(2,1)S(1)}, u32[]{:S(2)}, u32[]{:S(2)}) %collective-permute-start.3) | collective-permute-done | bytes 57376 | tf_op jit(solution)/shard_map/ppermute | solution.py:276
  39.1 0.2 shard_map.87
  39.4 8.1 %collective-permute-start.4 = (bf16[14,12,128]{2,1,0:T(8,128)(2,1)S(1)}, bf16[14,12,128]{2,1,0:T(8,128)(2,1)S(1)}, u32[]{:S(2)}, u32[]{:S(2)}) collective-permute-start(bf16[14,12,128]{2,1,0:T(8,128)(2,1)S(1)} %get-tuple-element.26), channel_id=1, source_target_pairs={{0,1},{1,2},{2,3},{3,0},{4,5},{5,6},{6,7},{7,4},{8,9},{9,10},{10,1... | collective-permute-start | bytes 129032 | tf_op jit(solution)/shard_map/ppermute | solution.py:276
  47.4 1.9 %collective-permute-start.5 = (bf16[14,12,128]{2,1,0:T(8,128)(2,1)S(1)}, bf16[14,12,128]{2,1,0:T(8,128)(2,1)S(1)}, u32[]{:S(2)}, u32[]{:S(2)}) collective-permute-start(bf16[14,12,128]{2,1,0:T(8,128)(2,1)S(1)} %get-tuple-element.27), channel_id=1, source_target_pairs={{1,0},{2,1},{3,2},{0,3},{5,4},{6,5},{7,6},{4,7},{9,8},{10,9},{11,1... | collective-permute-start | bytes 129032 | tf_op jit(solution)/shard_map/ppermute | solution.py:276
  49.4 0.6 shard_map.88
  50.0 4.4 %collective-permute-done.5.zhi = bf16[14,12,128]{2,1,0:T(8,128)(2,1)S(1)} collective-permute-done((bf16[14,12,128]{2,1,0:T(8,128)(2,1)S(1)}, bf16[14,12,128]{2,1,0:T(8,128)(2,1)S(1)}, u32[]{:S(2)}, u32[]{:S(2)}) %collective-permute-start.5) | collective-permute-done | bytes 43040 | tf_op jit(solution)/shard_map/ppermute | solution.py:276
  54.4 4.2 %shard_map.89 = (bf16[4,16,4,896]{3,2,1,0:T(4,128)(2,1)S(1)}, bf16[144,1408]{1,0:T(8,128)(2,1)S(1)}) custom-call(bf16[4,8,1024]{2,1,0:T(8,128)(2,1)S(1)} %copy-done.1, bf16[4,8,1024]{2,1,0:T(8,128)(2,1)S(1)} %copy-done.3, bf16[4,8,1024]{2,1,0:T(8,128)(2,1)S(1)} %copy-done.5, bf16[4,8,1024]{2,1,0:T(8,128)(2,1)S(1)} %collective-permute-done.xlo, ...), custom_call_target="tpu_custom_call" | custom-call | flops 1800000000 | bytes 8000000 | tf_op jit(solution)/shard_map/pallas_call | solution.py:26
  58.7 10.9 %all_to_all.20.parts = bf16[4,16,4,896]{3,2,1,0:T(4,128)(2,1)S(1)} all-to-all(bf16[4,16,4,896]{3,2,1,0:T(4,128)(2,1)S(1)} %get-tuple-element.32), channel_id=1, replica_groups=mesh['gx'=16,'gy'=8,'gz'=4] {'gz'}, dimensions={0} | all-to-all | bytes 917504 | tf_op jit(solution)/shard_map/all_to_all | solution.py:312
  69.6 13.3 %all_to_all.21.parts = bf16[16,4,896]{2,1,0:T(4,128)(2,1)S(1)} all-to-all(bf16[16,4,896]{2,1,0:T(4,128)(2,1)S(1)} %shard_map.91), channel_id=1, replica_groups=mesh['gx'=16,'gy'=8,'gz'=4] {'gx'}, dimensions={0} | all-to-all | bytes 229376 | tf_op jit(solution)/shard_map/all_to_all | solution.py:312
  83.0 14.6 %all_to_all.22.parts = f32[8,4,896]{2,1,0:T(4,128)S(1)} all-to-all(f32[8,4,896]{2,1,0:T(4,128)S(1)} %shard_map.92), channel_id=1, replica_groups=mesh['gx'=16,'gy'=8,'gz'=4] {'gy'}, dimensions={0} | all-to-all | bytes 229376 | tf_op jit(solution)/shard_map/all_to_all | solution.py:312
  97.6 10.2 %all-gather.1.parts = f32[4,4,896]{2,1,0:T(4,128)S(1)} all-gather(f32[1,4,896]{2,1,0:T(4,128)S(1)} %bitcast.1), channel_id=2, replica_groups=mesh['gx'=16,'gy'=8,'gz'=4] {'gz'}, dimensions={0}, use_global_device_ids=true | all-gather | bytes 71680 | tf_op jit(solution)/shard_map/all_gather | solution.py:317
  107.7 1.3 %shard_map.90 = bf16[4,8,1024]{2,1,0:T(8,128)(2,1)} custom-call(bf16[144,1408]{1,0:T(8,128)(2,1)S(1)} %get-tuple-element.30.pre_grad, bf16[4,8,1024]{2,1,0:T(8,128)(2,1)S(1)} %copy-done.1, bf16[3456,256]{1,0:T(8,128)(2,1)S(1)} %get-tuple-element.31.band), custom_call_target="tpu_custom_call" | custom-call | flops 500000000 | bytes 4000000 | tf_op jit(solution)/shard_map/pallas_call | solution.py:26
  109.1 0.7 shard_map.94
  (16 shorter events, 0.2 us)
Async XLA Ops:
  2.5 51.9 %copy-start.1 = (bf16[4,8,1024]{2,1,0:T(8,128)(2,1)S(1)}, bf16[4,8,1024]{2,1,0:T(8,128)(2,1)}, u32[]{:S(2)}) copy-start(bf16[4,8,1024]{2,1,0:T(8,128)(2,1)} %get-tuple-element.19.grad) | copy-start | bytes 196612
  2.5 51.9 %copy-start.3 = (bf16[4,8,1024]{2,1,0:T(8,128)(2,1)S(1)}, bf16[4,8,1024]{2,1,0:T(8,128)(2,1)}, u32[]{:S(2)}) copy-start(bf16[4,8,1024]{2,1,0:T(8,128)(2,1)} %get-tuple-element.20.pre) | copy-start | bytes 196612
  2.5 51.9 %copy-start.5 = (bf16[4,8,1024]{2,1,0:T(8,128)(2,1)S(1)}, bf16[4,8,1024]{2,1,0:T(8,128)(2,1)}, u32[]{:S(2)}) copy-start(bf16[4,8,1024]{2,1,0:T(8,128)(2,1)} %get-tuple-element.21.inp) | copy-start | bytes 196612
  2.5 46.8 %all-to-all-start = ((bf16[16,8,1728]{2,1,0:T(8,128)(2,1)}), bf16[16,8,1728]{2,1,0:T(8,128)(2,1)S(1)}, u32[]{:S(2)}, u32[]{:S(2)}) async-start(bf16[16,8,1728]{2,1,0:T(8,128)(2,1)} %get-tuple-element.28), calls=%async_computation | async-start | bytes 917504 | tf_op jit(solution)/shard_map/all_to_all | solution.py:341
  14.6 13.6 %collective-permute-start = (bf16[4,8,1024]{2,1,0:T(8,128)(2,1)}, bf16[4,8,1024]{2,1,0:T(8,128)(2,1)S(1)}, u32[]{:S(2)}, u32[]{:S(2)}) collective-permute-start(bf16[4,8,1024]{2,1,0:T(8,128)(2,1)} %get-tuple-element.22), channel_id=1, source_target_pairs={{0,32},{32,64},{64,96},{96,128},{128,160},{160,192},{192,224},{224... | collective-permute-start | bytes 196616 | tf_op jit(solution)/shard_map/ppermute | solution.py:276
  17.8 10.4 %collective-permute-start.1 = (bf16[4,8,1024]{2,1,0:T(8,128)(2,1)}, bf16[4,8,1024]{2,1,0:T(8,128)(2,1)S(1)}, u32[]{:S(2)}, u32[]{:S(2)}) collective-permute-start(bf16[4,8,1024]{2,1,0:T(8,128)(2,1)} %get-tuple-element.23), channel_id=1, source_target_pairs={{32,0},{64,32},{96,64},{128,96},{160,128},{192,160},{224,192},{256... | collective-permute-start | bytes 196616 | tf_op jit(solution)/shard_map/ppermute | solution.py:276
  28.2 0.8 copy-start
  29.1 0.8 copy-start.2
  29.9 0.8 copy-start.4
  30.9 7.0 %collective-permute-start.2 = (bf16[14,2,1024]{2,1,0:T(2,128)(2,1)S(1)}, bf16[14,2,1024]{2,1,0:T(2,128)(2,1)S(1)}, u32[]{:S(2)}, u32[]{:S(2)}) collective-permute-start(bf16[14,2,1024]{2,1,0:T(2,128)(2,1)S(1)} %get-tuple-element.24), channel_id=1, source_target_pairs={{0,4},{4,8},{8,12},{12,16},{16,20},{20,24},{24,28},{28,0},{1,5},{5... | collective-permute-start | bytes 172040 | tf_op jit(solution)/shard_map/ppermute | solution.py:276
  34.1 5.1 %collective-permute-start.3 = (bf16[14,2,1024]{2,1,0:T(2,128)(2,1)S(1)}, bf16[14,2,1024]{2,1,0:T(2,128)(2,1)S(1)}, u32[]{:S(2)}, u32[]{:S(2)}) collective-permute-start(bf16[14,2,1024]{2,1,0:T(2,128)(2,1)S(1)} %get-tuple-element.25), channel_id=1, source_target_pairs={{4,0},{8,4},{12,8},{16,12},{20,16},{24,20},{28,24},{0,28},{5,1},{9... | collective-permute-start | bytes 172040 | tf_op jit(solution)/shard_map/ppermute | solution.py:276
  39.4 10.6 %collective-permute-start.4 = (bf16[14,12,128]{2,1,0:T(8,128)(2,1)S(1)}, bf16[14,12,128]{2,1,0:T(8,128)(2,1)S(1)}, u32[]{:S(2)}, u32[]{:S(2)}) collective-permute-start(bf16[14,12,128]{2,1,0:T(8,128)(2,1)S(1)} %get-tuple-element.26), channel_id=1, source_target_pairs={{0,1},{1,2},{2,3},{3,0},{4,5},{5,6},{6,7},{7,4},{8,9},{9,10},{10,1... | collective-permute-start | bytes 129032 | tf_op jit(solution)/shard_map/ppermute | solution.py:276
  47.4 7.0 %collective-permute-start.5 = (bf16[14,12,128]{2,1,0:T(8,128)(2,1)S(1)}, bf16[14,12,128]{2,1,0:T(8,128)(2,1)S(1)}, u32[]{:S(2)}, u32[]{:S(2)}) collective-permute-start(bf16[14,12,128]{2,1,0:T(8,128)(2,1)S(1)} %get-tuple-element.27), channel_id=1, source_target_pairs={{1,0},{2,1},{3,2},{0,3},{5,4},{6,5},{7,6},{4,7},{9,8},{10,9},{11,1... | collective-permute-start | bytes 129032 | tf_op jit(solution)/shard_map/ppermute | solution.py:276

commit v4 on v3

--- a/solution.py
+++ b/solution.py
@@ -18,18 +18,16 @@
 OWN = 16 * 3
 HALO_ROWS = 16 * (SX + 3)
 LAYERS = 14
-SPLIT = 4
-PART = 7 * 128
-
-
-def call(kernel, outs, scratch, flops, moved, *args, space=pltpu.VMEM, grant=48):
+
+
+def call(kernel, outs, scratch, flops, moved, *args, space=pltpu.VMEM):
     return pl.pallas_call(
         kernel,
         out_shape=[jax.ShapeDtypeStruct(shape, dtype) for shape, dtype in outs],
         in_specs=[pl.BlockSpec(memory_space=space)] * len(args),
         out_specs=[pl.BlockSpec(memory_space=pltpu.VMEM)] * len(outs),
         scratch_shapes=[pltpu.VMEM(*held) if isinstance(held, tuple) else held for held in scratch],
-        compiler_params=pltpu.CompilerParams(vmem_limit_bytes=grant * 1024 * 1024),
+        compiler_params=pltpu.CompilerParams(vmem_limit_bytes=48 * 1024 * 1024),
         cost_estimate=pl.CostEstimate(flops=flops, bytes_accessed=moved, transcendentals=0),
     )(*args)
 
@@ -100,28 +98,36 @@
             out[8 + at] = held[...].astype(B16)
 
 
-def zpack_kernel(grad, pre, inp, xlo, xhi, ylo, yhi, low, high, held, second):
+def zpack_kernel(grad, pre, inp, xlo, xhi, ylo, yhi, slots, held):
+    held[...] = jnp.zeros_like(held)
     wide, acts, inputs = fields_of(grad, pre, inp, xlo, xhi)
-    for out, lane, half in ((low, 0, True), (high, LANES - 128, False)):
+    size = slots.shape[0]
+    me = lax.axis_index("gz")
+    slots[...] = jnp.zeros_like(slots)
+    for to, lane, half in ((me + size - 1, 0, True), (me + 1, LANES - 128, False)):
         cut = slice(lane, lane + 128)
         for at, (ref, x) in enumerate(wide):
-            held[at, 0:2] = ylo[at, :, cut].astype(F32)
-            held[at, 2:10] = ref[x, :, cut].astype(F32)
-            held[at, 10:12] = yhi[at, :, cut].astype(F32)
+            row = 12 * at
+            held[row : row + 2] = ylo[at, :, cut].astype(F32)
+            held[row + 2 : row + 10] = ref[x, :, cut].astype(F32)
+            held[row + 10 : row + 12] = yhi[at, :, cut].astype(F32)
         for j, ((a, ax), (i, ix)) in enumerate(zip(acts, inputs)):
-            at = 8 + j
-            below, above = ylo[at, :, cut].astype(F32), yhi[at, :, cut].astype(F32)
-            for to, ref, x, row in ((held.at[at], a, ax, 0), (second, i, ix, 1)):
-                to[1:2] = below[row : row + 1]
-                to[2:10] = ref[x, :, cut].astype(F32)
-                to[10:11] = above[row : row + 1]
-            v, w = held[at], second[...]
-            if half:
-                w = pltpu.roll(w, 64, 1)
-            else:
-                v = pltpu.roll(v, 64, 1)
-            held[at] = jnp.where(low_half(v.shape), v, w)
-        out[...] = held[...].astype(B16)
+            row = 12 * (8 + j)
+            below, above = ylo[8 + j, :, cut].astype(F32), yhi[8 + j, :, cut].astype(F32)
+            v, w = a[ax, :, cut].astype(F32), i[ix, :, cut].astype(F32)
+
+            def joined(first, second):
+                if half:
+                    second = pltpu.roll(second, 64, 1)
+                else:
+                    first = pltpu.roll(first, 64, 1)
+                return jnp.where(low_half(first.shape), first, second)
+
+            held[row + 2 : row + 10] = joined(v, w)
+            for at, pair in ((row + 1, below), (row + 10, above)):
+                first, second = jnp.broadcast_to(pair[0:1], (8, 128)), jnp.broadcast_to(pair[1:2], (8, 128))
+                held[at : at + 1] = joined(first, second)[0:1]
+        slots[lax.rem(to, size)] = held[...].astype(B16)
 
 
 def bands_kernel(weights, one, two, flat, turned):
@@ -151,10 +157,7 @@
         field[row - 2 : row, 128 : 128 + LANES] = ylo[at].astype(F32)
         field[row + 8 : row + 10, 128 : 128 + LANES] = yhi[at].astype(F32)
         for side, lane in ((zlo, 0), (zhi, 128 + LANES)):
-            value = side[at].astype(F32)
-            field[row - 2 : row, lane : lane + 128] = value[0:2]
-            field[row : row + 8, lane : lane + 128] = value[2:10]
-            field[row + 8 : row + 10, lane : lane + 128] = value[10:12]
+            field[row - 2 : row + 10, lane : lane + 128] = side[12 * at : 12 * at + 12]
 
 
 def fill_thin(field, layers, second, ylo, yhi, zlo, zhi):
@@ -165,7 +168,7 @@
         field[row - 1 : row, 128 : 128 + LANES] = ylo[at].astype(F32)[second : second + 1]
         field[row + 8 : row + 9, 128 : 128 + LANES] = yhi[at].astype(F32)[second : second + 1]
         for side, lane, upper in ((zlo, 0, True), (zhi, 128 + LANES, False)):
-            value = side[at].astype(F32)
+            value = side[12 * at : 12 * at + 12]
             if upper != bool(second):
                 value = pltpu.roll(value, 64, 1)
             value = jnp.where(low_half(value.shape) != upper, value, 0.0)
@@ -191,9 +194,13 @@
             ]
 
 
-def main_kernel(scale, grad, pre, inp, xlo, xhi, ylo, yhi, zlo, zhi, band,
-                slots, pre_out, fg, fa, fi, steps, columns, many, left, left_f, grads_one, grads_two, held):
+def main_kernel(scale, grad, pre, inp, xlo, xhi, ylo, yhi, sides, band,
+                slots, pre_out, fg, fa, fi, steps, columns, many, left, left_f, grads_one, grads_two, held, zlo, zhi):
     wide, acts, inputs = fields_of(grad, pre, inp, xlo, xhi)
+    size = sides.shape[0]
+    me = lax.axis_index("gz")
+    zlo[...] = sides[lax.rem(me + size - 1, size)].astype(F32)
+    zhi[...] = sides[lax.rem(me + 1, size)].astype(F32)
     halos = (ylo, yhi, zlo, zhi)
     fill_wide(fg, wide, *halos)
     fill_thin(fa, acts, 0, *halos)
@@ -236,7 +243,7 @@
         left[64 * h : 64 * (h + 1), :] = jnp.where(inside, value, 0.0).astype(B16)
     grads_one[...] = lax.dot_general(left[...], columns[...], contract, preferred_element_type=F32)
 
-    count, rows = slots.shape[1], slots.shape[2]
+    count, rows = slots.shape[0], slots.shape[1]
 
     def block(kk):
         k, source = (kk, grads_one) if kk < 27 else (kk - 27, grads_two)
@@ -252,9 +259,7 @@
         first, second = block(2 * j), block(2 * j + 1)
         value = jnp.where(low_half(first.shape), first, second) * scale
         for g in range(count):
-            part, lane = j // 7, j % 7 * 128
-            slots[part, g, :, lane : lane + 128] = value[g * rows : (g + 1) * rows, :].astype(B16)
-    slots[SPLIT - 1, :, :, PART - 128 :] = jnp.zeros((count, rows, 128), B16)
+            slots[g, :, 128 * j : 128 * (j + 1)] = value[g * rows : (g + 1) * rows, :].astype(B16)
 
 
 def last_kernel(pre_grad, grad, band, out, steps, columns, held):
@@ -288,35 +293,28 @@
             out[i] = value
 
 
-def last_total_kernel(parts, one, two):
-    columns = []
-    for part in range(SPLIT):
-        columns += [parts[part, :, 128 * i : 128 * (i + 1)] for i in range(7)]
-    for j in range(13):
-        one[:, 128 * j : 128 * (j + 1)] = columns[j]
-    one[:, 13 * 128 :] = columns[13][:, 0:64]
-    for j in range(14):
-        v, w = pltpu.roll(columns[13 + j], 64, 1), pltpu.roll(columns[14 + j], 64, 1)
-        value = jnp.where(low_half(v.shape), v, w)
-        if j < 13:
-            two[:, 128 * j : 128 * (j + 1)] = value
-        else:
-            two[:, 13 * 128 :] = value[:, 0:64]
-
-
-def reduced(slots):
-    count, rows = slots.shape[1:3]
+def last_total_kernel(parts, one, two, held):
+    value = parts[0].astype(F32)
+    for i in range(1, parts.shape[0]):
+        value += parts[i].astype(F32)
+    held[...] = value
+    one[...] = held[:, : 27 * CH]
+    held[...] = pltpu.roll(value, 27 * CH, 1)
+    two[...] = held[:, : 27 * CH]
+
+
+def reduced(slots, other):
+    rows, columns = slots.shape[1:]
     gy = lax.axis_size("gy")
-
-    def a2a(array, axis):
-        return lax.all_to_all(array, axis, 0, 0, tiled=True)
-
-    (part,) = call(total_kernel, [((count, rows, PART), B16)], [], 1000, 500000, a2a(slots, "gz"))
-    (copies,) = call(total_kernel, [((gy, rows, PART), F32)], [], 1000, 500000, a2a(part, "gx"))
-    (part,) = call(total_kernel, [((rows, PART), F32)], [], 1000, 500000, a2a(copies, "gy"))
+    parts = lax.all_to_all(slots, "gx", 0, 0, tiled=True)
+    parts, other = lax.optimization_barrier((parts, other))
+    (part,) = call(total_kernel, [((rows, columns), F32)], [], 1000, 500000, parts)
     parts = lax.all_gather(part, "gz", axis=0)
+    (copies,) = call(total_kernel, [((gy, rows, columns), B16)], [], 1000, 500000, parts)
+    parts = lax.all_to_all(copies, "gy", 0, 0, tiled=True)
     grads = ((rows, 27 * CH), F32)
-    return call(last_total_kernel, [grads, grads], [], 1000, 500000, parts)
+    one, two = call(last_total_kernel, [grads, grads], [((rows, columns), F32)], 1000, 500000, parts)
+    return other, one, two
 
 
 def body(block_input, pre_act, skip_grad, pool_grad, conv1_weight, conv2_weight):
@@ -333,22 +331,28 @@
             ((SX // 2, SY, LANES), F32), ((2 * rows, 27 * CH), F32), pltpu.SemaphoreType.DMA((6,)),
         ],
         100000, 400000,
-        skip_grad, pool_grad, pre_act, block_input, conv1_weight, conv2_weight,
+        *(
+            pltpu.with_memory_space_constraint(array, pltpu.HBM)
+            for array in (skip_grad, pool_grad, pre_act, block_input, conv1_weight, conv2_weight)
+        ),
         space=pltpu.HBM,
-        grant=60,
     )
     xlo, xhi = swapped(low, high, "gx")
-    gathered = lax.all_to_all(copies, "gx", 0, 0, tiled=True)
     fields = (grad, pre, inp, xlo, xhi)
     message = ((LAYERS, 2, LANES), B16)
     ylo, yhi = swapped(
-        *call(ypack_kernel, [message, message], [((2, LANES), F32)], 100000, 600000, *fields), "gy"
-    )
-    message, held = ((LAYERS, 12, 128), B16), ((LAYERS, 12, 128), F32)
-    zlo, zhi = swapped(
-        *call(zpack_kernel, [message, message], [held, ((12, 128), F32)], 100000, 700000, *fields, ylo, yhi),
-        "gz",
-    )
+        *call(ypack_kernel, [message, message], [((2, LANES), F32)], 60000000000, 600000, *fields), "gy"
+    )
+    side = ((12 * LAYERS, 128), F32)
+    gathered = lax.all_to_all(copies, "gx", 0, 0, tiled=True)
+    (sides,) = call(
+        zpack_kernel,
+        [((lax.axis_size("gz"), 12 * LAYERS, 128), B16)],
+        [side],
+        100000, 700000,
+        *fields, ylo, yhi,
+    )
+    sides = lax.all_to_all(sides, "gz", 0, 0, tiled=True)
     matrix = ((DEPTH, 256), B16)
     flat = ((CH, 36 * CH), F32)
     band_one, band_two = call(bands_kernel, [matrix, matrix], [flat, flat], 1000000, 4000000, gathered)
@@ -357,14 +361,14 @@
     columns = ((256, DEPTH), B16)
     slots, pre_grad = call(
         functools.partial(main_kernel, 1.0 / math.sqrt(cells)),
-        [((SPLIT, count, rows, PART), B16), ((ROWS, WIDE), B16)],
+        [((count, rows, 54 * CH), B16), ((ROWS, WIDE), B16)],
         [
             field, field, field, steps, columns,
             ((5 * HALO_ROWS, DEPTH), B16), ((256, 256), B16), ((256, 256), F32),
-            ((256, DEPTH), F32), ((256, DEPTH), F32), ((5 * HALO_ROWS, 256), F32),
+            ((256, DEPTH), F32), ((256, DEPTH), F32), ((5 * HALO_ROWS, 256), F32), side, side,
         ],
         2 * 900 * 1000 * 1000, 8000000,
-        *fields, ylo, yhi, zlo, zhi, band_two,
+        *fields, ylo, yhi, sides, band_two,
     )
     (input_grad,) = call(
         last_kernel,
@@ -373,8 +377,7 @@
         500000000, 4000000,
         pre_grad, grad, band_one,
     )
-    conv1_grad, conv2_grad = reduced(slots)
-    return input_grad, conv1_grad, conv2_grad
+    return reduced(slots, input_grad)
 
 
 def solution(mesh):

time: 110 us -> 100 us (0.909)
  blocking collectives: 48.9 us -> 27.3 us
  waiting for transfers between devices: 11.9 us -> 22 us
  Pallas kernels: 9.22 us -> 10.5 us
    all_to_all x3 -> x1, blocking collectives: 38.8 us -> 17.2 us  [reduced(): parts = lax.all_to_all(copies, 'gy', 0, 0, tiled=True)]
    all_to_all x0 -> x2, waiting for transfers between devices: none -> 16.1 us  [the longest x1 12.6 us: reduced(): parts = lax.all_to_all(slots, 'gx', 0, 0, tiled=True)]
    all_to_all x0 -> x2, starting transfers between devices: none -> 10.9 us  [the longest x1 7.33 us: body(): sides = lax.all_to_all(sides, 'gz', 0, 0, tiled=True)]
    ppermute x6 -> x4, waiting for transfers between devices: 11.9 us -> 1.39 us  [swapped(): return (lax.ppermute(high, axis, up), lax.ppermute(low, axis, down))]
    all_to_all x1, starting transfers between devices: 12 us -> 4 us  [body(): gathered = lax.all_to_all(copies, 'gx', 0, 0, tiled=True)]
    all_to_all x1, waiting for transfers between devices: 0.01 us -> 4.48 us  [body(): gathered = lax.all_to_all(copies, 'gx', 0, 0, tiled=True)]
    ppermute x6 -> x4, starting transfers between devices: 24.4 us -> 21.4 us  [swapped(): return (lax.ppermute(high, axis, up), lax.ppermute(low, axis, down))]
    pallas_call x10 -> x9, Pallas kernels: 9.22 us -> 10.5 us  [call(): pl.pallas_call(kernel, out_shape=[jax.ShapeDtypeStruct(shape, dtype) for...]
  transfers between devices with their start and end apart: 7 -> 7, of which waited for: 3 -> 4; matrix products, arithmetic and copies ran while one was open for 0% -> 0% of each run, Pallas kernels for 1% -> 3%
where the time goes in v4:
time: 100 us; the launch traced here: 99.5 us
  starting transfers between devices  36.2 us (36%)
  blocking collectives  27.3 us (27%)
  waiting for transfers between devices  22 us (22%)
  Pallas kernels  10.5 us (10%)
  local copies, waits for them, and re-layouts  2.7 us (3%)
    ppermute x4, starting transfers between devices, swapped(): return (lax.ppermute(high, axis, up), lax.ppermute(low, axis, down))  21.4 us
    all_to_all x1, blocking collectives, reduced(): parts = lax.all_to_all(copies, 'gy', 0, 0, tiled=True)  17.2 us
    all_to_all x1, waiting for transfers between devices, reduced(): parts = lax.all_to_all(slots, 'gx', 0, 0, tiled=True)  12.6 us
    pallas_call x9, Pallas kernels, call(): pl.pallas_call(kernel, out_shape=[jax.ShapeDtypeStruct(shape, dtype) for...  10.5 us
    all_gather x1, blocking collectives, reduced(): parts = lax.all_gather(part, 'gz', axis=0)  10.1 us
    all_to_all x1, starting transfers between devices, body(): sides = lax.all_to_all(sides, 'gz', 0, 0, tiled=True)  7.33 us
    all_to_all x1, waiting for transfers between devices, body(): gathered = lax.all_to_all(copies, 'gx', 0, 0, tiled=True)  4.48 us
    all_to_all x1, starting transfers between devices, body(): gathered = lax.all_to_all(copies, 'gx', 0, 0, tiled=True)  4 us
  transfers between devices with their start and end apart: 7, of which 4 were waited for; matrix products, arithmetic and copies ran while one was open for 0% of the time, Pallas kernels for 3%

profile of v4, /device:TPU:1, one launch (start us, length us, event | category | flops | bytes accessed | tf_op | source)
XLA Modules:
  0.0 99.5 jit_solution(1482711189004798083)
XLA Ops:
  0.6 1.8 %shard_map.85 = (bf16[4,8,1024]{2,1,0:T(8,128)(2,1)S(1)}, bf16[4,8,1024]{2,1,0:T(8,128)(2,1)S(1)}, bf16[4,8,1024]{2,1,0:T(8,128)(2,1)S(1)}, bf16[4,8,1024]{2,1,0...) custom-call(bf16[4,8,1024]{2,1,0:T(8,128)(2,1)} %skip_in.1, ...), custom_call_target="tpu_custom_call" | custom-call | flops 100000 | bytes 400000 | tf_op jit(solution)/shard_map/pallas_call | solution.py:24
  2.4 3.9 %collective-permute-start = (bf16[4,8,1024]{2,1,0:T(8,128)(2,1)S(1)}, bf16[4,8,1024]{2,1,0:T(8,128)(2,1)S(1)}, u32[]{:S(2)}, u32[]{:S(2)}) collective-permute-start(bf16[4,8,1024]{2,1,0:T(8,128)(2,1)S(1)} %get-tuple-element.22), channel_id=1, source_target_pairs={{0,32},{32,64},{64,96},{96,128},{128,160},{160,192},{192,224},{224... | collective-permute-start | bytes 196616 | tf_op jit(solution)/shard_map/ppermute | solution.py:281
  6.4 10.4 %collective-permute-start.1 = (bf16[4,8,1024]{2,1,0:T(8,128)(2,1)S(1)}, bf16[4,8,1024]{2,1,0:T(8,128)(2,1)S(1)}, u32[]{:S(2)}, u32[]{:S(2)}) collective-permute-start(bf16[4,8,1024]{2,1,0:T(8,128)(2,1)S(1)} %get-tuple-element.23), channel_id=1, source_target_pairs={{32,0},{64,32},{96,64},{128,96},{160,128},{192,160},{224,192},{256... | collective-permute-start | bytes 196616 | tf_op jit(solution)/shard_map/ppermute | solution.py:281
  16.8 4.0 %all-to-all-start.1 = ((bf16[16,8,1728]{2,1,0:T(8,128)(2,1)}), bf16[16,8,1728]{2,1,0:T(8,128)(2,1)S(1)}, u32[]{:S(2)}, u32[]{:S(2)}) async-start(bf16[16,8,1728]{2,1,0:T(8,128)(2,1)} %get-tuple-element.26), calls=%async_computation.1 | async-start | bytes 917504 | tf_op jit(solution)/shard_map/all_to_all | solution.py:347
  20.8 0.0 collective-permute-done.1.xhi
  20.8 0.1 shard_map.86
  21.0 3.2 %collective-permute-start.2 = (bf16[14,2,1024]{2,1,0:T(2,128)(2,1)S(1)}, bf16[14,2,1024]{2,1,0:T(2,128)(2,1)S(1)}, u32[]{:S(2)}, u32[]{:S(2)}) collective-permute-start(bf16[14,2,1024]{2,1,0:T(2,128)(2,1)S(1)} %get-tuple-element.24), channel_id=1, source_target_pairs={{0,4},{4,8},{8,12},{12,16},{16,20},{20,24},{24,28},{28,0},{1,5},{5... | collective-permute-start | bytes 172040 | tf_op jit(solution)/shard_map/ppermute | solution.py:281
  24.2 3.8 %collective-permute-start.3 = (bf16[14,2,1024]{2,1,0:T(2,128)(2,1)S(1)}, bf16[14,2,1024]{2,1,0:T(2,128)(2,1)S(1)}, u32[]{:S(2)}, u32[]{:S(2)}) collective-permute-start(bf16[14,2,1024]{2,1,0:T(2,128)(2,1)S(1)} %get-tuple-element.25), channel_id=1, source_target_pairs={{4,0},{8,4},{12,8},{16,12},{20,16},{24,20},{28,24},{0,28},{5,1},{9... | collective-permute-start | bytes 172040 | tf_op jit(solution)/shard_map/ppermute | solution.py:281
  28.0 1.4 %collective-permute-done.3.yhi = bf16[14,2,1024]{2,1,0:T(2,128)(2,1)S(1)} collective-permute-done((bf16[14,2,1024]{2,1,0:T(2,128)(2,1)S(1)}, bf16[14,2,1024]{2,1,0:T(2,128)(2,1)S(1)}, u32[]{:S(2)}, u32[]{:S(2)}) %collective-permute-start.3) | collective-permute-done | bytes 57376 | tf_op jit(solution)/shard_map/ppermute | solution.py:281
  29.4 0.8 shard_map.87
  30.2 4.5 %all-to-all-done.1.weights = bf16[16,8,1728]{2,1,0:T(8,128)(2,1)S(1)} async-done(((bf16[16,8,1728]{2,1,0:T(8,128)(2,1)}), bf16[16,8,1728]{2,1,0:T(8,128)(2,1)S(1)}, u32[]{:S(2)}, u32[]{:S(2)}) %all-to-all-start.1) | async-done | bytes 442400 | tf_op jit(solution)/shard_map/all_to_all | solution.py:347
  34.7 7.3 %all-to-all-start = ((bf16[4,168,128]{2,1,0:T(8,128)(2,1)}), bf16[4,168,128]{2,1,0:T(8,128)(2,1)S(1)}, u32[]{:S(2)}, u32[]{:S(2)}) async-start(bf16[4,168,128]{2,1,0:T(8,128)(2,1)} %shard_map.87), calls=%async_computation | async-start | bytes 344064 | tf_op jit(solution)/shard_map/all_to_all | solution.py:355
  42.0 0.6 shard_map.88
  42.7 1.2 %copy-done = bf16[3456,256]{1,0:T(8,128)(2,1)} copy-done((bf16[3456,256]{1,0:T(8,128)(2,1)}, bf16[3456,256]{1,0:T(8,128)(2,1)S(1)}, u32[]{:S(2)}) %copy-start) | copy-done | bytes 1769496
  43.9 3.6 %all-to-all-done.sides = bf16[4,168,128]{2,1,0:T(8,128)(2,1)S(1)} async-done(((bf16[4,168,128]{2,1,0:T(8,128)(2,1)}), bf16[4,168,128]{2,1,0:T(8,128)(2,1)S(1)}, u32[]{:S(2)}, u32[]{:S(2)}) %all-to-all-start) | async-done | bytes 172064 | tf_op jit(solution)/shard_map/all_to_all | solution.py:355
  47.4 1.5 %copy-done.1 = bf16[3456,256]{1,0:T(8,128)(2,1)S(1)} copy-done((bf16[3456,256]{1,0:T(8,128)(2,1)S(1)}, bf16[3456,256]{1,0:T(8,128)(2,1)}, u32[]{:S(2)}) %copy-start.1) | copy-done | bytes 1769496
  48.9 5.0 %shard_map.89 = (bf16[16,4,3456]{2,1,0:T(4,128)(2,1)}, bf16[144,1408]{1,0:T(8,128)(2,1)S(1)}) custom-call(bf16[4,8,1024]{2,1,0:T(8,128)(2,1)S(1)} %get-tuple-element.19.grad, bf16[4,8,1024]{2,1,0:T(8,128)(2,1)S(1)} %get-tuple-element.20.pre, bf16[4,8,1024]{2,1,0:T(8,128)(2,1)S(1)} %get-tuple-element.21.inp, ...), custom_call_target="tpu_custom_call" | custom-call | flops 1800000000 | bytes 8000000 | tf_op jit(solution)/shard_map/pallas_call | solution.py:24
  53.9 3.6 %all-to-all-start.2 = ((bf16[16,4,3456]{2,1,0:T(4,128)(2,1)}), bf16[16,4,3456]{2,1,0:T(4,128)(2,1)S(1)}, u32[]{:S(2)}, u32[]{:S(2)}) async-start(bf16[16,4,3456]{2,1,0:T(4,128)(2,1)} %get-tuple-element.28), calls=%async_computation.2 | async-start | bytes 884736 | tf_op jit(solution)/shard_map/all_to_all | solution.py:309
  57.5 1.3 %shard_map.90 = bf16[4,8,1024]{2,1,0:T(8,128)(2,1)} custom-call(bf16[144,1408]{1,0:T(8,128)(2,1)S(1)} %get-tuple-element.29.pre_grad, bf16[4,8,1024]{2,1,0:T(8,128)(2,1)S(1)} %get-tuple-element.19.grad, bf16[3456,256]{1,0:T(8,128)(2,1)S(1)} %get-tuple-element.30.band), custom_call_target="tpu_custom_call" | custom-call | flops 500000000 | bytes 4000000 | tf_op jit(solution)/shard_map/pallas_call | solution.py:24
  58.9 12.6 %all-to-all-done.2.parts = bf16[16,4,3456]{2,1,0:T(4,128)(2,1)S(1)} async-done(((bf16[16,4,3456]{2,1,0:T(4,128)(2,1)}), bf16[16,4,3456]{2,1,0:T(4,128)(2,1)S(1)}, u32[]{:S(2)}, u32[]{:S(2)}) %all-to-all-start.2) | async-done | bytes 442400 | tf_op jit(solution)/shard_map/all_to_all | solution.py:309
  71.4 0.1 shard_map.91
  71.5 10.1 %all-gather.1.parts = f32[4,4,3456]{2,1,0:T(4,128)S(1)} all-gather(f32[1,4,3456]{2,1,0:T(4,128)S(1)} %bitcast.1), channel_id=2, replica_groups=mesh['gx'=16,'gy'=8,'gz'=4] {'gz'}, dimensions={0}, use_global_device_ids=true | all-gather | bytes 276480 | tf_op jit(solution)/shard_map/all_gather | solution.py:312
  81.6 17.2 %all_to_all.20.parts = bf16[8,4,3456]{2,1,0:T(4,128)(2,1)S(1)} all-to-all(bf16[8,4,3456]{2,1,0:T(4,128)(2,1)S(1)} %shard_map.92), channel_id=1, replica_groups=mesh['gx'=16,'gy'=8,'gz'=4] {'gy'}, dimensions={0} | all-to-all | bytes 442368 | tf_op jit(solution)/shard_map/all_to_all | solution.py:314
  98.8 0.7 shard_map.93
  (5 shorter events, 0.0 us)
Async XLA Ops:
  2.4 18.4 %collective-permute-start = (bf16[4,8,1024]{2,1,0:T(8,128)(2,1)S(1)}, bf16[4,8,1024]{2,1,0:T(8,128)(2,1)S(1)}, u32[]{:S(2)}, u32[]{:S(2)}) collective-permute-start(bf16[4,8,1024]{2,1,0:T(8,128)(2,1)S(1)} %get-tuple-element.22), channel_id=1, source_target_pairs={{0,32},{32,64},{64,96},{96,128},{128,160},{160,192},{192,224},{224... | collective-permute-start | bytes 196616 | tf_op jit(solution)/shard_map/ppermute | solution.py:281
  6.4 14.4 %collective-permute-start.1 = (bf16[4,8,1024]{2,1,0:T(8,128)(2,1)S(1)}, bf16[4,8,1024]{2,1,0:T(8,128)(2,1)S(1)}, u32[]{:S(2)}, u32[]{:S(2)}) collective-permute-start(bf16[4,8,1024]{2,1,0:T(8,128)(2,1)S(1)} %get-tuple-element.23), channel_id=1, source_target_pairs={{32,0},{64,32},{96,64},{128,96},{160,128},{192,160},{224,192},{256... | collective-permute-start | bytes 196616 | tf_op jit(solution)/shard_map/ppermute | solution.py:281
  16.8 17.9 %all-to-all-start.1 = ((bf16[16,8,1728]{2,1,0:T(8,128)(2,1)}), bf16[16,8,1728]{2,1,0:T(8,128)(2,1)S(1)}, u32[]{:S(2)}, u32[]{:S(2)}) async-start(bf16[16,8,1728]{2,1,0:T(8,128)(2,1)} %get-tuple-element.26), calls=%async_computation.1 | async-start | bytes 917504 | tf_op jit(solution)/shard_map/all_to_all | solution.py:347
  21.0 7.0 %collective-permute-start.2 = (bf16[14,2,1024]{2,1,0:T(2,128)(2,1)S(1)}, bf16[14,2,1024]{2,1,0:T(2,128)(2,1)S(1)}, u32[]{:S(2)}, u32[]{:S(2)}) collective-permute-start(bf16[14,2,1024]{2,1,0:T(2,128)(2,1)S(1)} %get-tuple-element.24), channel_id=1, source_target_pairs={{0,4},{4,8},{8,12},{12,16},{16,20},{20,24},{24,28},{28,0},{1,5},{5... | collective-permute-start | bytes 172040 | tf_op jit(solution)/shard_map/ppermute | solution.py:281
  24.2 5.2 %collective-permute-start.3 = (bf16[14,2,1024]{2,1,0:T(2,128)(2,1)S(1)}, bf16[14,2,1024]{2,1,0:T(2,128)(2,1)S(1)}, u32[]{:S(2)}, u32[]{:S(2)}) collective-permute-start(bf16[14,2,1024]{2,1,0:T(2,128)(2,1)S(1)} %get-tuple-element.25), channel_id=1, source_target_pairs={{4,0},{8,4},{12,8},{16,12},{20,16},{24,20},{28,24},{0,28},{5,1},{9... | collective-permute-start | bytes 172040 | tf_op jit(solution)/shard_map/ppermute | solution.py:281
  34.7 12.8 %all-to-all-start = ((bf16[4,168,128]{2,1,0:T(8,128)(2,1)}), bf16[4,168,128]{2,1,0:T(8,128)(2,1)S(1)}, u32[]{:S(2)}, u32[]{:S(2)}) async-start(bf16[4,168,128]{2,1,0:T(8,128)(2,1)} %shard_map.87), calls=%async_computation | async-start | bytes 344064 | tf_op jit(solution)/shard_map/all_to_all | solution.py:355
  42.7 1.2 %copy-start = (bf16[3456,256]{1,0:T(8,128)(2,1)}, bf16[3456,256]{1,0:T(8,128)(2,1)S(1)}, u32[]{:S(2)}) copy-start(bf16[3456,256]{1,0:T(8,128)(2,1)S(1)} %get-tuple-element.27.band) | copy-start | bytes 5308420
  47.4 1.5 %copy-start.1 = (bf16[3456,256]{1,0:T(8,128)(2,1)S(1)}, bf16[3456,256]{1,0:T(8,128)(2,1)}, u32[]{:S(2)}) copy-start(bf16[3456,256]{1,0:T(8,128)(2,1)} %copy-done) | copy-start | bytes 5308420
  53.9 17.5 %all-to-all-start.2 = ((bf16[16,4,3456]{2,1,0:T(4,128)(2,1)}), bf16[16,4,3456]{2,1,0:T(4,128)(2,1)S(1)}, u32[]{:S(2)}, u32[]{:S(2)}) async-start(bf16[16,4,3456]{2,1,0:T(4,128)(2,1)} %get-tuple-element.28), calls=%async_computation.2 | async-start | bytes 884736 | tf_op jit(solution)/shard_map/all_to_all | solution.py:309

commit v5 on v4

--- a/solution.py
+++ b/solution.py
@@ -20,14 +20,14 @@
 LAYERS = 14
 
 
-def call(kernel, outs, scratch, flops, moved, *args, space=pltpu.VMEM):
+def call(kernel, outs, scratch, flops, moved, *args, space=pltpu.VMEM, grant=12):
     return pl.pallas_call(
         kernel,
         out_shape=[jax.ShapeDtypeStruct(shape, dtype) for shape, dtype in outs],
         in_specs=[pl.BlockSpec(memory_space=space)] * len(args),
         out_specs=[pl.BlockSpec(memory_space=pltpu.VMEM)] * len(outs),
         scratch_shapes=[pltpu.VMEM(*held) if isinstance(held, tuple) else held for held in scratch],
-        compiler_params=pltpu.CompilerParams(vmem_limit_bytes=48 * 1024 * 1024),
+        compiler_params=pltpu.CompilerParams(vmem_limit_bytes=grant * 1024 * 1024),
         cost_estimate=pl.CostEstimate(flops=flops, bytes_accessed=moved, transcendentals=0),
     )(*args)
 
@@ -98,13 +98,10 @@
             out[8 + at] = held[...].astype(B16)
 
 
-def zpack_kernel(grad, pre, inp, xlo, xhi, ylo, yhi, slots, held):
+def zpack_kernel(grad, pre, inp, xlo, xhi, ylo, yhi, low, high, held):
     held[...] = jnp.zeros_like(held)
     wide, acts, inputs = fields_of(grad, pre, inp, xlo, xhi)
-    size = slots.shape[0]
-    me = lax.axis_index("gz")
-    slots[...] = jnp.zeros_like(slots)
-    for to, lane, half in ((me + size - 1, 0, True), (me + 1, LANES - 128, False)):
+    for out, lane, half in ((low, 0, True), (high, LANES - 128, False)):
         cut = slice(lane, lane + 128)
         for at, (ref, x) in enumerate(wide):
             row = 12 * at
@@ -127,7 +124,7 @@
             for at, pair in ((row + 1, below), (row + 10, above)):
                 first, second = jnp.broadcast_to(pair[0:1], (8, 128)), jnp.broadcast_to(pair[1:2], (8, 128))
                 held[at : at + 1] = joined(first, second)[0:1]
-        slots[lax.rem(to, size)] = held[...].astype(B16)
+        out[...] = held[...].astype(B16)
 
 
 def bands_kernel(weights, one, two, flat, turned):
@@ -194,13 +191,11 @@
             ]
 
 
-def main_kernel(scale, grad, pre, inp, xlo, xhi, ylo, yhi, sides, band,
+def main_kernel(scale, grad, pre, inp, xlo, xhi, ylo, yhi, below, above, band,
                 slots, pre_out, fg, fa, fi, steps, columns, many, left, left_f, grads_one, grads_two, held, zlo, zhi):
     wide, acts, inputs = fields_of(grad, pre, inp, xlo, xhi)
-    size = sides.shape[0]
-    me = lax.axis_index("gz")
-    zlo[...] = sides[lax.rem(me + size - 1, size)].astype(F32)
-    zhi[...] = sides[lax.rem(me + 1, size)].astype(F32)
+    zlo[...] = below[...].astype(F32)
+    zhi[...] = above[...].astype(F32)
     halos = (ylo, yhi, zlo, zhi)
     fill_wide(fg, wide, *halos)
     fill_thin(fa, acts, 0, *halos)
@@ -345,14 +340,10 @@
     )
     side = ((12 * LAYERS, 128), F32)
     gathered = lax.all_to_all(copies, "gx", 0, 0, tiled=True)
-    (sides,) = call(
-        zpack_kernel,
-        [((lax.axis_size("gz"), 12 * LAYERS, 128), B16)],
-        [side],
-        100000, 700000,
-        *fields, ylo, yhi,
-    )
-    sides = lax.all_to_all(sides, "gz", 0, 0, tiled=True)
+    message = ((12 * LAYERS, 128), B16)
+    below, above = swapped(
+        *call(zpack_kernel, [message, message], [side], 100000, 700000, *fields, ylo, yhi), "gz"
+    )
     matrix = ((DEPTH, 256), B16)
     flat = ((CH, 36 * CH), F32)
     band_one, band_two = call(bands_kernel, [matrix, matrix], [flat, flat], 1000000, 4000000, gathered)
@@ -368,7 +359,8 @@
             ((256, DEPTH), F32), ((256, DEPTH), F32), ((5 * HALO_ROWS, 256), F32), side, side,
         ],
         2 * 900 * 1000 * 1000, 8000000,
-        *fields, ylo, yhi, sides, band_two,
+        *fields, ylo, yhi, below, above, band_two,
+        grant=32,
     )
     (input_grad,) = call(
         last_kernel,

time: 100 us -> 96.3 us (0.963)
  starting transfers between devices: 36.2 us -> 41.7 us
  waiting for transfers between devices: 22 us -> 18.5 us
  local copies, waits for them, and re-layouts: 2.7 us -> 0 us
  blocking collectives: 27.3 us -> 24.9 us
    ppermute x4 -> x6, starting transfers between devices: 21.4 us -> 30.5 us  [swapped(): return (lax.ppermute(high, axis, up), lax.ppermute(low, axis, down))]
    all_to_all x1 -> x0, starting transfers between devices: 7.33 us -> none  [body(): sides = lax.all_to_all(sides, 'gz', 0, 0, tiled=True)]
    all_to_all x1, waiting for transfers between devices: 4.48 us -> 0.01 us  [body(): gathered = lax.all_to_all(copies, 'gx', 0, 0, tiled=True)]
    ppermute x4 -> x6, waiting for transfers between devices: 1.39 us -> 5.65 us  [swapped(): return (lax.ppermute(high, axis, up), lax.ppermute(low, axis, down))]
    all_to_all x1, starting transfers between devices: 3.56 us -> 7.23 us  [reduced(): parts = lax.all_to_all(slots, 'gx', 0, 0, tiled=True)]
    all_to_all x1 -> x0, waiting for transfers between devices: 3.55 us -> none  [body(): sides = lax.all_to_all(sides, 'gz', 0, 0, tiled=True)]
    unnamed x4 -> x0, local copies, waits for them, and re-layouts: 2.7 us -> none
    all_gather x1, blocking collectives: 10.1 us -> 7.46 us  [reduced(): parts = lax.all_gather(part, 'gz', axis=0)]
  transfers between devices with their start and end apart: 7 -> 8, of which waited for: 4 -> 3; matrix products, arithmetic and copies ran while one was open for 0% -> 0% of each run, Pallas kernels for 3% -> 2%
where the time goes in v5:
time: 96.3 us; the launch traced here: 95.7 us
  starting transfers between devices  41.7 us (43%)
  blocking collectives  24.9 us (26%)
  waiting for transfers between devices  18.5 us (19%)
  Pallas kernels  9.84 us (10%)
    ppermute x6, starting transfers between devices, swapped(): return (lax.ppermute(high, axis, up), lax.ppermute(low, axis, down))  30.5 us
    all_to_all x1, blocking collectives, reduced(): parts = lax.all_to_all(copies, 'gy', 0, 0, tiled=True)  17.4 us
    all_to_all x1, waiting for transfers between devices, reduced(): parts = lax.all_to_all(slots, 'gx', 0, 0, tiled=True)  12.9 us
    pallas_call x9, Pallas kernels, call(): pl.pallas_call(kernel, out_shape=[jax.ShapeDtypeStruct(shape, dtype) for...  9.84 us
    all_gather x1, blocking collectives, reduced(): parts = lax.all_gather(part, 'gz', axis=0)  7.46 us
    all_to_all x1, starting transfers between devices, reduced(): parts = lax.all_to_all(slots, 'gx', 0, 0, tiled=True)  7.23 us
    ppermute x6, waiting for transfers between devices, swapped(): return (lax.ppermute(high, axis, up), lax.ppermute(low, axis, down))  5.65 us
    all_to_all x1, starting transfers between devices, body(): gathered = lax.all_to_all(copies, 'gx', 0, 0, tiled=True)  4 us
  transfers between devices with their start and end apart: 8, of which 3 were waited for; matrix products, arithmetic and copies ran while one was open for 0% of the time, Pallas kernels for 2%

profile of v5, /device:TPU:1, one launch (start us, length us, event | category | flops | bytes accessed | tf_op | source)
XLA Modules:
  0.0 95.7 jit_solution(13089108530738212995)
XLA Ops:
  0.6 1.8 %shard_map.85 = (bf16[4,8,1024]{2,1,0:T(8,128)(2,1)S(1)}, bf16[4,8,1024]{2,1,0:T(8,128)(2,1)S(1)}, bf16[4,8,1024]{2,1,0:T(8,128)(2,1)S(1)}, bf16[4,8,1024]{2,1,0...) custom-call(bf16[4,8,1024]{2,1,0:T(8,128)(2,1)} %skip_in.1, ...), custom_call_target="tpu_custom_call" | custom-call | flops 100000 | bytes 400000 | tf_op jit(solution)/shard_map/pallas_call | solution.py:24
  2.4 3.9 %collective-permute-start = (bf16[4,8,1024]{2,1,0:T(8,128)(2,1)S(1)}, bf16[4,8,1024]{2,1,0:T(8,128)(2,1)S(1)}, u32[]{:S(2)}, u32[]{:S(2)}) collective-permute-start(bf16[4,8,1024]{2,1,0:T(8,128)(2,1)S(1)} %get-tuple-element.24), channel_id=1, source_target_pairs={{0,32},{32,64},{64,96},{96,128},{128,160},{160,192},{192,224},{224... | collective-permute-start | bytes 196616 | tf_op jit(solution)/shard_map/ppermute | solution.py:276
  6.4 10.4 %collective-permute-start.1 = (bf16[4,8,1024]{2,1,0:T(8,128)(2,1)S(1)}, bf16[4,8,1024]{2,1,0:T(8,128)(2,1)S(1)}, u32[]{:S(2)}, u32[]{:S(2)}) collective-permute-start(bf16[4,8,1024]{2,1,0:T(8,128)(2,1)S(1)} %get-tuple-element.25), channel_id=1, source_target_pairs={{32,0},{64,32},{96,64},{128,96},{160,128},{192,160},{224,192},{256... | collective-permute-start | bytes 196616 | tf_op jit(solution)/shard_map/ppermute | solution.py:276
  16.8 4.0 %all-to-all-start = ((bf16[16,8,1728]{2,1,0:T(8,128)(2,1)}), bf16[16,8,1728]{2,1,0:T(8,128)(2,1)S(1)}, u32[]{:S(2)}, u32[]{:S(2)}) async-start(bf16[16,8,1728]{2,1,0:T(8,128)(2,1)} %get-tuple-element.30), calls=%async_computation | async-start | bytes 917504 | tf_op jit(solution)/shard_map/all_to_all | solution.py:342
  20.8 0.0 collective-permute-done.xlo
  20.8 0.1 shard_map.86
  21.0 3.2 %collective-permute-start.2 = (bf16[14,2,1024]{2,1,0:T(2,128)(2,1)S(1)}, bf16[14,2,1024]{2,1,0:T(2,128)(2,1)S(1)}, u32[]{:S(2)}, u32[]{:S(2)}) collective-permute-start(bf16[14,2,1024]{2,1,0:T(2,128)(2,1)S(1)} %get-tuple-element.26), channel_id=1, source_target_pairs={{0,4},{4,8},{8,12},{12,16},{16,20},{20,24},{24,28},{28,0},{1,5},{5... | collective-permute-start | bytes 172040 | tf_op jit(solution)/shard_map/ppermute | solution.py:276
  24.2 3.8 %collective-permute-start.3 = (bf16[14,2,1024]{2,1,0:T(2,128)(2,1)S(1)}, bf16[14,2,1024]{2,1,0:T(2,128)(2,1)S(1)}, u32[]{:S(2)}, u32[]{:S(2)}) collective-permute-start(bf16[14,2,1024]{2,1,0:T(2,128)(2,1)S(1)} %get-tuple-element.27), channel_id=1, source_target_pairs={{4,0},{8,4},{12,8},{16,12},{20,16},{24,20},{28,24},{0,28},{5,1},{9... | collective-permute-start | bytes 172040 | tf_op jit(solution)/shard_map/ppermute | solution.py:276
  28.0 0.0 collective-permute-done.2.ylo
  28.0 1.4 %collective-permute-done.3.yhi = bf16[14,2,1024]{2,1,0:T(2,128)(2,1)S(1)} collective-permute-done((bf16[14,2,1024]{2,1,0:T(2,128)(2,1)S(1)}, bf16[14,2,1024]{2,1,0:T(2,128)(2,1)S(1)}, u32[]{:S(2)}, u32[]{:S(2)}) %collective-permute-start.3) | collective-permute-done | bytes 57376 | tf_op jit(solution)/shard_map/ppermute | solution.py:276
  29.4 0.1 shard_map.87
  29.5 7.2 %collective-permute-start.4 = (bf16[168,128]{1,0:T(8,128)(2,1)S(1)}, bf16[168,128]{1,0:T(8,128)(2,1)S(1)}, u32[]{:S(2)}, u32[]{:S(2)}) collective-permute-start(bf16[168,128]{1,0:T(8,128)(2,1)S(1)} %get-tuple-element.28), channel_id=1, source_target_pairs={{0,1},{1,2},{2,3},{3,0},{4,5},{5,6},{6,7},{7,4},{8,9},{9,10},{10,1... | collective-permute-start | bytes 129032 | tf_op jit(solution)/shard_map/ppermute | solution.py:276
  36.7 1.9 %collective-permute-start.5 = (bf16[168,128]{1,0:T(8,128)(2,1)S(1)}, bf16[168,128]{1,0:T(8,128)(2,1)S(1)}, u32[]{:S(2)}, u32[]{:S(2)}) collective-permute-start(bf16[168,128]{1,0:T(8,128)(2,1)S(1)} %get-tuple-element.29), channel_id=1, source_target_pairs={{1,0},{2,1},{3,2},{0,3},{5,4},{6,5},{7,6},{4,7},{9,8},{10,9},{11,1... | collective-permute-start | bytes 129032 | tf_op jit(solution)/shard_map/ppermute | solution.py:276
  38.6 0.6 shard_map.88
  39.3 0.0 collective-permute-done.4.below
  39.3 4.3 %collective-permute-done.5.above = bf16[168,128]{1,0:T(8,128)(2,1)S(1)} collective-permute-done((bf16[168,128]{1,0:T(8,128)(2,1)S(1)}, bf16[168,128]{1,0:T(8,128)(2,1)S(1)}, u32[]{:S(2)}, u32[]{:S(2)}) %collective-permute-start.5) | collective-permute-done | bytes 43040 | tf_op jit(solution)/shard_map/ppermute | solution.py:276
  43.6 5.0 %shard_map.89 = (bf16[16,4,3456]{2,1,0:T(4,128)(2,1)}, bf16[144,1408]{1,0:T(8,128)(2,1)S(1)}) custom-call(bf16[4,8,1024]{2,1,0:T(8,128)(2,1)S(1)} %get-tuple-element.21.grad, bf16[4,8,1024]{2,1,0:T(8,128)(2,1)S(1)} %get-tuple-element.22.pre, bf16[4,8,1024]{2,1,0:T(8,128)(2,1)S(1)} %get-tuple-element.23.inp, ...), custom_call_target="tpu_custom_call" | custom-call | flops 1800000000 | bytes 8000000 | tf_op jit(solution)/shard_map/pallas_call | solution.py:24
  48.6 7.2 %all-to-all-start.1 = ((bf16[16,4,3456]{2,1,0:T(4,128)(2,1)}), bf16[16,4,3456]{2,1,0:T(4,128)(2,1)S(1)}, u32[]{:S(2)}, u32[]{:S(2)}) async-start(bf16[16,4,3456]{2,1,0:T(4,128)(2,1)} %get-tuple-element.32), calls=%async_computation.1 | async-start | bytes 884736 | tf_op jit(solution)/shard_map/all_to_all | solution.py:304
  55.8 1.3 %shard_map.90 = bf16[4,8,1024]{2,1,0:T(8,128)(2,1)} custom-call(bf16[144,1408]{1,0:T(8,128)(2,1)S(1)} %get-tuple-element.33.pre_grad, bf16[4,8,1024]{2,1,0:T(8,128)(2,1)S(1)} %get-tuple-element.21.grad, bf16[3456,256]{1,0:T(8,128)(2,1)S(1)} %get-tuple-element.34.band), custom_call_target="tpu_custom_call" | custom-call | flops 500000000 | bytes 4000000 | tf_op jit(solution)/shard_map/pallas_call | solution.py:24
  57.1 12.9 %all-to-all-done.1.parts = bf16[16,4,3456]{2,1,0:T(4,128)(2,1)S(1)} async-done(((bf16[16,4,3456]{2,1,0:T(4,128)(2,1)}), bf16[16,4,3456]{2,1,0:T(4,128)(2,1)S(1)}, u32[]{:S(2)}, u32[]{:S(2)}) %all-to-all-start.1) | async-done | bytes 442400 | tf_op jit(solution)/shard_map/all_to_all | solution.py:304
  70.0 0.1 shard_map.91
  70.1 7.5 %all-gather.1.parts = f32[4,4,3456]{2,1,0:T(4,128)S(1)} all-gather(f32[1,4,3456]{2,1,0:T(4,128)S(1)} %bitcast.1), channel_id=2, replica_groups=mesh['gx'=16,'gy'=8,'gz'=4] {'gz'}, dimensions={0}, use_global_device_ids=true | all-gather | bytes 276480 | tf_op jit(solution)/shard_map/all_gather | solution.py:307
  77.6 17.4 %all_to_all.15.parts = bf16[8,4,3456]{2,1,0:T(4,128)(2,1)S(1)} all-to-all(bf16[8,4,3456]{2,1,0:T(4,128)(2,1)S(1)} %shard_map.92), channel_id=1, replica_groups=mesh['gx'=16,'gy'=8,'gz'=4] {'gy'}, dimensions={0} | all-to-all | bytes 442368 | tf_op jit(solution)/shard_map/all_to_all | solution.py:309
  95.0 0.7 shard_map.93
  (3 shorter events, 0.0 us)
Async XLA Ops:
  2.4 18.4 %collective-permute-start = (bf16[4,8,1024]{2,1,0:T(8,128)(2,1)S(1)}, bf16[4,8,1024]{2,1,0:T(8,128)(2,1)S(1)}, u32[]{:S(2)}, u32[]{:S(2)}) collective-permute-start(bf16[4,8,1024]{2,1,0:T(8,128)(2,1)S(1)} %get-tuple-element.24), channel_id=1, source_target_pairs={{0,32},{32,64},{64,96},{96,128},{128,160},{160,192},{192,224},{224... | collective-permute-start | bytes 196616 | tf_op jit(solution)/shard_map/ppermute | solution.py:276
  6.4 14.4 %collective-permute-start.1 = (bf16[4,8,1024]{2,1,0:T(8,128)(2,1)S(1)}, bf16[4,8,1024]{2,1,0:T(8,128)(2,1)S(1)}, u32[]{:S(2)}, u32[]{:S(2)}) collective-permute-start(bf16[4,8,1024]{2,1,0:T(8,128)(2,1)S(1)} %get-tuple-element.25), channel_id=1, source_target_pairs={{32,0},{64,32},{96,64},{128,96},{160,128},{192,160},{224,192},{256... | collective-permute-start | bytes 196616 | tf_op jit(solution)/shard_map/ppermute | solution.py:276
  16.8 21.9 %all-to-all-start = ((bf16[16,8,1728]{2,1,0:T(8,128)(2,1)}), bf16[16,8,1728]{2,1,0:T(8,128)(2,1)S(1)}, u32[]{:S(2)}, u32[]{:S(2)}) async-start(bf16[16,8,1728]{2,1,0:T(8,128)(2,1)} %get-tuple-element.30), calls=%async_computation | async-start | bytes 917504 | tf_op jit(solution)/shard_map/all_to_all | solution.py:342
  21.0 7.0 %collective-permute-start.2 = (bf16[14,2,1024]{2,1,0:T(2,128)(2,1)S(1)}, bf16[14,2,1024]{2,1,0:T(2,128)(2,1)S(1)}, u32[]{:S(2)}, u32[]{:S(2)}) collective-permute-start(bf16[14,2,1024]{2,1,0:T(2,128)(2,1)S(1)} %get-tuple-element.26), channel_id=1, source_target_pairs={{0,4},{4,8},{8,12},{12,16},{16,20},{20,24},{24,28},{28,0},{1,5},{5... | collective-permute-start | bytes 172040 | tf_op jit(solution)/shard_map/ppermute | solution.py:276
  24.2 5.2 %collective-permute-start.3 = (bf16[14,2,1024]{2,1,0:T(2,128)(2,1)S(1)}, bf16[14,2,1024]{2,1,0:T(2,128)(2,1)S(1)}, u32[]{:S(2)}, u32[]{:S(2)}) collective-permute-start(bf16[14,2,1024]{2,1,0:T(2,128)(2,1)S(1)} %get-tuple-element.27), channel_id=1, source_target_pairs={{4,0},{8,4},{12,8},{16,12},{20,16},{24,20},{28,24},{0,28},{5,1},{9... | collective-permute-start | bytes 172040 | tf_op jit(solution)/shard_map/ppermute | solution.py:276
  29.5 9.8 %collective-permute-start.4 = (bf16[168,128]{1,0:T(8,128)(2,1)S(1)}, bf16[168,128]{1,0:T(8,128)(2,1)S(1)}, u32[]{:S(2)}, u32[]{:S(2)}) collective-permute-start(bf16[168,128]{1,0:T(8,128)(2,1)S(1)} %get-tuple-element.28), channel_id=1, source_target_pairs={{0,1},{1,2},{2,3},{3,0},{4,5},{5,6},{6,7},{7,4},{8,9},{9,10},{10,1... | collective-permute-start | bytes 129032 | tf_op jit(solution)/shard_map/ppermute | solution.py:276
  36.7 6.8 %collective-permute-start.5 = (bf16[168,128]{1,0:T(8,128)(2,1)S(1)}, bf16[168,128]{1,0:T(8,128)(2,1)S(1)}, u32[]{:S(2)}, u32[]{:S(2)}) collective-permute-start(bf16[168,128]{1,0:T(8,128)(2,1)S(1)} %get-tuple-element.29), channel_id=1, source_target_pairs={{1,0},{2,1},{3,2},{0,3},{5,4},{6,5},{7,6},{4,7},{9,8},{10,9},{11,1... | collective-permute-start | bytes 129032 | tf_op jit(solution)/shard_map/ppermute | solution.py:276
  48.6 21.5 %all-to-all-start.1 = ((bf16[16,4,3456]{2,1,0:T(4,128)(2,1)}), bf16[16,4,3456]{2,1,0:T(4,128)(2,1)S(1)}, u32[]{:S(2)}, u32[]{:S(2)}) async-start(bf16[16,4,3456]{2,1,0:T(4,128)(2,1)} %get-tuple-element.32), calls=%async_computation.1 | async-start | bytes 884736 | tf_op jit(solution)/shard_map/all_to_all | solution.py:304

commit v6 on v5

--- a/solution.py
+++ b/solution.py
@@ -192,7 +192,7 @@
 
 
 def main_kernel(scale, grad, pre, inp, xlo, xhi, ylo, yhi, below, above, band,
-                slots, pre_out, fg, fa, fi, steps, columns, many, left, left_f, grads_one, grads_two, held, zlo, zhi):
+                kept, sent, pre_out, fg, fa, fi, steps, columns, many, left, left_f, grads_one, grads_two, held, zlo, zhi):
     wide, acts, inputs = fields_of(grad, pre, inp, xlo, xhi)
     zlo[...] = below[...].astype(F32)
     zhi[...] = above[...].astype(F32)
@@ -238,23 +238,31 @@
         left[64 * h : 64 * (h + 1), :] = jnp.where(inside, value, 0.0).astype(B16)
     grads_one[...] = lax.dot_general(left[...], columns[...], contract, preferred_element_type=F32)
 
-    count, rows = slots.shape[0], slots.shape[1]
-
-    def block(kk):
-        k, source = (kk, grads_one) if kk < 27 else (kk - 27, grads_two)
+    count, rows = kept.shape[0], kept.shape[1]
+    even = lax.rem(lax.axis_index("gz"), 2) == 0
+
+    def block(source, k):
         m, t = k // 3, k % 3
         same, other = [], []
         for b in range(4):
             lane = (6 * m + b + t) // 2 * 128
             piece = source[64 * b : 64 * (b + 1), lane : lane + 128]
-            (same if (b + t) % 2 == kk % 2 else other).append(piece)
+            (same if (b + t) % 2 == k % 2 else other).append(piece)
         return (same[0] + same[1]) + pltpu.roll(other[0] + other[1], 64, 1)
 
-    for j in range(27):
-        first, second = block(2 * j), block(2 * j + 1)
-        value = jnp.where(low_half(first.shape), first, second) * scale
+    for j in range(14):
+        pair = []
+        for source in (grads_one, grads_two):
+            value = block(source, 2 * j)
+            if j < 13:
+                value = jnp.where(low_half(value.shape), value, block(source, 2 * j + 1))
+            pair.append(value * scale)
+        width = 128 if j < 13 else 64
+        keep = jnp.where(even, pair[0], pair[1])[:, :width]
+        send = jnp.where(even, pair[1], pair[0])[:, :width]
         for g in range(count):
-            slots[g, :, 128 * j : 128 * (j + 1)] = value[g * rows : (g + 1) * rows, :].astype(B16)
+            kept[g, :, 128 * j : 128 * j + width] = keep[g * rows : (g + 1) * rows, :]
+            sent[g, :, 128 * j : 128 * j + width] = send[g * rows : (g + 1) * rows, :].astype(B16)
 
 
 def last_kernel(pre_grad, grad, band, out, steps, columns, held):
@@ -288,27 +296,32 @@
             out[i] = value
 
 
-def last_total_kernel(parts, one, two, held):
-    value = parts[0].astype(F32)
-    for i in range(1, parts.shape[0]):
-        value += parts[i].astype(F32)
-    held[...] = value
-    one[...] = held[:, : 27 * CH]
-    held[...] = pltpu.roll(value, 27 * CH, 1)
-    two[...] = held[:, : 27 * CH]
-
-
-def reduced(slots, other):
-    rows, columns = slots.shape[1:]
-    gy = lax.axis_size("gy")
+def pair_kernel(kept, came, out):
+    out[...] = (kept[...] + came[...].astype(F32)).astype(B16)
+
+
+def last_total_kernel(parts, one, two):
+    first, second = parts[0], parts[1]
+    for i in range(2, parts.shape[0], 2):
+        first += parts[i]
+        second += parts[i + 1]
+    one[...] = first
+    two[...] = second
+
+
+def reduced(kept, sent, other):
+    rows, columns = kept.shape[1:]
+    gy, gz = lax.axis_size("gy"), lax.axis_size("gz")
+    came = lax.ppermute(sent, "gz", [(i, i + 1 - 2 * (i % 2)) for i in range(gz)])
+    came, other = lax.optimization_barrier((came, other))
+    (slots,) = call(pair_kernel, [(kept.shape, B16)], [], 1000, 500000, kept, came)
     parts = lax.all_to_all(slots, "gx", 0, 0, tiled=True)
-    parts, other = lax.optimization_barrier((parts, other))
+    (copies,) = call(total_kernel, [((gy, rows, columns), B16)], [], 1000, 500000, parts)
+    parts = lax.all_to_all(copies, "gy", 0, 0, tiled=True)
     (part,) = call(total_kernel, [((rows, columns), F32)], [], 1000, 500000, parts)
     parts = lax.all_gather(part, "gz", axis=0)
-    (copies,) = call(total_kernel, [((gy, rows, columns), B16)], [], 1000, 500000, parts)
-    parts = lax.all_to_all(copies, "gy", 0, 0, tiled=True)
-    grads = ((rows, 27 * CH), F32)
-    one, two = call(last_total_kernel, [grads, grads], [((rows, columns), F32)], 1000, 500000, parts)
+    grads = ((rows, columns), F32)
+    one, two = call(last_total_kernel, [grads, grads], [], 1000, 500000, parts)
     return other, one, two
 
 
@@ -350,9 +363,9 @@
     field = ((ROWS, WIDE), F32)
     steps = ((3, ROWS, WIDE), B16)
     columns = ((256, DEPTH), B16)
-    slots, pre_grad = call(
+    kept, sent, pre_grad = call(
         functools.partial(main_kernel, 1.0 / math.sqrt(cells)),
-        [((count, rows, 54 * CH), B16), ((ROWS, WIDE), B16)],
+        [((count, rows, 27 * CH), F32), ((count, rows, 27 * CH), B16), ((ROWS, WIDE), B16)],
         [
             field, field, field, steps, columns,
             ((5 * HALO_ROWS, DEPTH), B16), ((256, 256), B16), ((256, 256), F32),
@@ -369,7 +382,7 @@
         500000000, 4000000,
         pre_grad, grad, band_one,
     )
-    return reduced(slots, input_grad)
+    return reduced(kept, sent, input_grad)
 
 
 def solution(mesh):

time: 96.3 us -> 94.5 us (0.981)
  blocking collectives: 24.9 us -> 42.1 us
  waiting for transfers between devices: 18.5 us -> 5.74 us
  starting transfers between devices: 41.7 us -> 36.4 us
    all_to_all x0 -> x1, blocking collectives: none -> 17.3 us  [reduced(): parts = lax.all_to_all(slots, 'gx', 0, 0, tiled=True)]
    all_to_all x1 -> x0, waiting for transfers between devices: 12.9 us -> none  [reduced(): parts = lax.all_to_all(slots, 'gx', 0, 0, tiled=True)]
    all_to_all x1 -> x0, starting transfers between devices: 7.23 us -> none  [reduced(): parts = lax.all_to_all(slots, 'gx', 0, 0, tiled=True)]
    all_to_all x1, blocking collectives: 17.4 us -> 14.7 us  [reduced(): parts = lax.all_to_all(copies, 'gy', 0, 0, tiled=True)]
    all_gather x1, blocking collectives: 7.46 us -> 10.1 us  [reduced(): parts = lax.all_gather(part, 'gz', axis=0)]
    ppermute x0 -> x1, starting transfers between devices: none -> 1.92 us  [reduced(): lax.ppermute(sent, 'gz', [(i, i + 1 - 2 * (i % 2)) for i in range(gz)])]
    pallas_call x9 -> x10, Pallas kernels: 9.84 us -> 9.04 us  [call(): pl.pallas_call(kernel, out_shape=[jax.ShapeDtypeStruct(shape, dtype) for...]
where the time goes in v6:
time: 94.5 us; the launch traced here: 94 us
  blocking collectives  42.1 us (45%)
  starting transfers between devices  36.4 us (39%)
  Pallas kernels  9.04 us (10%)
  waiting for transfers between devices  5.74 us (6%)
    ppermute x6, starting transfers between devices, swapped(): return (lax.ppermute(high, axis, up), lax.ppermute(low, axis, down))  30.5 us
    all_to_all x1, blocking collectives, reduced(): parts = lax.all_to_all(slots, 'gx', 0, 0, tiled=True)  17.3 us
    all_to_all x1, blocking collectives, reduced(): parts = lax.all_to_all(copies, 'gy', 0, 0, tiled=True)  14.7 us
    all_gather x1, blocking collectives, reduced(): parts = lax.all_gather(part, 'gz', axis=0)  10.1 us
    pallas_call x10, Pallas kernels, call(): pl.pallas_call(kernel, out_shape=[jax.ShapeDtypeStruct(shape, dtype) for...  9.04 us
    ppermute x6, waiting for transfers between devices, swapped(): return (lax.ppermute(high, axis, up), lax.ppermute(low, axis, down))  5.65 us
    all_to_all x1, starting transfers between devices, body(): gathered = lax.all_to_all(copies, 'gx', 0, 0, tiled=True)  4 us
    ppermute x1, starting transfers between devices, reduced(): lax.ppermute(sent, 'gz', [(i, i + 1 - 2 * (i % 2)) for i in range(gz)])  1.92 us
  transfers between devices with their start and end apart: 8, of which 3 were waited for; matrix products, arithmetic and copies ran while one was open for 0% of the time, Pallas kernels for 2%

profile of v6, /device:TPU:1, one launch (start us, length us, event | category | flops | bytes accessed | tf_op | source)
XLA Modules:
  0.0 94.0 jit_solution(11498924504381652152)
XLA Ops:
  0.6 1.8 %shard_map.85 = (bf16[4,8,1024]{2,1,0:T(8,128)(2,1)S(1)}, bf16[4,8,1024]{2,1,0:T(8,128)(2,1)S(1)}, bf16[4,8,1024]{2,1,0:T(8,128)(2,1)S(1)}, bf16[4,8,1024]{2,1,0...) custom-call(bf16[4,8,1024]{2,1,0:T(8,128)(2,1)} %skip_in.1, ...), custom_call_target="tpu_custom_call" | custom-call | flops 100000 | bytes 400000 | tf_op jit(solution)/shard_map/pallas_call | solution.py:24
  2.4 3.9 %collective-permute-start = (bf16[4,8,1024]{2,1,0:T(8,128)(2,1)S(1)}, bf16[4,8,1024]{2,1,0:T(8,128)(2,1)S(1)}, u32[]{:S(2)}, u32[]{:S(2)}) collective-permute-start(bf16[4,8,1024]{2,1,0:T(8,128)(2,1)S(1)} %get-tuple-element.25), channel_id=1, source_target_pairs={{0,32},{32,64},{64,96},{96,128},{128,160},{160,192},{192,224},{224... | collective-permute-start | bytes 196616 | tf_op jit(solution)/shard_map/ppermute | solution.py:284
  6.4 10.4 %collective-permute-start.1 = (bf16[4,8,1024]{2,1,0:T(8,128)(2,1)S(1)}, bf16[4,8,1024]{2,1,0:T(8,128)(2,1)S(1)}, u32[]{:S(2)}, u32[]{:S(2)}) collective-permute-start(bf16[4,8,1024]{2,1,0:T(8,128)(2,1)S(1)} %get-tuple-element.26), channel_id=1, source_target_pairs={{32,0},{64,32},{96,64},{128,96},{160,128},{192,160},{224,192},{256... | collective-permute-start | bytes 196616 | tf_op jit(solution)/shard_map/ppermute | solution.py:284
  16.8 4.0 %all-to-all-start = ((bf16[16,8,1728]{2,1,0:T(8,128)(2,1)}), bf16[16,8,1728]{2,1,0:T(8,128)(2,1)S(1)}, u32[]{:S(2)}, u32[]{:S(2)}) async-start(bf16[16,8,1728]{2,1,0:T(8,128)(2,1)} %get-tuple-element.31), calls=%async_computation | async-start | bytes 917504 | tf_op jit(solution)/shard_map/all_to_all | solution.py:355
  20.8 0.0 collective-permute-done.1.xhi
  20.8 0.1 shard_map.86
  21.0 3.2 %collective-permute-start.2 = (bf16[14,2,1024]{2,1,0:T(2,128)(2,1)S(1)}, bf16[14,2,1024]{2,1,0:T(2,128)(2,1)S(1)}, u32[]{:S(2)}, u32[]{:S(2)}) collective-permute-start(bf16[14,2,1024]{2,1,0:T(2,128)(2,1)S(1)} %get-tuple-element.27), channel_id=1, source_target_pairs={{0,4},{4,8},{8,12},{12,16},{16,20},{20,24},{24,28},{28,0},{1,5},{5... | collective-permute-start | bytes 172040 | tf_op jit(solution)/shard_map/ppermute | solution.py:284
  24.2 3.8 %collective-permute-start.3 = (bf16[14,2,1024]{2,1,0:T(2,128)(2,1)S(1)}, bf16[14,2,1024]{2,1,0:T(2,128)(2,1)S(1)}, u32[]{:S(2)}, u32[]{:S(2)}) collective-permute-start(bf16[14,2,1024]{2,1,0:T(2,128)(2,1)S(1)} %get-tuple-element.28), channel_id=1, source_target_pairs={{4,0},{8,4},{12,8},{16,12},{20,16},{24,20},{28,24},{0,28},{5,1},{9... | collective-permute-start | bytes 172040 | tf_op jit(solution)/shard_map/ppermute | solution.py:284
  28.0 1.4 %collective-permute-done.3.yhi = bf16[14,2,1024]{2,1,0:T(2,128)(2,1)S(1)} collective-permute-done((bf16[14,2,1024]{2,1,0:T(2,128)(2,1)S(1)}, bf16[14,2,1024]{2,1,0:T(2,128)(2,1)S(1)}, u32[]{:S(2)}, u32[]{:S(2)}) %collective-permute-start.3) | collective-permute-done | bytes 57376 | tf_op jit(solution)/shard_map/ppermute | solution.py:284
  29.4 0.1 shard_map.87
  29.5 7.2 %collective-permute-start.4 = (bf16[168,128]{1,0:T(8,128)(2,1)S(1)}, bf16[168,128]{1,0:T(8,128)(2,1)S(1)}, u32[]{:S(2)}, u32[]{:S(2)}) collective-permute-start(bf16[168,128]{1,0:T(8,128)(2,1)S(1)} %get-tuple-element.29), channel_id=1, source_target_pairs={{0,1},{1,2},{2,3},{3,0},{4,5},{5,6},{6,7},{7,4},{8,9},{9,10},{10,1... | collective-permute-start | bytes 129032 | tf_op jit(solution)/shard_map/ppermute | solution.py:284
  36.7 1.9 %collective-permute-start.5 = (bf16[168,128]{1,0:T(8,128)(2,1)S(1)}, bf16[168,128]{1,0:T(8,128)(2,1)S(1)}, u32[]{:S(2)}, u32[]{:S(2)}) collective-permute-start(bf16[168,128]{1,0:T(8,128)(2,1)S(1)} %get-tuple-element.30), channel_id=1, source_target_pairs={{1,0},{2,1},{3,2},{0,3},{5,4},{6,5},{7,6},{4,7},{9,8},{10,9},{11,1... | collective-permute-start | bytes 129032 | tf_op jit(solution)/shard_map/ppermute | solution.py:284
  38.6 0.0 all-to-all-done.weights
  38.7 0.6 shard_map.88
  39.3 4.3 %collective-permute-done.5.above = bf16[168,128]{1,0:T(8,128)(2,1)S(1)} collective-permute-done((bf16[168,128]{1,0:T(8,128)(2,1)S(1)}, bf16[168,128]{1,0:T(8,128)(2,1)S(1)}, u32[]{:S(2)}, u32[]{:S(2)}) %collective-permute-start.5) | collective-permute-done | bytes 43040 | tf_op jit(solution)/shard_map/ppermute | solution.py:284
  43.6 4.2 %shard_map.89 = (f32[16,4,1728]{2,1,0:T(4,128)S(1)}, bf16[16,4,1728]{2,1,0:T(4,128)(2,1)S(1)}, bf16[144,1408]{1,0:T(8,128)(2,1)S(1)}) custom-call(bf16[4,8,1024]{2,1,0:T(8,128)(2,1)S(1)} %get-tuple-element.22.grad, bf16[4,8,1024]{2,1,0:T(8,128)(2,1)S(1)} %get-tuple-element.23.pre, bf16[4,8,1024]{2,1,0:T(8,128)(2,1)S(1)} %get-tuple-element.24.inp, ...), custom_call_target="tpu_custom_call" | custom-call | flops 1800000000 | bytes 8000000 | tf_op jit(solution)/shard_map/pallas_call | solution.py:24
  47.8 1.9 %collective-permute-start.6 = (bf16[16,4,1728]{2,1,0:T(4,128)(2,1)S(1)}, bf16[16,4,1728]{2,1,0:T(4,128)(2,1)S(1)}, u32[]{:S(2)}, u32[]{:S(2)}) collective-permute-start(bf16[16,4,1728]{2,1,0:T(4,128)(2,1)S(1)} %get-tuple-element.33), channel_id=1, source_target_pairs={{0,1},{1,0},{2,3},{3,2},{4,5},{5,4},{6,7},{7,6},{8,9},{9,8},{10,11... | collective-permute-start | bytes 663560 | tf_op jit(solution)/shard_map/ppermute | solution.py:315
  49.7 1.4 %shard_map.90 = bf16[4,8,1024]{2,1,0:T(8,128)(2,1)} custom-call(bf16[144,1408]{1,0:T(8,128)(2,1)S(1)} %get-tuple-element.34.pre_grad, bf16[4,8,1024]{2,1,0:T(8,128)(2,1)S(1)} %get-tuple-element.22.grad, bf16[3456,256]{1,0:T(8,128)(2,1)S(1)} %get-tuple-element.35.band), custom_call_target="tpu_custom_call" | custom-call | flops 500000000 | bytes 4000000 | tf_op jit(solution)/shard_map/pallas_call | solution.py:24
  51.1 0.1 collective-permute-done.6.came
  51.1 0.1 shard_map.91
  51.2 17.3 %all_to_all.15.parts = bf16[16,4,1728]{2,1,0:T(4,128)(2,1)S(1)} all-to-all(bf16[16,4,1728]{2,1,0:T(4,128)(2,1)S(1)} %shard_map.91), channel_id=1, replica_groups=mesh['gx'=16,'gy'=8,'gz'=4] {'gx'}, dimensions={0} | all-to-all | bytes 442368 | tf_op jit(solution)/shard_map/all_to_all | solution.py:318
  68.6 14.7 %all_to_all.16.parts = bf16[8,4,1728]{2,1,0:T(4,128)(2,1)S(1)} all-to-all(bf16[8,4,1728]{2,1,0:T(4,128)(2,1)S(1)} %shard_map.92), channel_id=1, replica_groups=mesh['gx'=16,'gy'=8,'gz'=4] {'gy'}, dimensions={0} | all-to-all | bytes 221184 | tf_op jit(solution)/shard_map/all_to_all | solution.py:320
  83.2 10.1 %all-gather.1.parts = f32[4,4,1728]{2,1,0:T(4,128)S(1)} all-gather(f32[1,4,1728]{2,1,0:T(4,128)S(1)} %bitcast.1), channel_id=2, replica_groups=mesh['gx'=16,'gy'=8,'gz'=4] {'gz'}, dimensions={0}, use_global_device_ids=true | all-gather | bytes 138240 | tf_op jit(solution)/shard_map/all_gather | solution.py:322
  93.4 0.6 shard_map.94
  (5 shorter events, 0.1 us)
Async XLA Ops:
  2.4 18.4 %collective-permute-start = (bf16[4,8,1024]{2,1,0:T(8,128)(2,1)S(1)}, bf16[4,8,1024]{2,1,0:T(8,128)(2,1)S(1)}, u32[]{:S(2)}, u32[]{:S(2)}) collective-permute-start(bf16[4,8,1024]{2,1,0:T(8,128)(2,1)S(1)} %get-tuple-element.25), channel_id=1, source_target_pairs={{0,32},{32,64},{64,96},{96,128},{128,160},{160,192},{192,224},{224... | collective-permute-start | bytes 196616 | tf_op jit(solution)/shard_map/ppermute | solution.py:284
  6.4 14.4 %collective-permute-start.1 = (bf16[4,8,1024]{2,1,0:T(8,128)(2,1)S(1)}, bf16[4,8,1024]{2,1,0:T(8,128)(2,1)S(1)}, u32[]{:S(2)}, u32[]{:S(2)}) collective-permute-start(bf16[4,8,1024]{2,1,0:T(8,128)(2,1)S(1)} %get-tuple-element.26), channel_id=1, source_target_pairs={{32,0},{64,32},{96,64},{128,96},{160,128},{192,160},{224,192},{256... | collective-permute-start | bytes 196616 | tf_op jit(solution)/shard_map/ppermute | solution.py:284
  16.8 21.9 %all-to-all-start = ((bf16[16,8,1728]{2,1,0:T(8,128)(2,1)}), bf16[16,8,1728]{2,1,0:T(8,128)(2,1)S(1)}, u32[]{:S(2)}, u32[]{:S(2)}) async-start(bf16[16,8,1728]{2,1,0:T(8,128)(2,1)} %get-tuple-element.31), calls=%async_computation | async-start | bytes 917504 | tf_op jit(solution)/shard_map/all_to_all | solution.py:355
  21.0 7.0 %collective-permute-start.2 = (bf16[14,2,1024]{2,1,0:T(2,128)(2,1)S(1)}, bf16[14,2,1024]{2,1,0:T(2,128)(2,1)S(1)}, u32[]{:S(2)}, u32[]{:S(2)}) collective-permute-start(bf16[14,2,1024]{2,1,0:T(2,128)(2,1)S(1)} %get-tuple-element.27), channel_id=1, source_target_pairs={{0,4},{4,8},{8,12},{12,16},{16,20},{20,24},{24,28},{28,0},{1,5},{5... | collective-permute-start | bytes 172040 | tf_op jit(solution)/shard_map/ppermute | solution.py:284
  24.2 5.2 %collective-permute-start.3 = (bf16[14,2,1024]{2,1,0:T(2,128)(2,1)S(1)}, bf16[14,2,1024]{2,1,0:T(2,128)(2,1)S(1)}, u32[]{:S(2)}, u32[]{:S(2)}) collective-permute-start(bf16[14,2,1024]{2,1,0:T(2,128)(2,1)S(1)} %get-tuple-element.28), channel_id=1, source_target_pairs={{4,0},{8,4},{12,8},{16,12},{20,16},{24,20},{28,24},{0,28},{5,1},{9... | collective-permute-start | bytes 172040 | tf_op jit(solution)/shard_map/ppermute | solution.py:284
  29.5 9.8 %collective-permute-start.4 = (bf16[168,128]{1,0:T(8,128)(2,1)S(1)}, bf16[168,128]{1,0:T(8,128)(2,1)S(1)}, u32[]{:S(2)}, u32[]{:S(2)}) collective-permute-start(bf16[168,128]{1,0:T(8,128)(2,1)S(1)} %get-tuple-element.29), channel_id=1, source_target_pairs={{0,1},{1,2},{2,3},{3,0},{4,5},{5,6},{6,7},{7,4},{8,9},{9,10},{10,1... | collective-permute-start | bytes 129032 | tf_op jit(solution)/shard_map/ppermute | solution.py:284
  36.7 6.8 %collective-permute-start.5 = (bf16[168,128]{1,0:T(8,128)(2,1)S(1)}, bf16[168,128]{1,0:T(8,128)(2,1)S(1)}, u32[]{:S(2)}, u32[]{:S(2)}) collective-permute-start(bf16[168,128]{1,0:T(8,128)(2,1)S(1)} %get-tuple-element.30), channel_id=1, source_target_pairs={{1,0},{2,1},{3,2},{0,3},{5,4},{6,5},{7,6},{4,7},{9,8},{10,9},{11,1... | collective-permute-start | bytes 129032 | tf_op jit(solution)/shard_map/ppermute | solution.py:284
  47.8 3.4 %collective-permute-start.6 = (bf16[16,4,1728]{2,1,0:T(4,128)(2,1)S(1)}, bf16[16,4,1728]{2,1,0:T(4,128)(2,1)S(1)}, u32[]{:S(2)}, u32[]{:S(2)}) collective-permute-start(bf16[16,4,1728]{2,1,0:T(4,128)(2,1)S(1)} %get-tuple-element.33), channel_id=1, source_target_pairs={{0,1},{1,0},{2,3},{3,2},{4,5},{5,4},{6,7},{7,6},{8,9},{9,8},{10,11... | collective-permute-start | bytes 663560 | tf_op jit(solution)/shard_map/ppermute | solution.py:315

commit v7 on v6

--- a/solution.py
+++ b/solution.py
@@ -36,8 +36,27 @@
     return lax.broadcasted_iota(jnp.int32, shape, len(shape) - 1) % 128 < 64
 
 
+class Either:
+    def __init__(self, axis, if_odd, if_even):
+        self.odd = lax.rem(lax.axis_index(axis), 2) == 1
+        self.refs = if_odd, if_even
+
+    def __getitem__(self, at):
+        first, second = (ref[at].astype(F32) for ref in self.refs)
+        return jnp.where(self.odd, first, second)
+
+
+def below_above(axis, far, near):
+    return Either(axis, near, far), Either(axis, far, near)
+
+
+def far_near(axis, low, high):
+    odd = lax.rem(lax.axis_index(axis), 2) == 1
+    return jnp.where(odd, high, low).astype(B16), jnp.where(odd, low, high).astype(B16)
+
+
 def prep_kernel(skip_in, pool_in, pre_in, inp_in, one_in, two_in,
-                grad, pre, inp, low, high, copies, skip, pool, one, two, up, rows, sems):
+                grad, pre, inp, far, near, copies, skip, pool, one, two, up, rows, sems):
     moves = [
         pltpu.make_async_copy(source, target, sems.at[i])
         for i, (source, target) in enumerate(
@@ -66,12 +85,9 @@
     for x in range(SX):
         value = (skip[x].astype(F32) + 0.125 * up[x // 2]).astype(B16)
         grad[x] = value
-        if x < 2:
-            low[x] = value
-        else:
-            high[x - 2] = value
-    low[2], low[3] = pre[0], inp[0]
-    high[2], high[3] = pre[SX - 1], inp[SX - 1]
+    ends = ((grad, 0, 2), (grad, 1, 3), (pre, 0, SX - 1), (inp, 0, SX - 1))
+    for at, (ref, bottom, top) in enumerate(ends):
+        far[at], near[at] = far_near("gx", ref[bottom].astype(F32), ref[top].astype(F32))
 
 
 def fields_of(grad, pre, inp, xlo, xhi):
@@ -85,23 +101,23 @@
     )
 
 
-def ypack_kernel(grad, pre, inp, xlo, xhi, low, high, held):
-    wide, acts, inputs = fields_of(grad, pre, inp, xlo, xhi)
+def ypack_kernel(grad, pre, inp, xfar, xnear, far, near, held):
+    wide, acts, inputs = fields_of(grad, pre, inp, *below_above("gx", xfar, xnear))
     for at, (ref, x) in enumerate(wide):
         value = ref[x].astype(F32)
-        low[at] = value[0:2].astype(B16)
-        high[at] = value[SY - 2 : SY].astype(B16)
-    for out, row in ((low, 0), (high, SY - 1)):
-        for at, ((a, ax), (i, ix)) in enumerate(zip(acts, inputs)):
-            held[0:1] = a[ax].astype(F32)[row : row + 1]
-            held[1:2] = i[ix].astype(F32)[row : row + 1]
-            out[8 + at] = held[...].astype(B16)
-
-
-def zpack_kernel(grad, pre, inp, xlo, xhi, ylo, yhi, low, high, held):
-    held[...] = jnp.zeros_like(held)
-    wide, acts, inputs = fields_of(grad, pre, inp, xlo, xhi)
-    for out, lane, half in ((low, 0, True), (high, LANES - 128, False)):
+        far[at], near[at] = far_near("gy", value[0:2], value[SY - 2 : SY])
+    for at, ((a, ax), (i, ix)) in enumerate(zip(acts, inputs)):
+        v, w = a[ax].astype(F32), i[ix].astype(F32)
+        held[0:1], held[1:2] = v[0:1], w[0:1]
+        held[2:3], held[3:4] = v[SY - 1 :], w[SY - 1 :]
+        far[8 + at], near[8 + at] = far_near("gy", held[0:2], held[2:4])
+
+
+def zpack_kernel(grad, pre, inp, xfar, xnear, yfar, ynear, far, near, low, high):
+    wide, acts, inputs = fields_of(grad, pre, inp, *below_above("gx", xfar, xnear))
+    ylo, yhi = below_above("gy", yfar, ynear)
+    for held, lane, half in ((low, 0, True), (high, LANES - 128, False)):
+        held[...] = jnp.zeros_like(held)
         cut = slice(lane, lane + 128)
         for at, (ref, x) in enumerate(wide):
             row = 12 * at
@@ -124,7 +140,7 @@
             for at, pair in ((row + 1, below), (row + 10, above)):
                 first, second = jnp.broadcast_to(pair[0:1], (8, 128)), jnp.broadcast_to(pair[1:2], (8, 128))
                 held[at : at + 1] = joined(first, second)[0:1]
-        out[...] = held[...].astype(B16)
+    far[...], near[...] = far_near("gz", low[...], high[...])
 
 
 def bands_kernel(weights, one, two, flat, turned):
@@ -191,11 +207,13 @@
             ]
 
 
-def main_kernel(scale, grad, pre, inp, xlo, xhi, ylo, yhi, below, above, band,
+def main_kernel(scale, grad, pre, inp, xfar, xnear, yfar, ynear, zfar, znear, band,
                 kept, sent, pre_out, fg, fa, fi, steps, columns, many, left, left_f, grads_one, grads_two, held, zlo, zhi):
-    wide, acts, inputs = fields_of(grad, pre, inp, xlo, xhi)
-    zlo[...] = below[...].astype(F32)
-    zhi[...] = above[...].astype(F32)
+    wide, acts, inputs = fields_of(grad, pre, inp, *below_above("gx", xfar, xnear))
+    ylo, yhi = below_above("gy", yfar, ynear)
+    below, above = below_above("gz", zfar, znear)
+    zlo[...] = below[...]
+    zhi[...] = above[...]
     halos = (ylo, yhi, zlo, zhi)
     fill_wide(fg, wide, *halos)
     fill_thin(fa, acts, 0, *halos)
@@ -277,11 +295,13 @@
             out[x, :, lanes] = (held[row : row + 8, :] + grad[x, :, lanes].astype(F32)).astype(B16)
 
 
-def swapped(low, high, axis):
+def swapped(far, near, axis):
     count = lax.axis_size(axis)
-    up = [(i, (i + 1) % count) for i in range(count)]
-    down = [(target, source) for source, target in up]
-    return lax.ppermute(high, axis, up), lax.ppermute(low, axis, down)
+    steps = [1 if i % 2 else -1 for i in range(count)]
+    return (
+        lax.ppermute(far, axis, [(i, (i + step) % count) for i, step in enumerate(steps)]),
+        lax.ppermute(near, axis, [(i, i - step) for i, step in enumerate(steps)]),
+    )
 
 
 def total_kernel(parts, out):
@@ -331,7 +351,7 @@
     cells = SX * SY * SZ * count * lax.axis_size("gy") * lax.axis_size("gz")
     block, message = ((SX, SY, LANES), B16), ((4, SY, LANES), B16)
     weight = ((rows, 27 * CH), B16)
-    grad, pre, inp, low, high, copies = call(
+    grad, pre, inp, far, near, copies = call(
         prep_kernel,
         [block, block, block, message, message, ((count, 2 * rows, 27 * CH), B16)],
         [
@@ -345,17 +365,17 @@
         ),
         space=pltpu.HBM,
     )
-    xlo, xhi = swapped(low, high, "gx")
-    fields = (grad, pre, inp, xlo, xhi)
+    xfar, xnear = swapped(far, near, "gx")
+    fields = (grad, pre, inp, xfar, xnear)
     message = ((LAYERS, 2, LANES), B16)
-    ylo, yhi = swapped(
-        *call(ypack_kernel, [message, message], [((2, LANES), F32)], 60000000000, 600000, *fields), "gy"
+    yfar, ynear = swapped(
+        *call(ypack_kernel, [message, message], [((4, LANES), F32)], 60000000000, 600000, *fields), "gy"
     )
     side = ((12 * LAYERS, 128), F32)
     gathered = lax.all_to_all(copies, "gx", 0, 0, tiled=True)
     message = ((12 * LAYERS, 128), B16)
-    below, above = swapped(
-        *call(zpack_kernel, [message, message], [side], 100000, 700000, *fields, ylo, yhi), "gz"
+    zfar, znear = swapped(
+        *call(zpack_kernel, [message, message], [side, side], 100000, 700000, *fields, yfar, ynear), "gz"
     )
     matrix = ((DEPTH, 256), B16)
     flat = ((CH, 36 * CH), F32)
@@ -372,7 +392,7 @@
             ((256, DEPTH), F32), ((256, DEPTH), F32), ((5 * HALO_ROWS, 256), F32), side, side,
         ],
         2 * 900 * 1000 * 1000, 8000000,
-        *fields, ylo, yhi, below, above, band_two,
+        *fields, yfar, ynear, zfar, znear, band_two,
         grant=32,
     )
     (input_grad,) = call(

time: 94.5 us -> 88.6 us (0.938)
  blocking collectives: 42.1 us -> 38.4 us
  waiting for transfers between devices: 5.74 us -> 3.82 us
    all_to_all x1, blocking collectives: 14.7 us -> 11.6 us  [reduced(): parts = lax.all_to_all(copies, 'gy', 0, 0, tiled=True)]
    ppermute x6, waiting for transfers between devices: 5.65 us -> 3.81 us  [the longest x3 3.8 us: swapped(): lax.ppermute(near, axis, [(i, i - step) for i, step in enumerate(steps)])]
  transfers between devices with their start and end apart: 8 -> 8, of which waited for: 3 -> 2; matrix products, arithmetic and copies ran while one was open for 0% -> 0% of each run, Pallas kernels for 2% -> 3%
where the time goes in v7:
time: 88.6 us; the launch traced here: 88.1 us
  blocking collectives  38.4 us (43%)
  starting transfers between devices  35.9 us (41%)
  Pallas kernels  9.16 us (10%)
  waiting for transfers between devices  3.82 us (4%)
    ppermute x3, starting transfers between devices, swapped(): lax.ppermute(far, axis, [(i, (i + step) % count) for i, step in enumerate...  24.5 us
    all_to_all x1, blocking collectives, reduced(): parts = lax.all_to_all(slots, 'gx', 0, 0, tiled=True)  16.8 us
    all_to_all x1, blocking collectives, reduced(): parts = lax.all_to_all(copies, 'gy', 0, 0, tiled=True)  11.6 us
    all_gather x1, blocking collectives, reduced(): parts = lax.all_gather(part, 'gz', axis=0)  10 us
    pallas_call x10, Pallas kernels, call(): pl.pallas_call(kernel, out_shape=[jax.ShapeDtypeStruct(shape, dtype) for...  9.16 us
    ppermute x3, starting transfers between devices, swapped(): lax.ppermute(near, axis, [(i, i - step) for i, step in enumerate(steps)])  5.76 us
    ppermute x3, waiting for transfers between devices, swapped(): lax.ppermute(near, axis, [(i, i - step) for i, step in enumerate(steps)])  3.8 us
    all_to_all x1, starting transfers between devices, body(): gathered = lax.all_to_all(copies, 'gx', 0, 0, tiled=True)  3.57 us
  transfers between devices with their start and end apart: 8, of which 2 were waited for; matrix products, arithmetic and copies ran while one was open for 0% of the time, Pallas kernels for 3%

profile of v7, /device:TPU:1, one launch (start us, length us, event | category | flops | bytes accessed | tf_op | source)
XLA Modules:
  0.0 88.1 jit_solution(14642904323566977834)
XLA Ops:
  0.6 1.8 %shard_map.85 = (bf16[4,8,1024]{2,1,0:T(8,128)(2,1)S(1)}, bf16[4,8,1024]{2,1,0:T(8,128)(2,1)S(1)}, bf16[4,8,1024]{2,1,0:T(8,128)(2,1)S(1)}, bf16[4,8,1024]{2,1,0...) custom-call(bf16[4,8,1024]{2,1,0:T(8,128)(2,1)} %skip_in.1, ...), custom_call_target="tpu_custom_call" | custom-call | flops 100000 | bytes 400000 | tf_op jit(solution)/shard_map/pallas_call | solution.py:24
  2.4 12.4 %collective-permute-start = (bf16[4,8,1024]{2,1,0:T(8,128)(2,1)S(1)}, bf16[4,8,1024]{2,1,0:T(8,128)(2,1)S(1)}, u32[]{:S(2)}, u32[]{:S(2)}) collective-permute-start(bf16[4,8,1024]{2,1,0:T(8,128)(2,1)S(1)} %get-tuple-element.25), channel_id=1, source_target_pairs={{0,480},{32,64},{64,32},{96,128},{128,96},{160,192},{192,160},{224... | collective-permute-start | bytes 196616 | tf_op jit(solution)/shard_map/ppermute | solution.py:302
  14.9 1.9 %collective-permute-start.1 = (bf16[4,8,1024]{2,1,0:T(8,128)(2,1)S(1)}, bf16[4,8,1024]{2,1,0:T(8,128)(2,1)S(1)}, u32[]{:S(2)}, u32[]{:S(2)}) collective-permute-start(bf16[4,8,1024]{2,1,0:T(8,128)(2,1)S(1)} %get-tuple-element.26), channel_id=1, source_target_pairs={{0,32},{32,0},{64,96},{96,64},{128,160},{160,128},{192,224},{224,1... | collective-permute-start | bytes 196616 | tf_op jit(solution)/shard_map/ppermute | solution.py:303
  16.8 3.6 %all-to-all-start = ((bf16[16,8,1728]{2,1,0:T(8,128)(2,1)}), bf16[16,8,1728]{2,1,0:T(8,128)(2,1)S(1)}, u32[]{:S(2)}, u32[]{:S(2)}) async-start(bf16[16,8,1728]{2,1,0:T(8,128)(2,1)} %get-tuple-element.31), calls=%async_computation | async-start | bytes 917504 | tf_op jit(solution)/shard_map/all_to_all | solution.py:375
  20.4 0.0 collective-permute-done.xfar
  20.4 0.0 collective-permute-done.1.xnear
  20.4 0.2 shard_map.86
  20.6 5.1 %collective-permute-start.2 = (bf16[14,2,1024]{2,1,0:T(2,128)(2,1)S(1)}, bf16[14,2,1024]{2,1,0:T(2,128)(2,1)S(1)}, u32[]{:S(2)}, u32[]{:S(2)}) collective-permute-start(bf16[14,2,1024]{2,1,0:T(2,128)(2,1)S(1)} %get-tuple-element.27), channel_id=1, source_target_pairs={{0,28},{4,8},{8,4},{12,16},{16,12},{20,24},{24,20},{28,0},{1,29},{... | collective-permute-start | bytes 172040 | tf_op jit(solution)/shard_map/ppermute | solution.py:302
  25.7 1.9 %collective-permute-start.3 = (bf16[14,2,1024]{2,1,0:T(2,128)(2,1)S(1)}, bf16[14,2,1024]{2,1,0:T(2,128)(2,1)S(1)}, u32[]{:S(2)}, u32[]{:S(2)}) collective-permute-start(bf16[14,2,1024]{2,1,0:T(2,128)(2,1)S(1)} %get-tuple-element.28), channel_id=1, source_target_pairs={{0,4},{4,0},{8,12},{12,8},{16,20},{20,16},{24,28},{28,24},{1,5},{5... | collective-permute-start | bytes 172040 | tf_op jit(solution)/shard_map/ppermute | solution.py:303
  27.7 3.3 %collective-permute-done.3.ynear = bf16[14,2,1024]{2,1,0:T(2,128)(2,1)S(1)} collective-permute-done((bf16[14,2,1024]{2,1,0:T(2,128)(2,1)S(1)}, bf16[14,2,1024]{2,1,0:T(2,128)(2,1)S(1)}, u32[]{:S(2)}, u32[]{:S(2)}) %collective-permute-start.3) | collective-permute-done | bytes 57376 | tf_op jit(solution)/shard_map/ppermute | solution.py:303
  30.9 0.1 shard_map.87
  31.1 7.0 %collective-permute-start.4 = (bf16[168,128]{1,0:T(8,128)(2,1)S(1)}, bf16[168,128]{1,0:T(8,128)(2,1)S(1)}, u32[]{:S(2)}, u32[]{:S(2)}) collective-permute-start(bf16[168,128]{1,0:T(8,128)(2,1)S(1)} %get-tuple-element.29), channel_id=1, source_target_pairs={{0,3},{1,2},{2,1},{3,0},{4,7},{5,6},{6,5},{7,4},{8,11},{9,10},{10,... | collective-permute-start | bytes 129032 | tf_op jit(solution)/shard_map/ppermute | solution.py:302
  38.0 1.9 %collective-permute-start.5 = (bf16[168,128]{1,0:T(8,128)(2,1)S(1)}, bf16[168,128]{1,0:T(8,128)(2,1)S(1)}, u32[]{:S(2)}, u32[]{:S(2)}) collective-permute-start(bf16[168,128]{1,0:T(8,128)(2,1)S(1)} %get-tuple-element.30), channel_id=1, source_target_pairs={{0,1},{1,0},{2,3},{3,2},{4,5},{5,4},{6,7},{7,6},{8,9},{9,8},{10,11... | collective-permute-start | bytes 129032 | tf_op jit(solution)/shard_map/ppermute | solution.py:303
  40.0 0.6 shard_map.88
  40.6 0.5 collective-permute-done.5.znear
  41.2 4.2 %shard_map.89 = (f32[16,4,1728]{2,1,0:T(4,128)S(1)}, bf16[16,4,1728]{2,1,0:T(4,128)(2,1)S(1)}, bf16[144,1408]{1,0:T(8,128)(2,1)S(1)}) custom-call(bf16[4,8,1024]{2,1,0:T(8,128)(2,1)S(1)} %get-tuple-element.22.grad, bf16[4,8,1024]{2,1,0:T(8,128)(2,1)S(1)} %get-tuple-element.23.pre, bf16[4,8,1024]{2,1,0:T(8,128)(2,1)S(1)} %get-tuple-element.24.inp, ...), custom_call_target="tpu_custom_call" | custom-call | flops 1800000000 | bytes 8000000 | tf_op jit(solution)/shard_map/pallas_call | solution.py:24
  45.4 2.1 %collective-permute-start.6 = (bf16[16,4,1728]{2,1,0:T(4,128)(2,1)S(1)}, bf16[16,4,1728]{2,1,0:T(4,128)(2,1)S(1)}, u32[]{:S(2)}, u32[]{:S(2)}) collective-permute-start(bf16[16,4,1728]{2,1,0:T(4,128)(2,1)S(1)} %get-tuple-element.33), channel_id=1, source_target_pairs={{0,1},{1,0},{2,3},{3,2},{4,5},{5,4},{6,7},{7,6},{8,9},{9,8},{10,11... | collective-permute-start | bytes 663560 | tf_op jit(solution)/shard_map/ppermute | solution.py:335
  47.5 1.4 %shard_map.90 = bf16[4,8,1024]{2,1,0:T(8,128)(2,1)} custom-call(bf16[144,1408]{1,0:T(8,128)(2,1)S(1)} %get-tuple-element.34.pre_grad, bf16[4,8,1024]{2,1,0:T(8,128)(2,1)S(1)} %get-tuple-element.22.grad, bf16[3456,256]{1,0:T(8,128)(2,1)S(1)} %get-tuple-element.35.band), custom_call_target="tpu_custom_call" | custom-call | flops 500000000 | bytes 4000000 | tf_op jit(solution)/shard_map/pallas_call | solution.py:24
  48.8 0.0 collective-permute-done.6.came
  48.8 0.1 shard_map.91
  48.9 16.8 %all_to_all.15.parts = bf16[16,4,1728]{2,1,0:T(4,128)(2,1)S(1)} all-to-all(bf16[16,4,1728]{2,1,0:T(4,128)(2,1)S(1)} %shard_map.91), channel_id=1, replica_groups=mesh['gx'=16,'gy'=8,'gz'=4] {'gx'}, dimensions={0} | all-to-all | bytes 442368 | tf_op jit(solution)/shard_map/all_to_all | solution.py:338
  65.8 11.6 %all_to_all.16.parts = bf16[8,4,1728]{2,1,0:T(4,128)(2,1)S(1)} all-to-all(bf16[8,4,1728]{2,1,0:T(4,128)(2,1)S(1)} %shard_map.92), channel_id=1, replica_groups=mesh['gx'=16,'gy'=8,'gz'=4] {'gy'}, dimensions={0} | all-to-all | bytes 221184 | tf_op jit(solution)/shard_map/all_to_all | solution.py:340
  77.4 10.0 %all-gather.1.parts = f32[4,4,1728]{2,1,0:T(4,128)S(1)} all-gather(f32[1,4,1728]{2,1,0:T(4,128)S(1)} %bitcast.1), channel_id=2, replica_groups=mesh['gx'=16,'gy'=8,'gz'=4] {'gz'}, dimensions={0}, use_global_device_ids=true | all-gather | bytes 138240 | tf_op jit(solution)/shard_map/all_gather | solution.py:342
  87.4 0.6 shard_map.94
  (5 shorter events, 0.1 us)
Async XLA Ops:
  2.4 17.9 %collective-permute-start = (bf16[4,8,1024]{2,1,0:T(8,128)(2,1)S(1)}, bf16[4,8,1024]{2,1,0:T(8,128)(2,1)S(1)}, u32[]{:S(2)}, u32[]{:S(2)}) collective-permute-start(bf16[4,8,1024]{2,1,0:T(8,128)(2,1)S(1)} %get-tuple-element.25), channel_id=1, source_target_pairs={{0,480},{32,64},{64,32},{96,128},{128,96},{160,192},{192,160},{224... | collective-permute-start | bytes 196616 | tf_op jit(solution)/shard_map/ppermute | solution.py:302
  14.9 5.5 %collective-permute-start.1 = (bf16[4,8,1024]{2,1,0:T(8,128)(2,1)S(1)}, bf16[4,8,1024]{2,1,0:T(8,128)(2,1)S(1)}, u32[]{:S(2)}, u32[]{:S(2)}) collective-permute-start(bf16[4,8,1024]{2,1,0:T(8,128)(2,1)S(1)} %get-tuple-element.26), channel_id=1, source_target_pairs={{0,32},{32,0},{64,96},{96,64},{128,160},{160,128},{192,224},{224,1... | collective-permute-start | bytes 196616 | tf_op jit(solution)/shard_map/ppermute | solution.py:303
  16.8 23.2 %all-to-all-start = ((bf16[16,8,1728]{2,1,0:T(8,128)(2,1)}), bf16[16,8,1728]{2,1,0:T(8,128)(2,1)S(1)}, u32[]{:S(2)}, u32[]{:S(2)}) async-start(bf16[16,8,1728]{2,1,0:T(8,128)(2,1)} %get-tuple-element.31), calls=%async_computation | async-start | bytes 917504 | tf_op jit(solution)/shard_map/all_to_all | solution.py:375
  20.6 7.0 %collective-permute-start.2 = (bf16[14,2,1024]{2,1,0:T(2,128)(2,1)S(1)}, bf16[14,2,1024]{2,1,0:T(2,128)(2,1)S(1)}, u32[]{:S(2)}, u32[]{:S(2)}) collective-permute-start(bf16[14,2,1024]{2,1,0:T(2,128)(2,1)S(1)} %get-tuple-element.27), channel_id=1, source_target_pairs={{0,28},{4,8},{8,4},{12,16},{16,12},{20,24},{24,20},{28,0},{1,29},{... | collective-permute-start | bytes 172040 | tf_op jit(solution)/shard_map/ppermute | solution.py:302
  25.7 5.2 %collective-permute-start.3 = (bf16[14,2,1024]{2,1,0:T(2,128)(2,1)S(1)}, bf16[14,2,1024]{2,1,0:T(2,128)(2,1)S(1)}, u32[]{:S(2)}, u32[]{:S(2)}) collective-permute-start(bf16[14,2,1024]{2,1,0:T(2,128)(2,1)S(1)} %get-tuple-element.28), channel_id=1, source_target_pairs={{0,4},{4,0},{8,12},{12,8},{16,20},{20,16},{24,28},{28,24},{1,5},{5... | collective-permute-start | bytes 172040 | tf_op jit(solution)/shard_map/ppermute | solution.py:303
  31.1 9.5 %collective-permute-start.4 = (bf16[168,128]{1,0:T(8,128)(2,1)S(1)}, bf16[168,128]{1,0:T(8,128)(2,1)S(1)}, u32[]{:S(2)}, u32[]{:S(2)}) collective-permute-start(bf16[168,128]{1,0:T(8,128)(2,1)S(1)} %get-tuple-element.29), channel_id=1, source_target_pairs={{0,3},{1,2},{2,1},{3,0},{4,7},{5,6},{6,5},{7,4},{8,11},{9,10},{10,... | collective-permute-start | bytes 129032 | tf_op jit(solution)/shard_map/ppermute | solution.py:302
  38.0 3.1 %collective-permute-start.5 = (bf16[168,128]{1,0:T(8,128)(2,1)S(1)}, bf16[168,128]{1,0:T(8,128)(2,1)S(1)}, u32[]{:S(2)}, u32[]{:S(2)}) collective-permute-start(bf16[168,128]{1,0:T(8,128)(2,1)S(1)} %get-tuple-element.30), channel_id=1, source_target_pairs={{0,1},{1,0},{2,3},{3,2},{4,5},{5,4},{6,7},{7,6},{8,9},{9,8},{10,11... | collective-permute-start | bytes 129032 | tf_op jit(solution)/shard_map/ppermute | solution.py:303
  45.4 3.5 %collective-permute-start.6 = (bf16[16,4,1728]{2,1,0:T(4,128)(2,1)S(1)}, bf16[16,4,1728]{2,1,0:T(4,128)(2,1)S(1)}, u32[]{:S(2)}, u32[]{:S(2)}) collective-permute-start(bf16[16,4,1728]{2,1,0:T(4,128)(2,1)S(1)} %get-tuple-element.33), channel_id=1, source_target_pairs={{0,1},{1,0},{2,3},{3,2},{4,5},{5,4},{6,7},{7,6},{8,9},{9,8},{10,11... | collective-permute-start | bytes 663560 | tf_op jit(solution)/shard_map/ppermute | solution.py:335

commit v8 on v7

--- a/solution.py
+++ b/solution.py
@@ -316,7 +316,15 @@
             out[i] = value
 
 
-def pair_kernel(kept, came, out):
+def pair_kernel(kept, came, stay, leave):
+    odd = lax.rem(lax.axis_index("gx"), 2) == 1
+    for i in range(stay.shape[0]):
+        first, second = (kept[2 * i + j] + came[2 * i + j].astype(F32) for j in range(2))
+        stay[i] = jnp.where(odd, second, first)
+        leave[i] = jnp.where(odd, first, second).astype(B16)
+
+
+def add_kernel(kept, came, out):
     out[...] = (kept[...] + came[...].astype(F32)).astype(B16)
 
 
@@ -334,8 +342,13 @@
     gy, gz = lax.axis_size("gy"), lax.axis_size("gz")
     came = lax.ppermute(sent, "gz", [(i, i + 1 - 2 * (i % 2)) for i in range(gz)])
     came, other = lax.optimization_barrier((came, other))
-    (slots,) = call(pair_kernel, [(kept.shape, B16)], [], 1000, 500000, kept, came)
-    parts = lax.all_to_all(slots, "gx", 0, 0, tiled=True)
+    count = kept.shape[0]
+    half = (count // 2, rows, columns)
+    stay, leave = call(pair_kernel, [(half, F32), (half, B16)], [], 1000, 500000, kept, came)
+    came = lax.ppermute(leave, "gx", [(i, i + 1 - 2 * (i % 2)) for i in range(count)])
+    (slots,) = call(add_kernel, [(half, B16)], [], 1000, 500000, stay, came)
+    groups = [list(range(0, count, 2)), list(range(1, count, 2))]
+    parts = lax.all_to_all(slots, "gx", 0, 0, axis_index_groups=groups, tiled=True)
     (copies,) = call(total_kernel, [((gy, rows, columns), B16)], [], 1000, 500000, parts)
     parts = lax.all_to_all(copies, "gy", 0, 0, tiled=True)
     (part,) = call(total_kernel, [((rows, columns), F32)], [], 1000, 500000, parts)

time: 88.6 us -> 92.6 us (1.045)
  waiting for transfers between devices: 3.82 us -> 7.67 us
  starting transfers between devices: 35.9 us -> 38.3 us
  blocking collectives: 38.4 us -> 36.1 us
    ppermute x0 -> x1, waiting for transfers between devices: none -> 3.85 us  [reduced(): lax.ppermute(leave, 'gx', [(i, i + 1 - 2 * (i % 2)) for i in range(count)])]
    all_to_all x1, blocking collectives: 16.8 us -> 13.9 us  [reduced(): lax.all_to_all(slots, 'gx', 0, 0, axis_index_groups=groups, tiled=True)]
    ppermute x0 -> x1, starting transfers between devices: none -> 2.42 us  [reduced(): lax.ppermute(leave, 'gx', [(i, i + 1 - 2 * (i % 2)) for i in range(count)])]
    pallas_call x10 -> x11, Pallas kernels: 9.16 us -> 9.2 us  [call(): pl.pallas_call(kernel, out_shape=[jax.ShapeDtypeStruct(shape, dtype) for...]
  transfers between devices with their start and end apart: 8 -> 9, of which waited for: 2 -> 3; matrix products, arithmetic and copies ran while one was open for 0% -> 0% of each run, Pallas kernels for 3% -> 3%
where the time goes in v8:
time: 92.6 us; the launch traced here: 92 us
  starting transfers between devices  38.3 us (41%)
  blocking collectives  36.1 us (39%)
  Pallas kernels  9.2 us (10%)
  waiting for transfers between devices  7.67 us (8%)
    ppermute x3, starting transfers between devices, swapped(): lax.ppermute(far, axis, [(i, (i + step) % count) for i, step in enumerate...  24.5 us
    all_to_all x1, blocking collectives, reduced(): lax.all_to_all(slots, 'gx', 0, 0, axis_index_groups=groups, tiled=True)  13.9 us
    all_to_all x1, blocking collectives, reduced(): parts = lax.all_to_all(copies, 'gy', 0, 0, tiled=True)  11.5 us
    all_gather x1, blocking collectives, reduced(): parts = lax.all_gather(part, 'gz', axis=0)  10.7 us
    pallas_call x11, Pallas kernels, call(): pl.pallas_call(kernel, out_shape=[jax.ShapeDtypeStruct(shape, dtype) for...  9.2 us
    ppermute x3, starting transfers between devices, swapped(): lax.ppermute(near, axis, [(i, i - step) for i, step in enumerate(steps)])  5.76 us
    ppermute x1, waiting for transfers between devices, reduced(): lax.ppermute(leave, 'gx', [(i, i + 1 - 2 * (i % 2)) for i in range(count)])  3.85 us
    ppermute x3, waiting for transfers between devices, swapped(): lax.ppermute(near, axis, [(i, i - step) for i, step in enumerate(steps)])  3.8 us
  transfers between devices with their start and end apart: 9, of which 3 were waited for; matrix products, arithmetic and copies ran while one was open for 0% of the time, Pallas kernels for 3%

profile of v8, /device:TPU:1, one launch (start us, length us, event | category | flops | bytes accessed | tf_op | source)
XLA Modules:
  0.0 92.0 jit_solution(14307467692802807080)
XLA Ops:
  0.6 1.8 %shard_map.85 = (bf16[4,8,1024]{2,1,0:T(8,128)(2,1)S(1)}, bf16[4,8,1024]{2,1,0:T(8,128)(2,1)S(1)}, bf16[4,8,1024]{2,1,0:T(8,128)(2,1)S(1)}, bf16[4,8,1024]{2,1,0...) custom-call(bf16[4,8,1024]{2,1,0:T(8,128)(2,1)} %skip_in.1, ...), custom_call_target="tpu_custom_call" | custom-call | flops 100000 | bytes 400000 | tf_op jit(solution)/shard_map/pallas_call | solution.py:24
  2.4 12.4 %collective-permute-start = (bf16[4,8,1024]{2,1,0:T(8,128)(2,1)S(1)}, bf16[4,8,1024]{2,1,0:T(8,128)(2,1)S(1)}, u32[]{:S(2)}, u32[]{:S(2)}) collective-permute-start(bf16[4,8,1024]{2,1,0:T(8,128)(2,1)S(1)} %get-tuple-element.27), channel_id=1, source_target_pairs={{0,480},{32,64},{64,32},{96,128},{128,96},{160,192},{192,160},{224... | collective-permute-start | bytes 196616 | tf_op jit(solution)/shard_map/ppermute | solution.py:302
  14.9 1.9 %collective-permute-start.1 = (bf16[4,8,1024]{2,1,0:T(8,128)(2,1)S(1)}, bf16[4,8,1024]{2,1,0:T(8,128)(2,1)S(1)}, u32[]{:S(2)}, u32[]{:S(2)}) collective-permute-start(bf16[4,8,1024]{2,1,0:T(8,128)(2,1)S(1)} %get-tuple-element.28), channel_id=1, source_target_pairs={{0,32},{32,0},{64,96},{96,64},{128,160},{160,128},{192,224},{224,1... | collective-permute-start | bytes 196616 | tf_op jit(solution)/shard_map/ppermute | solution.py:303
  16.8 3.6 %all-to-all-start = ((bf16[16,8,1728]{2,1,0:T(8,128)(2,1)}), bf16[16,8,1728]{2,1,0:T(8,128)(2,1)S(1)}, u32[]{:S(2)}, u32[]{:S(2)}) async-start(bf16[16,8,1728]{2,1,0:T(8,128)(2,1)} %get-tuple-element.33), calls=%async_computation | async-start | bytes 917504 | tf_op jit(solution)/shard_map/all_to_all | solution.py:388
  20.4 0.0 collective-permute-done.xfar
  20.4 0.2 shard_map.86
  20.6 5.1 %collective-permute-start.2 = (bf16[14,2,1024]{2,1,0:T(2,128)(2,1)S(1)}, bf16[14,2,1024]{2,1,0:T(2,128)(2,1)S(1)}, u32[]{:S(2)}, u32[]{:S(2)}) collective-permute-start(bf16[14,2,1024]{2,1,0:T(2,128)(2,1)S(1)} %get-tuple-element.29), channel_id=1, source_target_pairs={{0,28},{4,8},{8,4},{12,16},{16,12},{20,24},{24,20},{28,0},{1,29},{... | collective-permute-start | bytes 172040 | tf_op jit(solution)/shard_map/ppermute | solution.py:302
  25.7 1.9 %collective-permute-start.3 = (bf16[14,2,1024]{2,1,0:T(2,128)(2,1)S(1)}, bf16[14,2,1024]{2,1,0:T(2,128)(2,1)S(1)}, u32[]{:S(2)}, u32[]{:S(2)}) collective-permute-start(bf16[14,2,1024]{2,1,0:T(2,128)(2,1)S(1)} %get-tuple-element.30), channel_id=1, source_target_pairs={{0,4},{4,0},{8,12},{12,8},{16,20},{20,16},{24,28},{28,24},{1,5},{5... | collective-permute-start | bytes 172040 | tf_op jit(solution)/shard_map/ppermute | solution.py:303
  27.7 3.3 %collective-permute-done.3.ynear = bf16[14,2,1024]{2,1,0:T(2,128)(2,1)S(1)} collective-permute-done((bf16[14,2,1024]{2,1,0:T(2,128)(2,1)S(1)}, bf16[14,2,1024]{2,1,0:T(2,128)(2,1)S(1)}, u32[]{:S(2)}, u32[]{:S(2)}) %collective-permute-start.3) | collective-permute-done | bytes 57376 | tf_op jit(solution)/shard_map/ppermute | solution.py:303
  30.9 0.1 shard_map.87
  31.1 7.0 %collective-permute-start.4 = (bf16[168,128]{1,0:T(8,128)(2,1)S(1)}, bf16[168,128]{1,0:T(8,128)(2,1)S(1)}, u32[]{:S(2)}, u32[]{:S(2)}) collective-permute-start(bf16[168,128]{1,0:T(8,128)(2,1)S(1)} %get-tuple-element.31), channel_id=1, source_target_pairs={{0,3},{1,2},{2,1},{3,0},{4,7},{5,6},{6,5},{7,4},{8,11},{9,10},{10,... | collective-permute-start | bytes 129032 | tf_op jit(solution)/shard_map/ppermute | solution.py:302
  38.0 1.9 %collective-permute-start.5 = (bf16[168,128]{1,0:T(8,128)(2,1)S(1)}, bf16[168,128]{1,0:T(8,128)(2,1)S(1)}, u32[]{:S(2)}, u32[]{:S(2)}) collective-permute-start(bf16[168,128]{1,0:T(8,128)(2,1)S(1)} %get-tuple-element.32), channel_id=1, source_target_pairs={{0,1},{1,0},{2,3},{3,2},{4,5},{5,4},{6,7},{7,6},{8,9},{9,8},{10,11... | collective-permute-start | bytes 129032 | tf_op jit(solution)/shard_map/ppermute | solution.py:303
  40.0 0.6 shard_map.88
  40.6 0.5 collective-permute-done.5.znear
  41.2 4.2 %shard_map.89 = (f32[16,4,1728]{2,1,0:T(4,128)S(1)}, bf16[16,4,1728]{2,1,0:T(4,128)(2,1)S(1)}, bf16[144,1408]{1,0:T(8,128)(2,1)S(1)}) custom-call(bf16[4,8,1024]{2,1,0:T(8,128)(2,1)S(1)} %get-tuple-element.24.grad, bf16[4,8,1024]{2,1,0:T(8,128)(2,1)S(1)} %get-tuple-element.25.pre, bf16[4,8,1024]{2,1,0:T(8,128)(2,1)S(1)} %get-tuple-element.26.inp, ...), custom_call_target="tpu_custom_call" | custom-call | flops 1800000000 | bytes 8000000 | tf_op jit(solution)/shard_map/pallas_call | solution.py:24
  45.4 2.1 %collective-permute-start.6 = (bf16[16,4,1728]{2,1,0:T(4,128)(2,1)S(1)}, bf16[16,4,1728]{2,1,0:T(4,128)(2,1)S(1)}, u32[]{:S(2)}, u32[]{:S(2)}) collective-permute-start(bf16[16,4,1728]{2,1,0:T(4,128)(2,1)S(1)} %get-tuple-element.35), channel_id=1, source_target_pairs={{0,1},{1,0},{2,3},{3,2},{4,5},{5,4},{6,7},{7,6},{8,9},{9,8},{10,11... | collective-permute-start | bytes 663560 | tf_op jit(solution)/shard_map/ppermute | solution.py:343
  47.5 1.4 %shard_map.90 = bf16[4,8,1024]{2,1,0:T(8,128)(2,1)} custom-call(bf16[144,1408]{1,0:T(8,128)(2,1)S(1)} %get-tuple-element.36.pre_grad, bf16[4,8,1024]{2,1,0:T(8,128)(2,1)S(1)} %get-tuple-element.24.grad, bf16[3456,256]{1,0:T(8,128)(2,1)S(1)} %get-tuple-element.37.band), custom_call_target="tpu_custom_call" | custom-call | flops 500000000 | bytes 4000000 | tf_op jit(solution)/shard_map/pallas_call | solution.py:24
  48.8 0.1 shard_map.91
  48.9 2.4 %collective-permute-start.7 = (bf16[8,4,1728]{2,1,0:T(4,128)(2,1)S(1)}, bf16[8,4,1728]{2,1,0:T(4,128)(2,1)S(1)}, u32[]{:S(2)}, u32[]{:S(2)}) collective-permute-start(bf16[8,4,1728]{2,1,0:T(4,128)(2,1)S(1)} %get-tuple-element.42), channel_id=1, source_target_pairs={{0,32},{32,0},{64,96},{96,64},{128,160},{160,128},{192,224},{224,1... | collective-permute-start | bytes 331784 | tf_op jit(solution)/shard_map/ppermute | solution.py:348
  51.4 3.8 %collective-permute-done.7.came = bf16[8,4,1728]{2,1,0:T(4,128)(2,1)S(1)} collective-permute-done((bf16[8,4,1728]{2,1,0:T(4,128)(2,1)S(1)}, bf16[8,4,1728]{2,1,0:T(4,128)(2,1)S(1)}, u32[]{:S(2)}, u32[]{:S(2)}) %collective-permute-start.7) | collective-permute-done | bytes 110624 | tf_op jit(solution)/shard_map/ppermute | solution.py:348
  55.3 13.9 %all_to_all.15.parts = bf16[8,4,1728]{2,1,0:T(4,128)(2,1)S(1)} all-to-all(bf16[8,4,1728]{2,1,0:T(4,128)(2,1)S(1)} %shard_map.92), channel_id=1, replica_groups={{0,64,128,192,256,320,384,448},{32,96,160,224,288,352,416,480},{1,65,12..., dimensions={0} | all-to-all | bytes 221184 | tf_op jit(solution)/shard_map/all_to_all | solution.py:351
  69.2 11.5 %all_to_all.16.parts = bf16[8,4,1728]{2,1,0:T(4,128)(2,1)S(1)} all-to-all(bf16[8,4,1728]{2,1,0:T(4,128)(2,1)S(1)} %shard_map.93), channel_id=1, replica_groups=mesh['gx'=16,'gy'=8,'gz'=4] {'gy'}, dimensions={0} | all-to-all | bytes 221184 | tf_op jit(solution)/shard_map/all_to_all | solution.py:353
  80.7 10.7 %all-gather.1.parts = f32[4,4,1728]{2,1,0:T(4,128)S(1)} all-gather(f32[1,4,1728]{2,1,0:T(4,128)S(1)} %bitcast.1), channel_id=2, replica_groups=mesh['gx'=16,'gy'=8,'gz'=4] {'gz'}, dimensions={0}, use_global_device_ids=true | all-gather | bytes 138240 | tf_op jit(solution)/shard_map/all_gather | solution.py:355
  91.4 0.6 shard_map.95
  (8 shorter events, 0.1 us)
Async XLA Ops:
  2.4 17.9 %collective-permute-start = (bf16[4,8,1024]{2,1,0:T(8,128)(2,1)S(1)}, bf16[4,8,1024]{2,1,0:T(8,128)(2,1)S(1)}, u32[]{:S(2)}, u32[]{:S(2)}) collective-permute-start(bf16[4,8,1024]{2,1,0:T(8,128)(2,1)S(1)} %get-tuple-element.27), channel_id=1, source_target_pairs={{0,480},{32,64},{64,32},{96,128},{128,96},{160,192},{192,160},{224... | collective-permute-start | bytes 196616 | tf_op jit(solution)/shard_map/ppermute | solution.py:302
  14.9 5.5 %collective-permute-start.1 = (bf16[4,8,1024]{2,1,0:T(8,128)(2,1)S(1)}, bf16[4,8,1024]{2,1,0:T(8,128)(2,1)S(1)}, u32[]{:S(2)}, u32[]{:S(2)}) collective-permute-start(bf16[4,8,1024]{2,1,0:T(8,128)(2,1)S(1)} %get-tuple-element.28), channel_id=1, source_target_pairs={{0,32},{32,0},{64,96},{96,64},{128,160},{160,128},{192,224},{224,1... | collective-permute-start | bytes 196616 | tf_op jit(solution)/shard_map/ppermute | solution.py:303
  16.8 23.2 %all-to-all-start = ((bf16[16,8,1728]{2,1,0:T(8,128)(2,1)}), bf16[16,8,1728]{2,1,0:T(8,128)(2,1)S(1)}, u32[]{:S(2)}, u32[]{:S(2)}) async-start(bf16[16,8,1728]{2,1,0:T(8,128)(2,1)} %get-tuple-element.33), calls=%async_computation | async-start | bytes 917504 | tf_op jit(solution)/shard_map/all_to_all | solution.py:388
  20.6 7.0 %collective-permute-start.2 = (bf16[14,2,1024]{2,1,0:T(2,128)(2,1)S(1)}, bf16[14,2,1024]{2,1,0:T(2,128)(2,1)S(1)}, u32[]{:S(2)}, u32[]{:S(2)}) collective-permute-start(bf16[14,2,1024]{2,1,0:T(2,128)(2,1)S(1)} %get-tuple-element.29), channel_id=1, source_target_pairs={{0,28},{4,8},{8,4},{12,16},{16,12},{20,24},{24,20},{28,0},{1,29},{... | collective-permute-start | bytes 172040 | tf_op jit(solution)/shard_map/ppermute | solution.py:302
  25.7 5.2 %collective-permute-start.3 = (bf16[14,2,1024]{2,1,0:T(2,128)(2,1)S(1)}, bf16[14,2,1024]{2,1,0:T(2,128)(2,1)S(1)}, u32[]{:S(2)}, u32[]{:S(2)}) collective-permute-start(bf16[14,2,1024]{2,1,0:T(2,128)(2,1)S(1)} %get-tuple-element.30), channel_id=1, source_target_pairs={{0,4},{4,0},{8,12},{12,8},{16,20},{20,16},{24,28},{28,24},{1,5},{5... | collective-permute-start | bytes 172040 | tf_op jit(solution)/shard_map/ppermute | solution.py:303
  31.1 9.5 %collective-permute-start.4 = (bf16[168,128]{1,0:T(8,128)(2,1)S(1)}, bf16[168,128]{1,0:T(8,128)(2,1)S(1)}, u32[]{:S(2)}, u32[]{:S(2)}) collective-permute-start(bf16[168,128]{1,0:T(8,128)(2,1)S(1)} %get-tuple-element.31), channel_id=1, source_target_pairs={{0,3},{1,2},{2,1},{3,0},{4,7},{5,6},{6,5},{7,4},{8,11},{9,10},{10,... | collective-permute-start | bytes 129032 | tf_op jit(solution)/shard_map/ppermute | solution.py:302
  38.0 3.1 %collective-permute-start.5 = (bf16[168,128]{1,0:T(8,128)(2,1)S(1)}, bf16[168,128]{1,0:T(8,128)(2,1)S(1)}, u32[]{:S(2)}, u32[]{:S(2)}) collective-permute-start(bf16[168,128]{1,0:T(8,128)(2,1)S(1)} %get-tuple-element.32), channel_id=1, source_target_pairs={{0,1},{1,0},{2,3},{3,2},{4,5},{5,4},{6,7},{7,6},{8,9},{9,8},{10,11... | collective-permute-start | bytes 129032 | tf_op jit(solution)/shard_map/ppermute | solution.py:303
  45.4 3.5 %collective-permute-start.6 = (bf16[16,4,1728]{2,1,0:T(4,128)(2,1)S(1)}, bf16[16,4,1728]{2,1,0:T(4,128)(2,1)S(1)}, u32[]{:S(2)}, u32[]{:S(2)}) collective-permute-start(bf16[16,4,1728]{2,1,0:T(4,128)(2,1)S(1)} %get-tuple-element.35), channel_id=1, source_target_pairs={{0,1},{1,0},{2,3},{3,2},{4,5},{5,4},{6,7},{7,6},{8,9},{9,8},{10,11... | collective-permute-start | bytes 663560 | tf_op jit(solution)/shard_map/ppermute | solution.py:343
  48.9 6.3 %collective-permute-start.7 = (bf16[8,4,1728]{2,1,0:T(4,128)(2,1)S(1)}, bf16[8,4,1728]{2,1,0:T(4,128)(2,1)S(1)}, u32[]{:S(2)}, u32[]{:S(2)}) collective-permute-start(bf16[8,4,1728]{2,1,0:T(4,128)(2,1)S(1)} %get-tuple-element.42), channel_id=1, source_target_pairs={{0,32},{32,0},{64,96},{96,64},{128,160},{160,128},{192,224},{224,1... | collective-permute-start | bytes 331784 | tf_op jit(solution)/shard_map/ppermute | solution.py:348

commit v9 on v7

--- a/solution.py
+++ b/solution.py
@@ -13,10 +13,13 @@
 LANES = SZ * CH
 ROWS = 16 * (SX + 5)
 WIDE = LANES + 6 * CH
-BAND = 6 * CH
+BAND = 4 * CH
+OWN_GROUPS, HALO_GROUPS = SZ // 2, SZ // 2 + 2
 DEPTH = 9 * BAND
-OWN = 16 * 3
-HALO_ROWS = 16 * (SX + 3)
+OWN_ROWS = 8 * SX
+HALO_ROWS = 8 * (SX + 2)
+EDGES = HALO_GROUPS * HALO_ROWS
+MANY = EDGES + HALO_GROUPS * 16
 LAYERS = 14
 
 
@@ -145,7 +148,7 @@
 
 def bands_kernel(weights, one, two, flat, turned):
     count, rows = weights.shape[0], weights.shape[1] // 2
-    block = lax.broadcasted_iota(jnp.int32, (CH, 256), 1) // CH
+    block = lax.broadcasted_iota(jnp.int32, (CH, 128), 1) // CH
     for which, out in enumerate((one, two)):
         flat[...] = jnp.zeros_like(flat)
         for g in range(count):
@@ -153,12 +156,12 @@
             flat[g * rows : (g + 1) * rows, 256 : 256 + 27 * CH] = value
         turned[...] = pltpu.roll(flat[...], flat.shape[1] - 64, 1)
         for m in range(9):
-            for a in range(6):
+            for a in range(4):
                 at = 4 + 3 * m + 2 - a
                 source = turned if at % 2 else flat
                 lane = at // 2 * 128
                 valid = (block + 2 - a >= 0) & (block - a <= 0)
-                value = jnp.where(valid, source[:, lane : lane + 256], 0.0)
+                value = jnp.where(valid, source[:, lane : lane + 128], 0.0)
                 out[m * BAND + a * CH : m * BAND + (a + 1) * CH, :] = value.astype(B16)
 
 
@@ -190,25 +193,43 @@
             field[row + 8 : row + 9, lane : lane + 128] = value[10:11]
 
 
-def spread(value, steps, sign):
-    moved = pltpu.roll(value, 64, 1)
+def spread(moved, evens, odds, sign, layers):
     for i, dy in enumerate((-1, 0, 1)):
         by = (-sign * dy) % ROWS
-        steps[i] = (pltpu.roll(moved, by, 0) if by else moved).astype(B16)
-
-
-def own_columns(steps, columns, sign):
+        value = pltpu.roll(moved, by, 0) if by else moved
+        tiles = [value[16 * (x + 1) : 16 * (x + 1) + 8] for x in layers]
+        evens[i, 0 : 8 * len(tiles)] = jnp.concatenate(tiles, 0).astype(B16)
+        odds[i, 0 : 8 * len(tiles) - 16] = jnp.concatenate(tiles[1:-1], 0).astype(B16)
+
+
+def stepped(evens, odds, dy, dx, rows, lane):
+    ref, row = (odds, 0) if dx == 0 else (evens, 8 + 8 * dx)
+    return ref[dy, row : row + rows, lane : lane + BAND]
+
+
+def own_columns(evens, odds, columns, sign):
     for m in range(9):
-        dx, dy = m // 3 - 1, m % 3
-        row = OWN + sign * 16 * dx
-        for h in range(4):
-            columns[64 * h : 64 * (h + 1), BAND * m : BAND * (m + 1)] = steps[
-                dy, row : row + 64, 256 * h + 128 : 256 * h + 128 + BAND
-            ]
+        for h in range(OWN_GROUPS):
+            columns[OWN_ROWS * h : OWN_ROWS * (h + 1), BAND * m : BAND * (m + 1)] = stepped(
+                evens, odds, m % 3, sign * (m // 3 - 1), OWN_ROWS, 128 * h + 128
+            )
+
+
+def edge_rows(count):
+    row = lax.broadcasted_iota(jnp.int32, (16 * count, ROWS), 0)
+    column = lax.broadcasted_iota(jnp.int32, (16 * count, ROWS), 1)
+    m, x = row // 16 + (4 if count == 1 else 0), row % 8
+    source = 16 * (x - m // 3 + 2) + jnp.where(row % 16 < 8, -1, 8) - m % 3 + 1
+    return jnp.where(column == source, 1.0, 0.0).astype(B16)
+
+
+def slope(v):
+    g = jax.nn.sigmoid(v)
+    return g * (1.0 + v * (1.0 - g))
 
 
 def main_kernel(scale, grad, pre, inp, xfar, xnear, yfar, ynear, zfar, znear, band,
-                kept, sent, pre_out, fg, fa, fi, steps, columns, many, left, left_f, grads_one, grads_two, held, zlo, zhi):
+                kept, sent, pre_out, fg, fa, fi, moved, picked, evens, odds, columns, many, left, left_f, grads_one, grads_two, held, zlo, zhi):
     wide, acts, inputs = fields_of(grad, pre, inp, *below_above("gx", xfar, xnear))
     ylo, yhi = below_above("gy", yfar, ynear)
     below, above = below_above("gz", zfar, znear)
@@ -221,39 +242,52 @@
     contract = (((0,), (0,)), ((), ()))
 
     v = fa[...]
-    spread((v * jax.nn.sigmoid(v)).astype(B16).astype(F32), steps, 1)
-    own_columns(steps, columns, 1)
-    left_f[...] = jnp.zeros_like(left_f)
-    for h in range(4):
+    act = (v * jax.nn.sigmoid(v)).astype(B16).astype(F32)
+    spread(pltpu.roll(act, 64, 1), evens, odds, 1, range(1, SX + 3))
+    own_columns(evens, odds, columns, 1)
+    for h in range(OWN_GROUPS):
         for x in range(SX):
-            row = 64 * h + 16 * x
-            left_f[row : row + 8, :] = grad[x, :, 256 * h : 256 * (h + 1)].astype(F32)
+            row = OWN_ROWS * h + 8 * x
+            left_f[row : row + 8, :] = grad[x, :, 128 * h : 128 * (h + 1)].astype(F32)
     left[...] = left_f[...].astype(B16)
     grads_two[...] = lax.dot_general(left[...], columns[...], contract, preferred_element_type=F32)
 
-    spread(fg[...], steps, -1)
+    moved[...] = pltpu.roll(fg[...], 64, 1)
+    spread(moved[...], evens, odds, -1, range(SX + 4))
     for m in range(9):
         dx, dy = m // 3 - 1, m % 3
-        row = 16 - 16 * dx
-        for h in range(5):
-            many[HALO_ROWS * h : HALO_ROWS * (h + 1), BAND * m : BAND * (m + 1)] = steps[
-                dy, row : row + HALO_ROWS, 256 * h : 256 * h + BAND
+        for h in range(HALO_GROUPS):
+            many[HALO_ROWS * h : HALO_ROWS * (h + 1), BAND * m : BAND * (m + 1)] = stepped(
+                evens, odds, dy, -dx, HALO_ROWS, 128 * h
+            )
+    picked[...] = jnp.dot(edge_rows(9), moved[...].astype(B16), preferred_element_type=F32).astype(B16)
+    for m in range(9):
+        for h in range(HALO_GROUPS):
+            row = EDGES + 16 * h
+            many[row : row + 16, BAND * m : BAND * (m + 1)] = picked[
+                16 * m : 16 * (m + 1), 128 * h : 128 * h + BAND
             ]
     held[...] = jnp.dot(many[...], band[...], preferred_element_type=F32)
-    fg[...] = jnp.zeros_like(fg)
-    for h in range(5):
-        v = fa[16 : 16 + HALO_ROWS, 256 * h : 256 * (h + 1)]
-        g = jax.nn.sigmoid(v)
-        value = held[HALO_ROWS * h : HALO_ROWS * (h + 1), :] * (g * (1.0 + v * (1.0 - g)))
-        fg[16 : 16 + HALO_ROWS, 256 * h : 256 * (h + 1)] = value.astype(B16).astype(F32)
+    fg[:, 128 * HALO_GROUPS :] = jnp.zeros((ROWS, WIDE - 128 * HALO_GROUPS), F32)
+    place = edge_rows(1)
+    beside = slope(jnp.dot(place, fa[:, : 128 * HALO_GROUPS].astype(B16), preferred_element_type=F32))
+    for h in range(HALO_GROUPS):
+        lanes = slice(128 * h, 128 * (h + 1))
+        value = (held[EDGES + 16 * h : EDGES + 16 * (h + 1), :] * beside[:, lanes]).astype(B16)
+        fg[:, lanes] = lax.dot_general(place, value, contract, preferred_element_type=F32)
+        for x in range(1, SX + 3):
+            row, at = HALO_ROWS * h + 8 * (x - 1), slice(16 * (x + 1), 16 * (x + 1) + 8)
+            value = held[row : row + 8, :] * slope(fa[at, lanes])
+            fg[at, lanes] = value.astype(B16).astype(F32)
     pre_out[...] = pltpu.roll(fg[...], 64, 1).astype(B16)
 
-    spread(fi[...], steps, 1)
-    own_columns(steps, columns, 1)
-    inside = lax.broadcasted_iota(jnp.int32, (64, 256), 0) % 16 < 8
-    for h in range(4):
-        value = fg[OWN : OWN + 64, 256 * h + 128 : 256 * h + 384]
-        left[64 * h : 64 * (h + 1), :] = jnp.where(inside, value, 0.0).astype(B16)
+    spread(pltpu.roll(fi[...], 64, 1), evens, odds, 1, range(1, SX + 3))
+    own_columns(evens, odds, columns, 1)
+    for h in range(OWN_GROUPS):
+        for x in range(SX):
+            row, at = OWN_ROWS * h + 8 * x, 16 * (x + 3)
+            left_f[row : row + 8, :] = fg[at : at + 8, 128 * h + 128 : 128 * h + 256]
+    left[...] = left_f[...].astype(B16)
     grads_one[...] = lax.dot_general(left[...], columns[...], contract, preferred_element_type=F32)
 
     count, rows = kept.shape[0], kept.shape[1]
@@ -261,12 +295,11 @@
 
     def block(source, k):
         m, t = k // 3, k % 3
-        same, other = [], []
-        for b in range(4):
-            lane = (6 * m + b + t) // 2 * 128
-            piece = source[64 * b : 64 * (b + 1), lane : lane + 128]
-            (same if (b + t) % 2 == k % 2 else other).append(piece)
-        return (same[0] + same[1]) + pltpu.roll(other[0] + other[1], 64, 1)
+        pieces = []
+        for b in ((k + t) % 2, (k + t + 1) % 2):
+            lane = (4 * m + b + t) // 2 * 128
+            pieces.append(source[64 * b : 64 * (b + 1), lane : lane + 128])
+        return pieces[0] + pltpu.roll(pieces[1], 64, 1)
 
     for j in range(14):
         pair = []
@@ -283,15 +316,13 @@
             sent[g, :, 128 * j : 128 * j + width] = send[g * rows : (g + 1) * rows, :].astype(B16)
 
 
-def last_kernel(pre_grad, grad, band, out, steps, columns, held):
-    value = pre_grad[...].astype(F32)
-    for i, dy in enumerate((-1, 0, 1)):
-        steps[i] = (pltpu.roll(value, dy % ROWS, 0) if dy else value).astype(B16)
-    own_columns(steps, columns, -1)
+def last_kernel(pre_grad, grad, band, out, evens, odds, columns, held):
+    spread(pre_grad[...].astype(F32), evens, odds, -1, range(1, SX + 3))
+    own_columns(evens, odds, columns, -1)
     held[...] = jnp.dot(columns[...], band[...], preferred_element_type=F32)
-    for h in range(4):
+    for h in range(OWN_GROUPS):
         for x in range(SX):
-            row, lanes = 64 * h + 16 * x, slice(256 * h, 256 * (h + 1))
+            row, lanes = OWN_ROWS * h + 8 * x, slice(128 * h, 128 * (h + 1))
             out[x, :, lanes] = (held[row : row + 8, :] + grad[x, :, lanes].astype(F32)).astype(B16)
 
 
@@ -377,19 +408,19 @@
     zfar, znear = swapped(
         *call(zpack_kernel, [message, message], [side, side], 100000, 700000, *fields, yfar, ynear), "gz"
     )
-    matrix = ((DEPTH, 256), B16)
+    matrix = ((DEPTH, 128), B16)
     flat = ((CH, 36 * CH), F32)
     band_one, band_two = call(bands_kernel, [matrix, matrix], [flat, flat], 1000000, 4000000, gathered)
     field = ((ROWS, WIDE), F32)
-    steps = ((3, ROWS, WIDE), B16)
-    columns = ((256, DEPTH), B16)
+    evens, odds = ((3, 8 * (SX + 4), WIDE), B16), ((3, 8 * (SX + 2), WIDE), B16)
+    columns = ((OWN_GROUPS * OWN_ROWS, DEPTH), B16)
     kept, sent, pre_grad = call(
         functools.partial(main_kernel, 1.0 / math.sqrt(cells)),
         [((count, rows, 27 * CH), F32), ((count, rows, 27 * CH), B16), ((ROWS, WIDE), B16)],
         [
-            field, field, field, steps, columns,
-            ((5 * HALO_ROWS, DEPTH), B16), ((256, 256), B16), ((256, 256), F32),
-            ((256, DEPTH), F32), ((256, DEPTH), F32), ((5 * HALO_ROWS, 256), F32), side, side,
+            field, field, field, field, ((ROWS, WIDE), B16), evens, odds, columns,
+            ((MANY, DEPTH), B16), ((OWN_GROUPS * OWN_ROWS, 128), B16), ((OWN_GROUPS * OWN_ROWS, 128), F32),
+            ((128, DEPTH), F32), ((128, DEPTH), F32), ((MANY, 128), F32), side, side,
         ],
         2 * 900 * 1000 * 1000, 8000000,
         *fields, yfar, ynear, zfar, znear, band_two,
@@ -398,7 +429,7 @@
     (input_grad,) = call(
         last_kernel,
         [((SX, SY, LANES), B16)],
-        [steps, columns, ((256, 256), F32)],
+        [evens, odds, columns, ((OWN_GROUPS * OWN_ROWS, 128), F32)],
         500000000, 4000000,
         pre_grad, grad, band_one,
     )

time: 88.6 us -> 87.6 us (0.989)
  Pallas kernels: 9.16 us -> 7.83 us
    pallas_call x10, Pallas kernels: 9.16 us -> 7.83 us  [call(): pl.pallas_call(kernel, out_shape=[jax.ShapeDtypeStruct(shape, dtype) for...]
  transfers between devices with their start and end apart: 8 -> 8, of which waited for: 2 -> 3; matrix products, arithmetic and copies ran while one was open for 0% -> 0% of each run, Pallas kernels for 3% -> 2%
where the time goes in v9:
time: 87.6 us; the launch traced here: 87.1 us
  blocking collectives  38.4 us (44%)
  starting transfers between devices  35.9 us (41%)
  Pallas kernels  7.83 us (9%)
  waiting for transfers between devices  4.22 us (5%)
    ppermute x3, starting transfers between devices, swapped(): lax.ppermute(far, axis, [(i, (i + step) % count) for i, step in enumerate...  24.5 us
    all_to_all x1, blocking collectives, reduced(): parts = lax.all_to_all(slots, 'gx', 0, 0, tiled=True)  17.1 us
    all_to_all x1, blocking collectives, reduced(): parts = lax.all_to_all(copies, 'gy', 0, 0, tiled=True)  11.6 us
    all_gather x1, blocking collectives, reduced(): parts = lax.all_gather(part, 'gz', axis=0)  9.77 us
    pallas_call x10, Pallas kernels, call(): pl.pallas_call(kernel, out_shape=[jax.ShapeDtypeStruct(shape, dtype) for...  7.83 us
    ppermute x3, starting transfers between devices, swapped(): lax.ppermute(near, axis, [(i, i - step) for i, step in enumerate(steps)])  5.76 us
    ppermute x3, waiting for transfers between devices, swapped(): lax.ppermute(near, axis, [(i, i - step) for i, step in enumerate(steps)])  4.02 us
    all_to_all x1, starting transfers between devices, body(): gathered = lax.all_to_all(copies, 'gx', 0, 0, tiled=True)  3.57 us
  transfers between devices with their start and end apart: 8, of which 3 were waited for; matrix products, arithmetic and copies ran while one was open for 0% of the time, Pallas kernels for 2%

profile of v9, /device:TPU:1, one launch (start us, length us, event | category | flops | bytes accessed | tf_op | source)
XLA Modules:
  0.0 87.1 jit_solution(11738424941116966256)
XLA Ops:
  0.6 1.8 %shard_map.85 = (bf16[4,8,1024]{2,1,0:T(8,128)(2,1)S(1)}, bf16[4,8,1024]{2,1,0:T(8,128)(2,1)S(1)}, bf16[4,8,1024]{2,1,0:T(8,128)(2,1)S(1)}, bf16[4,8,1024]{2,1,0...) custom-call(bf16[4,8,1024]{2,1,0:T(8,128)(2,1)} %skip_in.1, ...), custom_call_target="tpu_custom_call" | custom-call | flops 100000 | bytes 400000 | tf_op jit(solution)/shard_map/pallas_call | solution.py:27
  2.4 12.4 %collective-permute-start = (bf16[4,8,1024]{2,1,0:T(8,128)(2,1)S(1)}, bf16[4,8,1024]{2,1,0:T(8,128)(2,1)S(1)}, u32[]{:S(2)}, u32[]{:S(2)}) collective-permute-start(bf16[4,8,1024]{2,1,0:T(8,128)(2,1)S(1)} %get-tuple-element.25), channel_id=1, source_target_pairs={{0,480},{32,64},{64,32},{96,128},{128,96},{160,192},{192,160},{224... | collective-permute-start | bytes 196616 | tf_op jit(solution)/shard_map/ppermute | solution.py:333
  14.9 1.9 %collective-permute-start.1 = (bf16[4,8,1024]{2,1,0:T(8,128)(2,1)S(1)}, bf16[4,8,1024]{2,1,0:T(8,128)(2,1)S(1)}, u32[]{:S(2)}, u32[]{:S(2)}) collective-permute-start(bf16[4,8,1024]{2,1,0:T(8,128)(2,1)S(1)} %get-tuple-element.26), channel_id=1, source_target_pairs={{0,32},{32,0},{64,96},{96,64},{128,160},{160,128},{192,224},{224,1... | collective-permute-start | bytes 196616 | tf_op jit(solution)/shard_map/ppermute | solution.py:334
  16.8 3.6 %all-to-all-start = ((bf16[16,8,1728]{2,1,0:T(8,128)(2,1)}), bf16[16,8,1728]{2,1,0:T(8,128)(2,1)S(1)}, u32[]{:S(2)}, u32[]{:S(2)}) async-start(bf16[16,8,1728]{2,1,0:T(8,128)(2,1)} %get-tuple-element.31), calls=%async_computation | async-start | bytes 917504 | tf_op jit(solution)/shard_map/all_to_all | solution.py:406
  20.4 0.0 collective-permute-done.1.xnear
  20.4 0.2 shard_map.86
  20.6 5.1 %collective-permute-start.2 = (bf16[14,2,1024]{2,1,0:T(2,128)(2,1)S(1)}, bf16[14,2,1024]{2,1,0:T(2,128)(2,1)S(1)}, u32[]{:S(2)}, u32[]{:S(2)}) collective-permute-start(bf16[14,2,1024]{2,1,0:T(2,128)(2,1)S(1)} %get-tuple-element.27), channel_id=1, source_target_pairs={{0,28},{4,8},{8,4},{12,16},{16,12},{20,24},{24,20},{28,0},{1,29},{... | collective-permute-start | bytes 172040 | tf_op jit(solution)/shard_map/ppermute | solution.py:333
  25.7 1.9 %collective-permute-start.3 = (bf16[14,2,1024]{2,1,0:T(2,128)(2,1)S(1)}, bf16[14,2,1024]{2,1,0:T(2,128)(2,1)S(1)}, u32[]{:S(2)}, u32[]{:S(2)}) collective-permute-start(bf16[14,2,1024]{2,1,0:T(2,128)(2,1)S(1)} %get-tuple-element.28), channel_id=1, source_target_pairs={{0,4},{4,0},{8,12},{12,8},{16,20},{20,16},{24,28},{28,24},{1,5},{5... | collective-permute-start | bytes 172040 | tf_op jit(solution)/shard_map/ppermute | solution.py:334
  27.7 3.3 %collective-permute-done.3.ynear = bf16[14,2,1024]{2,1,0:T(2,128)(2,1)S(1)} collective-permute-done((bf16[14,2,1024]{2,1,0:T(2,128)(2,1)S(1)}, bf16[14,2,1024]{2,1,0:T(2,128)(2,1)S(1)}, u32[]{:S(2)}, u32[]{:S(2)}) %collective-permute-start.3) | collective-permute-done | bytes 57376 | tf_op jit(solution)/shard_map/ppermute | solution.py:334
  30.9 0.1 shard_map.87
  31.1 7.0 %collective-permute-start.4 = (bf16[168,128]{1,0:T(8,128)(2,1)S(1)}, bf16[168,128]{1,0:T(8,128)(2,1)S(1)}, u32[]{:S(2)}, u32[]{:S(2)}) collective-permute-start(bf16[168,128]{1,0:T(8,128)(2,1)S(1)} %get-tuple-element.29), channel_id=1, source_target_pairs={{0,3},{1,2},{2,1},{3,0},{4,7},{5,6},{6,5},{7,4},{8,11},{9,10},{10,... | collective-permute-start | bytes 129032 | tf_op jit(solution)/shard_map/ppermute | solution.py:333
  38.0 1.9 %collective-permute-start.5 = (bf16[168,128]{1,0:T(8,128)(2,1)S(1)}, bf16[168,128]{1,0:T(8,128)(2,1)S(1)}, u32[]{:S(2)}, u32[]{:S(2)}) collective-permute-start(bf16[168,128]{1,0:T(8,128)(2,1)S(1)} %get-tuple-element.30), channel_id=1, source_target_pairs={{0,1},{1,0},{2,3},{3,2},{4,5},{5,4},{6,7},{7,6},{8,9},{9,8},{10,11... | collective-permute-start | bytes 129032 | tf_op jit(solution)/shard_map/ppermute | solution.py:334
  40.0 0.4 shard_map.88
  40.4 0.0 collective-permute-done.4.zfar
  40.4 0.7 collective-permute-done.5.znear
  41.2 3.4 %shard_map.89 = (f32[16,4,1728]{2,1,0:T(4,128)S(1)}, bf16[16,4,1728]{2,1,0:T(4,128)(2,1)S(1)}, bf16[144,1408]{1,0:T(8,128)(2,1)S(1)}) custom-call(bf16[4,8,1024]{2,1,0:T(8,128)(2,1)S(1)} %get-tuple-element.22.grad, bf16[4,8,1024]{2,1,0:T(8,128)(2,1)S(1)} %get-tuple-element.23.pre, bf16[4,8,1024]{2,1,0:T(8,128)(2,1)S(1)} %get-tuple-element.24.inp, ...), custom_call_target="tpu_custom_call" | custom-call | flops 1800000000 | bytes 8000000 | tf_op jit(solution)/shard_map/pallas_call | solution.py:27
  44.5 2.1 %collective-permute-start.6 = (bf16[16,4,1728]{2,1,0:T(4,128)(2,1)S(1)}, bf16[16,4,1728]{2,1,0:T(4,128)(2,1)S(1)}, u32[]{:S(2)}, u32[]{:S(2)}) collective-permute-start(bf16[16,4,1728]{2,1,0:T(4,128)(2,1)S(1)} %get-tuple-element.33), channel_id=1, source_target_pairs={{0,1},{1,0},{2,3},{3,2},{4,5},{5,4},{6,7},{7,6},{8,9},{9,8},{10,11... | collective-permute-start | bytes 663560 | tf_op jit(solution)/shard_map/ppermute | solution.py:366
  46.6 1.1 %shard_map.90 = bf16[4,8,1024]{2,1,0:T(8,128)(2,1)} custom-call(bf16[144,1408]{1,0:T(8,128)(2,1)S(1)} %get-tuple-element.34.pre_grad, bf16[4,8,1024]{2,1,0:T(8,128)(2,1)S(1)} %get-tuple-element.22.grad, bf16[2304,128]{1,0:T(8,128)(2,1)S(1)} %get-tuple-element.35.band), custom_call_target="tpu_custom_call" | custom-call | flops 500000000 | bytes 4000000 | tf_op jit(solution)/shard_map/pallas_call | solution.py:27
  47.7 0.2 collective-permute-done.6.came
  47.9 0.1 shard_map.91
  48.0 17.1 %all_to_all.15.parts = bf16[16,4,1728]{2,1,0:T(4,128)(2,1)S(1)} all-to-all(bf16[16,4,1728]{2,1,0:T(4,128)(2,1)S(1)} %shard_map.91), channel_id=1, replica_groups=mesh['gx'=16,'gy'=8,'gz'=4] {'gx'}, dimensions={0} | all-to-all | bytes 442368 | tf_op jit(solution)/shard_map/all_to_all | solution.py:369
  65.1 11.6 %all_to_all.16.parts = bf16[8,4,1728]{2,1,0:T(4,128)(2,1)S(1)} all-to-all(bf16[8,4,1728]{2,1,0:T(4,128)(2,1)S(1)} %shard_map.92), channel_id=1, replica_groups=mesh['gx'=16,'gy'=8,'gz'=4] {'gy'}, dimensions={0} | all-to-all | bytes 221184 | tf_op jit(solution)/shard_map/all_to_all | solution.py:371
  76.7 9.8 %all-gather.1.parts = f32[4,4,1728]{2,1,0:T(4,128)S(1)} all-gather(f32[1,4,1728]{2,1,0:T(4,128)S(1)} %bitcast.1), channel_id=2, replica_groups=mesh['gx'=16,'gy'=8,'gz'=4] {'gz'}, dimensions={0}, use_global_device_ids=true | all-gather | bytes 138240 | tf_op jit(solution)/shard_map/all_gather | solution.py:373
  86.5 0.6 shard_map.94
  (5 shorter events, 0.1 us)
Async XLA Ops:
  2.4 17.9 %collective-permute-start = (bf16[4,8,1024]{2,1,0:T(8,128)(2,1)S(1)}, bf16[4,8,1024]{2,1,0:T(8,128)(2,1)S(1)}, u32[]{:S(2)}, u32[]{:S(2)}) collective-permute-start(bf16[4,8,1024]{2,1,0:T(8,128)(2,1)S(1)} %get-tuple-element.25), channel_id=1, source_target_pairs={{0,480},{32,64},{64,32},{96,128},{128,96},{160,192},{192,160},{224... | collective-permute-start | bytes 196616 | tf_op jit(solution)/shard_map/ppermute | solution.py:333
  14.9 5.5 %collective-permute-start.1 = (bf16[4,8,1024]{2,1,0:T(8,128)(2,1)S(1)}, bf16[4,8,1024]{2,1,0:T(8,128)(2,1)S(1)}, u32[]{:S(2)}, u32[]{:S(2)}) collective-permute-start(bf16[4,8,1024]{2,1,0:T(8,128)(2,1)S(1)} %get-tuple-element.26), channel_id=1, source_target_pairs={{0,32},{32,0},{64,96},{96,64},{128,160},{160,128},{192,224},{224,1... | collective-permute-start | bytes 196616 | tf_op jit(solution)/shard_map/ppermute | solution.py:334
  16.8 23.2 %all-to-all-start = ((bf16[16,8,1728]{2,1,0:T(8,128)(2,1)}), bf16[16,8,1728]{2,1,0:T(8,128)(2,1)S(1)}, u32[]{:S(2)}, u32[]{:S(2)}) async-start(bf16[16,8,1728]{2,1,0:T(8,128)(2,1)} %get-tuple-element.31), calls=%async_computation | async-start | bytes 917504 | tf_op jit(solution)/shard_map/all_to_all | solution.py:406
  20.6 7.0 %collective-permute-start.2 = (bf16[14,2,1024]{2,1,0:T(2,128)(2,1)S(1)}, bf16[14,2,1024]{2,1,0:T(2,128)(2,1)S(1)}, u32[]{:S(2)}, u32[]{:S(2)}) collective-permute-start(bf16[14,2,1024]{2,1,0:T(2,128)(2,1)S(1)} %get-tuple-element.27), channel_id=1, source_target_pairs={{0,28},{4,8},{8,4},{12,16},{16,12},{20,24},{24,20},{28,0},{1,29},{... | collective-permute-start | bytes 172040 | tf_op jit(solution)/shard_map/ppermute | solution.py:333
  25.7 5.2 %collective-permute-start.3 = (bf16[14,2,1024]{2,1,0:T(2,128)(2,1)S(1)}, bf16[14,2,1024]{2,1,0:T(2,128)(2,1)S(1)}, u32[]{:S(2)}, u32[]{:S(2)}) collective-permute-start(bf16[14,2,1024]{2,1,0:T(2,128)(2,1)S(1)} %get-tuple-element.28), channel_id=1, source_target_pairs={{0,4},{4,0},{8,12},{12,8},{16,20},{20,16},{24,28},{28,24},{1,5},{5... | collective-permute-start | bytes 172040 | tf_op jit(solution)/shard_map/ppermute | solution.py:334
  31.1 9.3 %collective-permute-start.4 = (bf16[168,128]{1,0:T(8,128)(2,1)S(1)}, bf16[168,128]{1,0:T(8,128)(2,1)S(1)}, u32[]{:S(2)}, u32[]{:S(2)}) collective-permute-start(bf16[168,128]{1,0:T(8,128)(2,1)S(1)} %get-tuple-element.29), channel_id=1, source_target_pairs={{0,3},{1,2},{2,1},{3,0},{4,7},{5,6},{6,5},{7,4},{8,11},{9,10},{10,... | collective-permute-start | bytes 129032 | tf_op jit(solution)/shard_map/ppermute | solution.py:333
  38.0 3.1 %collective-permute-start.5 = (bf16[168,128]{1,0:T(8,128)(2,1)S(1)}, bf16[168,128]{1,0:T(8,128)(2,1)S(1)}, u32[]{:S(2)}, u32[]{:S(2)}) collective-permute-start(bf16[168,128]{1,0:T(8,128)(2,1)S(1)} %get-tuple-element.30), channel_id=1, source_target_pairs={{0,1},{1,0},{2,3},{3,2},{4,5},{5,4},{6,7},{7,6},{8,9},{9,8},{10,11... | collective-permute-start | bytes 129032 | tf_op jit(solution)/shard_map/ppermute | solution.py:334
  44.5 3.4 %collective-permute-start.6 = (bf16[16,4,1728]{2,1,0:T(4,128)(2,1)S(1)}, bf16[16,4,1728]{2,1,0:T(4,128)(2,1)S(1)}, u32[]{:S(2)}, u32[]{:S(2)}) collective-permute-start(bf16[16,4,1728]{2,1,0:T(4,128)(2,1)S(1)} %get-tuple-element.33), channel_id=1, source_target_pairs={{0,1},{1,0},{2,3},{3,2},{4,5},{5,4},{6,7},{7,6},{8,9},{9,8},{10,11... | collective-permute-start | bytes 663560 | tf_op jit(solution)/shard_map/ppermute | solution.py:366

commit v10 on v9

--- a/solution.py
+++ b/solution.py
@@ -364,9 +364,9 @@
     rows, columns = kept.shape[1:]
     gy, gz = lax.axis_size("gy"), lax.axis_size("gz")
     came = lax.ppermute(sent, "gz", [(i, i + 1 - 2 * (i % 2)) for i in range(gz)])
-    came, other = lax.optimization_barrier((came, other))
     (slots,) = call(pair_kernel, [(kept.shape, B16)], [], 1000, 500000, kept, came)
     parts = lax.all_to_all(slots, "gx", 0, 0, tiled=True)
+    parts, other = lax.optimization_barrier((parts, other))
     (copies,) = call(total_kernel, [((gy, rows, columns), B16)], [], 1000, 500000, parts)
     parts = lax.all_to_all(copies, "gy", 0, 0, tiled=True)
     (part,) = call(total_kernel, [((rows, columns), F32)], [], 1000, 500000, parts)

time: 87.6 us -> 88.6 us (1.011)
  blocking collectives: 38.4 us -> 21.3 us
  waiting for transfers between devices: 4.22 us -> 14.8 us
  starting transfers between devices: 35.9 us -> 42.6 us
    all_to_all x1 -> x0, blocking collectives: 17.1 us -> none  [reduced(): parts = lax.all_to_all(slots, 'gx', 0, 0, tiled=True)]
    all_to_all x0 -> x1, waiting for transfers between devices: none -> 9.47 us  [reduced(): parts = lax.all_to_all(slots, 'gx', 0, 0, tiled=True)]
    all_to_all x0 -> x1, starting transfers between devices: none -> 6.7 us  [reduced(): parts = lax.all_to_all(slots, 'gx', 0, 0, tiled=True)]
    ppermute x1, waiting for transfers between devices: 0.19 us -> 1.31 us  [reduced(): lax.ppermute(sent, 'gz', [(i, i + 1 - 2 * (i % 2)) for i in range(gz)])]
  transfers between devices with their start and end apart: 8 -> 9, of which waited for: 3 -> 4; matrix products, arithmetic and copies ran while one was open for 0% -> 0% of each run, Pallas kernels for 2% -> 2%
where the time goes in v10:
time: 88.6 us; the launch traced here: 88 us
  starting transfers between devices  42.6 us (48%)
  blocking collectives  21.3 us (24%)
  waiting for transfers between devices  14.8 us (17%)
  Pallas kernels  8.53 us (10%)
    ppermute x3, starting transfers between devices, swapped(): lax.ppermute(far, axis, [(i, (i + step) % count) for i, step in enumerate...  24.5 us
    all_to_all x1, blocking collectives, reduced(): parts = lax.all_to_all(copies, 'gy', 0, 0, tiled=True)  11.6 us
    all_gather x1, blocking collectives, reduced(): parts = lax.all_gather(part, 'gz', axis=0)  9.77 us
    all_to_all x1, waiting for transfers between devices, reduced(): parts = lax.all_to_all(slots, 'gx', 0, 0, tiled=True)  9.47 us
    pallas_call x10, Pallas kernels, call(): pl.pallas_call(kernel, out_shape=[jax.ShapeDtypeStruct(shape, dtype) for...  8.53 us
    all_to_all x1, starting transfers between devices, reduced(): parts = lax.all_to_all(slots, 'gx', 0, 0, tiled=True)  6.7 us
    ppermute x3, starting transfers between devices, swapped(): lax.ppermute(near, axis, [(i, i - step) for i, step in enumerate(steps)])  5.76 us
    ppermute x3, waiting for transfers between devices, swapped(): lax.ppermute(near, axis, [(i, i - step) for i, step in enumerate(steps)])  4.02 us
  transfers between devices with their start and end apart: 9, of which 4 were waited for; matrix products, arithmetic and copies ran while one was open for 0% of the time, Pallas kernels for 2%

profile of v10, /device:TPU:1, one launch (start us, length us, event | category | flops | bytes accessed | tf_op | source)
XLA Modules:
  0.0 88.0 jit_solution(8961099036183993953)
XLA Ops:
  0.6 1.8 %shard_map.85 = (bf16[4,8,1024]{2,1,0:T(8,128)(2,1)S(1)}, bf16[4,8,1024]{2,1,0:T(8,128)(2,1)S(1)}, bf16[4,8,1024]{2,1,0:T(8,128)(2,1)S(1)}, bf16[4,8,1024]{2,1,0...) custom-call(bf16[4,8,1024]{2,1,0:T(8,128)(2,1)} %skip_in.1, ...), custom_call_target="tpu_custom_call" | custom-call | flops 100000 | bytes 400000 | tf_op jit(solution)/shard_map/pallas_call | solution.py:27
  2.4 12.4 %collective-permute-start = (bf16[4,8,1024]{2,1,0:T(8,128)(2,1)S(1)}, bf16[4,8,1024]{2,1,0:T(8,128)(2,1)S(1)}, u32[]{:S(2)}, u32[]{:S(2)}) collective-permute-start(bf16[4,8,1024]{2,1,0:T(8,128)(2,1)S(1)} %get-tuple-element.25), channel_id=1, source_target_pairs={{0,480},{32,64},{64,32},{96,128},{128,96},{160,192},{192,160},{224... | collective-permute-start | bytes 196616 | tf_op jit(solution)/shard_map/ppermute | solution.py:333
  14.9 1.9 %collective-permute-start.1 = (bf16[4,8,1024]{2,1,0:T(8,128)(2,1)S(1)}, bf16[4,8,1024]{2,1,0:T(8,128)(2,1)S(1)}, u32[]{:S(2)}, u32[]{:S(2)}) collective-permute-start(bf16[4,8,1024]{2,1,0:T(8,128)(2,1)S(1)} %get-tuple-element.26), channel_id=1, source_target_pairs={{0,32},{32,0},{64,96},{96,64},{128,160},{160,128},{192,224},{224,1... | collective-permute-start | bytes 196616 | tf_op jit(solution)/shard_map/ppermute | solution.py:334
  16.8 3.6 %all-to-all-start = ((bf16[16,8,1728]{2,1,0:T(8,128)(2,1)}), bf16[16,8,1728]{2,1,0:T(8,128)(2,1)S(1)}, u32[]{:S(2)}, u32[]{:S(2)}) async-start(bf16[16,8,1728]{2,1,0:T(8,128)(2,1)} %get-tuple-element.31), calls=%async_computation | async-start | bytes 917504 | tf_op jit(solution)/shard_map/all_to_all | solution.py:406
  20.4 0.0 collective-permute-done.xfar
  20.4 0.2 shard_map.86
  20.6 5.1 %collective-permute-start.2 = (bf16[14,2,1024]{2,1,0:T(2,128)(2,1)S(1)}, bf16[14,2,1024]{2,1,0:T(2,128)(2,1)S(1)}, u32[]{:S(2)}, u32[]{:S(2)}) collective-permute-start(bf16[14,2,1024]{2,1,0:T(2,128)(2,1)S(1)} %get-tuple-element.27), channel_id=1, source_target_pairs={{0,28},{4,8},{8,4},{12,16},{16,12},{20,24},{24,20},{28,0},{1,29},{... | collective-permute-start | bytes 172040 | tf_op jit(solution)/shard_map/ppermute | solution.py:333
  25.7 1.9 %collective-permute-start.3 = (bf16[14,2,1024]{2,1,0:T(2,128)(2,1)S(1)}, bf16[14,2,1024]{2,1,0:T(2,128)(2,1)S(1)}, u32[]{:S(2)}, u32[]{:S(2)}) collective-permute-start(bf16[14,2,1024]{2,1,0:T(2,128)(2,1)S(1)} %get-tuple-element.28), channel_id=1, source_target_pairs={{0,4},{4,0},{8,12},{12,8},{16,20},{20,16},{24,28},{28,24},{1,5},{5... | collective-permute-start | bytes 172040 | tf_op jit(solution)/shard_map/ppermute | solution.py:334
  27.7 3.3 %collective-permute-done.3.ynear = bf16[14,2,1024]{2,1,0:T(2,128)(2,1)S(1)} collective-permute-done((bf16[14,2,1024]{2,1,0:T(2,128)(2,1)S(1)}, bf16[14,2,1024]{2,1,0:T(2,128)(2,1)S(1)}, u32[]{:S(2)}, u32[]{:S(2)}) %collective-permute-start.3) | collective-permute-done | bytes 57376 | tf_op jit(solution)/shard_map/ppermute | solution.py:334
  30.9 0.1 shard_map.87
  31.1 7.0 %collective-permute-start.4 = (bf16[168,128]{1,0:T(8,128)(2,1)S(1)}, bf16[168,128]{1,0:T(8,128)(2,1)S(1)}, u32[]{:S(2)}, u32[]{:S(2)}) collective-permute-start(bf16[168,128]{1,0:T(8,128)(2,1)S(1)} %get-tuple-element.29), channel_id=1, source_target_pairs={{0,3},{1,2},{2,1},{3,0},{4,7},{5,6},{6,5},{7,4},{8,11},{9,10},{10,... | collective-permute-start | bytes 129032 | tf_op jit(solution)/shard_map/ppermute | solution.py:333
  38.0 1.9 %collective-permute-start.5 = (bf16[168,128]{1,0:T(8,128)(2,1)S(1)}, bf16[168,128]{1,0:T(8,128)(2,1)S(1)}, u32[]{:S(2)}, u32[]{:S(2)}) collective-permute-start(bf16[168,128]{1,0:T(8,128)(2,1)S(1)} %get-tuple-element.30), channel_id=1, source_target_pairs={{0,1},{1,0},{2,3},{3,2},{4,5},{5,4},{6,7},{7,6},{8,9},{9,8},{10,11... | collective-permute-start | bytes 129032 | tf_op jit(solution)/shard_map/ppermute | solution.py:334
  40.0 0.4 shard_map.88
  40.4 0.7 collective-permute-done.5.znear
  41.2 3.4 %shard_map.89 = (f32[16,4,1728]{2,1,0:T(4,128)S(1)}, bf16[16,4,1728]{2,1,0:T(4,128)(2,1)S(1)}, bf16[144,1408]{1,0:T(8,128)(2,1)S(1)}) custom-call(bf16[4,8,1024]{2,1,0:T(8,128)(2,1)S(1)} %get-tuple-element.22.grad, bf16[4,8,1024]{2,1,0:T(8,128)(2,1)S(1)} %get-tuple-element.23.pre, bf16[4,8,1024]{2,1,0:T(8,128)(2,1)S(1)} %get-tuple-element.24.inp, ...), custom_call_target="tpu_custom_call" | custom-call | flops 1800000000 | bytes 8000000 | tf_op jit(solution)/shard_map/pallas_call | solution.py:27
  44.5 2.1 %collective-permute-start.6 = (bf16[16,4,1728]{2,1,0:T(4,128)(2,1)S(1)}, bf16[16,4,1728]{2,1,0:T(4,128)(2,1)S(1)}, u32[]{:S(2)}, u32[]{:S(2)}) collective-permute-start(bf16[16,4,1728]{2,1,0:T(4,128)(2,1)S(1)} %get-tuple-element.34), channel_id=1, source_target_pairs={{0,1},{1,0},{2,3},{3,2},{4,5},{5,4},{6,7},{7,6},{8,9},{9,8},{10,11... | collective-permute-start | bytes 663560 | tf_op jit(solution)/shard_map/ppermute | solution.py:366
  46.6 1.3 %collective-permute-done.6.came = bf16[16,4,1728]{2,1,0:T(4,128)(2,1)S(1)} collective-permute-done((bf16[16,4,1728]{2,1,0:T(4,128)(2,1)S(1)}, bf16[16,4,1728]{2,1,0:T(4,128)(2,1)S(1)}, u32[]{:S(2)}, u32[]{:S(2)}) %collective-permute-start.6) | collective-permute-done | bytes 221216 | tf_op jit(solution)/shard_map/ppermute | solution.py:366
  47.9 0.8 shard_map.90
  48.7 6.7 %all-to-all-start.1 = ((bf16[16,4,1728]{2,1,0:T(4,128)(2,1)}), bf16[16,4,1728]{2,1,0:T(4,128)(2,1)S(1)}, u32[]{:S(2)}, u32[]{:S(2)}) async-start(bf16[16,4,1728]{2,1,0:T(4,128)(2,1)} %shard_map.90), calls=%async_computation.1 | async-start | bytes 458752 | tf_op jit(solution)/shard_map/all_to_all | solution.py:368
  55.4 1.1 %shard_map.91 = bf16[4,8,1024]{2,1,0:T(8,128)(2,1)} custom-call(bf16[144,1408]{1,0:T(8,128)(2,1)S(1)} %get-tuple-element.35.pre_grad, bf16[4,8,1024]{2,1,0:T(8,128)(2,1)S(1)} %get-tuple-element.22.grad, bf16[2304,128]{1,0:T(8,128)(2,1)S(1)} %get-tuple-element.36.band), custom_call_target="tpu_custom_call" | custom-call | flops 500000000 | bytes 4000000 | tf_op jit(solution)/shard_map/pallas_call | solution.py:27
  56.5 9.5 %all-to-all-done.1.parts = bf16[16,4,1728]{2,1,0:T(4,128)(2,1)S(1)} async-done(((bf16[16,4,1728]{2,1,0:T(4,128)(2,1)}), bf16[16,4,1728]{2,1,0:T(4,128)(2,1)S(1)}, u32[]{:S(2)}, u32[]{:S(2)}) %all-to-all-start.1) | async-done | bytes 221216 | tf_op jit(solution)/shard_map/all_to_all | solution.py:368
  66.0 11.6 %all_to_all.15.parts = bf16[8,4,1728]{2,1,0:T(4,128)(2,1)S(1)} all-to-all(bf16[8,4,1728]{2,1,0:T(4,128)(2,1)S(1)} %shard_map.92), channel_id=1, replica_groups=mesh['gx'=16,'gy'=8,'gz'=4] {'gy'}, dimensions={0} | all-to-all | bytes 221184 | tf_op jit(solution)/shard_map/all_to_all | solution.py:371
  77.6 9.8 %all-gather.1.parts = f32[4,4,1728]{2,1,0:T(4,128)S(1)} all-gather(f32[1,4,1728]{2,1,0:T(4,128)S(1)} %bitcast.1), channel_id=2, replica_groups=mesh['gx'=16,'gy'=8,'gz'=4] {'gz'}, dimensions={0}, use_global_device_ids=true | all-gather | bytes 138240 | tf_op jit(solution)/shard_map/all_gather | solution.py:373
  87.4 0.6 shard_map.94
  (6 shorter events, 0.1 us)
Async XLA Ops:
  2.4 17.9 %collective-permute-start = (bf16[4,8,1024]{2,1,0:T(8,128)(2,1)S(1)}, bf16[4,8,1024]{2,1,0:T(8,128)(2,1)S(1)}, u32[]{:S(2)}, u32[]{:S(2)}) collective-permute-start(bf16[4,8,1024]{2,1,0:T(8,128)(2,1)S(1)} %get-tuple-element.25), channel_id=1, source_target_pairs={{0,480},{32,64},{64,32},{96,128},{128,96},{160,192},{192,160},{224... | collective-permute-start | bytes 196616 | tf_op jit(solution)/shard_map/ppermute | solution.py:333
  14.9 5.5 %collective-permute-start.1 = (bf16[4,8,1024]{2,1,0:T(8,128)(2,1)S(1)}, bf16[4,8,1024]{2,1,0:T(8,128)(2,1)S(1)}, u32[]{:S(2)}, u32[]{:S(2)}) collective-permute-start(bf16[4,8,1024]{2,1,0:T(8,128)(2,1)S(1)} %get-tuple-element.26), channel_id=1, source_target_pairs={{0,32},{32,0},{64,96},{96,64},{128,160},{160,128},{192,224},{224,1... | collective-permute-start | bytes 196616 | tf_op jit(solution)/shard_map/ppermute | solution.py:334
  16.8 23.2 %all-to-all-start = ((bf16[16,8,1728]{2,1,0:T(8,128)(2,1)}), bf16[16,8,1728]{2,1,0:T(8,128)(2,1)S(1)}, u32[]{:S(2)}, u32[]{:S(2)}) async-start(bf16[16,8,1728]{2,1,0:T(8,128)(2,1)} %get-tuple-element.31), calls=%async_computation | async-start | bytes 917504 | tf_op jit(solution)/shard_map/all_to_all | solution.py:406
  20.6 7.0 %collective-permute-start.2 = (bf16[14,2,1024]{2,1,0:T(2,128)(2,1)S(1)}, bf16[14,2,1024]{2,1,0:T(2,128)(2,1)S(1)}, u32[]{:S(2)}, u32[]{:S(2)}) collective-permute-start(bf16[14,2,1024]{2,1,0:T(2,128)(2,1)S(1)} %get-tuple-element.27), channel_id=1, source_target_pairs={{0,28},{4,8},{8,4},{12,16},{16,12},{20,24},{24,20},{28,0},{1,29},{... | collective-permute-start | bytes 172040 | tf_op jit(solution)/shard_map/ppermute | solution.py:333
  25.7 5.2 %collective-permute-start.3 = (bf16[14,2,1024]{2,1,0:T(2,128)(2,1)S(1)}, bf16[14,2,1024]{2,1,0:T(2,128)(2,1)S(1)}, u32[]{:S(2)}, u32[]{:S(2)}) collective-permute-start(bf16[14,2,1024]{2,1,0:T(2,128)(2,1)S(1)} %get-tuple-element.28), channel_id=1, source_target_pairs={{0,4},{4,0},{8,12},{12,8},{16,20},{20,16},{24,28},{28,24},{1,5},{5... | collective-permute-start | bytes 172040 | tf_op jit(solution)/shard_map/ppermute | solution.py:334
  31.1 9.3 %collective-permute-start.4 = (bf16[168,128]{1,0:T(8,128)(2,1)S(1)}, bf16[168,128]{1,0:T(8,128)(2,1)S(1)}, u32[]{:S(2)}, u32[]{:S(2)}) collective-permute-start(bf16[168,128]{1,0:T(8,128)(2,1)S(1)} %get-tuple-element.29), channel_id=1, source_target_pairs={{0,3},{1,2},{2,1},{3,0},{4,7},{5,6},{6,5},{7,4},{8,11},{9,10},{10,... | collective-permute-start | bytes 129032 | tf_op jit(solution)/shard_map/ppermute | solution.py:333
  38.0 3.1 %collective-permute-start.5 = (bf16[168,128]{1,0:T(8,128)(2,1)S(1)}, bf16[168,128]{1,0:T(8,128)(2,1)S(1)}, u32[]{:S(2)}, u32[]{:S(2)}) collective-permute-start(bf16[168,128]{1,0:T(8,128)(2,1)S(1)} %get-tuple-element.30), channel_id=1, source_target_pairs={{0,1},{1,0},{2,3},{3,2},{4,5},{5,4},{6,7},{7,6},{8,9},{9,8},{10,11... | collective-permute-start | bytes 129032 | tf_op jit(solution)/shard_map/ppermute | solution.py:334
  44.5 3.4 %collective-permute-start.6 = (bf16[16,4,1728]{2,1,0:T(4,128)(2,1)S(1)}, bf16[16,4,1728]{2,1,0:T(4,128)(2,1)S(1)}, u32[]{:S(2)}, u32[]{:S(2)}) collective-permute-start(bf16[16,4,1728]{2,1,0:T(4,128)(2,1)S(1)} %get-tuple-element.34), channel_id=1, source_target_pairs={{0,1},{1,0},{2,3},{3,2},{4,5},{5,4},{6,7},{7,6},{8,9},{9,8},{10,11... | collective-permute-start | bytes 663560 | tf_op jit(solution)/shard_map/ppermute | solution.py:366
  48.7 17.3 %all-to-all-start.1 = ((bf16[16,4,1728]{2,1,0:T(4,128)(2,1)}), bf16[16,4,1728]{2,1,0:T(4,128)(2,1)S(1)}, u32[]{:S(2)}, u32[]{:S(2)}) async-start(bf16[16,4,1728]{2,1,0:T(4,128)(2,1)} %shard_map.90), calls=%async_computation.1 | async-start | bytes 458752 | tf_op jit(solution)/shard_map/all_to_all | solution.py:368

commit v11 on v9

--- a/solution.py
+++ b/solution.py
@@ -271,10 +271,13 @@
     fg[:, 128 * HALO_GROUPS :] = jnp.zeros((ROWS, WIDE - 128 * HALO_GROUPS), F32)
     place = edge_rows(1)
     beside = slope(jnp.dot(place, fa[:, : 128 * HALO_GROUPS].astype(B16), preferred_element_type=F32))
+    ends = jnp.concatenate(
+        [held[EDGES + 16 * h : EDGES + 16 * (h + 1), :] for h in range(HALO_GROUPS)], 1
+    )
+    value = (ends * beside).astype(B16)
+    fg[:, : 128 * HALO_GROUPS] = lax.dot_general(place, value, contract, preferred_element_type=F32)
     for h in range(HALO_GROUPS):
         lanes = slice(128 * h, 128 * (h + 1))
-        value = (held[EDGES + 16 * h : EDGES + 16 * (h + 1), :] * beside[:, lanes]).astype(B16)
-        fg[:, lanes] = lax.dot_general(place, value, contract, preferred_element_type=F32)
         for x in range(1, SX + 3):
             row, at = HALO_ROWS * h + 8 * (x - 1), slice(16 * (x + 1), 16 * (x + 1) + 8)
             value = held[row : row + 8, :] * slope(fa[at, lanes])

time: 87.6 us -> 87.4 us (level)
  no operation moved by 1% of the time
where the time goes in v11:
time: 87.4 us; the launch traced here: 86.9 us
  blocking collectives  38.4 us (44%)
  starting transfers between devices  35.9 us (41%)
  Pallas kernels  7.57 us (9%)
  waiting for transfers between devices  4.22 us (5%)
    ppermute x3, starting transfers between devices, swapped(): lax.ppermute(far, axis, [(i, (i + step) % count) for i, step in enumerate...  24.5 us
    all_to_all x1, blocking collectives, reduced(): parts = lax.all_to_all(slots, 'gx', 0, 0, tiled=True)  17.1 us
    all_to_all x1, blocking collectives, reduced(): parts = lax.all_to_all(copies, 'gy', 0, 0, tiled=True)  11.6 us
    all_gather x1, blocking collectives, reduced(): parts = lax.all_gather(part, 'gz', axis=0)  9.77 us
    pallas_call x10, Pallas kernels, call(): pl.pallas_call(kernel, out_shape=[jax.ShapeDtypeStruct(shape, dtype) for...  7.57 us
    ppermute x3, starting transfers between devices, swapped(): lax.ppermute(near, axis, [(i, i - step) for i, step in enumerate(steps)])  5.76 us
    ppermute x3, waiting for transfers between devices, swapped(): lax.ppermute(near, axis, [(i, i - step) for i, step in enumerate(steps)])  4.02 us
    all_to_all x1, starting transfers between devices, body(): gathered = lax.all_to_all(copies, 'gx', 0, 0, tiled=True)  3.57 us
  transfers between devices with their start and end apart: 8, of which 3 were waited for; matrix products, arithmetic and copies ran while one was open for 0% of the time, Pallas kernels for 2%

profile of v11, /device:TPU:1, one launch (start us, length us, event | category | flops | bytes accessed | tf_op | source)
XLA Modules:
  0.0 86.9 jit_solution(7182413148075249734)
XLA Ops:
  0.6 1.8 %shard_map.85 = (bf16[4,8,1024]{2,1,0:T(8,128)(2,1)S(1)}, bf16[4,8,1024]{2,1,0:T(8,128)(2,1)S(1)}, bf16[4,8,1024]{2,1,0:T(8,128)(2,1)S(1)}, bf16[4,8,1024]{2,1,0...) custom-call(bf16[4,8,1024]{2,1,0:T(8,128)(2,1)} %skip_in.1, ...), custom_call_target="tpu_custom_call" | custom-call | flops 100000 | bytes 400000 | tf_op jit(solution)/shard_map/pallas_call | solution.py:27
  2.4 12.4 %collective-permute-start = (bf16[4,8,1024]{2,1,0:T(8,128)(2,1)S(1)}, bf16[4,8,1024]{2,1,0:T(8,128)(2,1)S(1)}, u32[]{:S(2)}, u32[]{:S(2)}) collective-permute-start(bf16[4,8,1024]{2,1,0:T(8,128)(2,1)S(1)} %get-tuple-element.25), channel_id=1, source_target_pairs={{0,480},{32,64},{64,32},{96,128},{128,96},{160,192},{192,160},{224... | collective-permute-start | bytes 196616 | tf_op jit(solution)/shard_map/ppermute | solution.py:336
  14.9 1.9 %collective-permute-start.1 = (bf16[4,8,1024]{2,1,0:T(8,128)(2,1)S(1)}, bf16[4,8,1024]{2,1,0:T(8,128)(2,1)S(1)}, u32[]{:S(2)}, u32[]{:S(2)}) collective-permute-start(bf16[4,8,1024]{2,1,0:T(8,128)(2,1)S(1)} %get-tuple-element.26), channel_id=1, source_target_pairs={{0,32},{32,0},{64,96},{96,64},{128,160},{160,128},{192,224},{224,1... | collective-permute-start | bytes 196616 | tf_op jit(solution)/shard_map/ppermute | solution.py:337
  16.8 3.6 %all-to-all-start = ((bf16[16,8,1728]{2,1,0:T(8,128)(2,1)}), bf16[16,8,1728]{2,1,0:T(8,128)(2,1)S(1)}, u32[]{:S(2)}, u32[]{:S(2)}) async-start(bf16[16,8,1728]{2,1,0:T(8,128)(2,1)} %get-tuple-element.31), calls=%async_computation | async-start | bytes 917504 | tf_op jit(solution)/shard_map/all_to_all | solution.py:409
  20.4 0.0 collective-permute-done.xfar
  20.4 0.0 collective-permute-done.1.xnear
  20.4 0.2 shard_map.86
  20.6 5.1 %collective-permute-start.2 = (bf16[14,2,1024]{2,1,0:T(2,128)(2,1)S(1)}, bf16[14,2,1024]{2,1,0:T(2,128)(2,1)S(1)}, u32[]{:S(2)}, u32[]{:S(2)}) collective-permute-start(bf16[14,2,1024]{2,1,0:T(2,128)(2,1)S(1)} %get-tuple-element.27), channel_id=1, source_target_pairs={{0,28},{4,8},{8,4},{12,16},{16,12},{20,24},{24,20},{28,0},{1,29},{... | collective-permute-start | bytes 172040 | tf_op jit(solution)/shard_map/ppermute | solution.py:336
  25.7 1.9 %collective-permute-start.3 = (bf16[14,2,1024]{2,1,0:T(2,128)(2,1)S(1)}, bf16[14,2,1024]{2,1,0:T(2,128)(2,1)S(1)}, u32[]{:S(2)}, u32[]{:S(2)}) collective-permute-start(bf16[14,2,1024]{2,1,0:T(2,128)(2,1)S(1)} %get-tuple-element.28), channel_id=1, source_target_pairs={{0,4},{4,0},{8,12},{12,8},{16,20},{20,16},{24,28},{28,24},{1,5},{5... | collective-permute-start | bytes 172040 | tf_op jit(solution)/shard_map/ppermute | solution.py:337
  27.7 3.3 %collective-permute-done.3.ynear = bf16[14,2,1024]{2,1,0:T(2,128)(2,1)S(1)} collective-permute-done((bf16[14,2,1024]{2,1,0:T(2,128)(2,1)S(1)}, bf16[14,2,1024]{2,1,0:T(2,128)(2,1)S(1)}, u32[]{:S(2)}, u32[]{:S(2)}) %collective-permute-start.3) | collective-permute-done | bytes 57376 | tf_op jit(solution)/shard_map/ppermute | solution.py:337
  30.9 0.1 shard_map.87
  31.1 7.0 %collective-permute-start.4 = (bf16[168,128]{1,0:T(8,128)(2,1)S(1)}, bf16[168,128]{1,0:T(8,128)(2,1)S(1)}, u32[]{:S(2)}, u32[]{:S(2)}) collective-permute-start(bf16[168,128]{1,0:T(8,128)(2,1)S(1)} %get-tuple-element.29), channel_id=1, source_target_pairs={{0,3},{1,2},{2,1},{3,0},{4,7},{5,6},{6,5},{7,4},{8,11},{9,10},{10,... | collective-permute-start | bytes 129032 | tf_op jit(solution)/shard_map/ppermute | solution.py:336
  38.0 1.9 %collective-permute-start.5 = (bf16[168,128]{1,0:T(8,128)(2,1)S(1)}, bf16[168,128]{1,0:T(8,128)(2,1)S(1)}, u32[]{:S(2)}, u32[]{:S(2)}) collective-permute-start(bf16[168,128]{1,0:T(8,128)(2,1)S(1)} %get-tuple-element.30), channel_id=1, source_target_pairs={{0,1},{1,0},{2,3},{3,2},{4,5},{5,4},{6,7},{7,6},{8,9},{9,8},{10,11... | collective-permute-start | bytes 129032 | tf_op jit(solution)/shard_map/ppermute | solution.py:337
  40.0 0.4 shard_map.88
  40.4 0.7 collective-permute-done.5.znear
  41.2 3.1 %shard_map.89 = (f32[16,4,1728]{2,1,0:T(4,128)S(1)}, bf16[16,4,1728]{2,1,0:T(4,128)(2,1)S(1)}, bf16[144,1408]{1,0:T(8,128)(2,1)S(1)}) custom-call(bf16[4,8,1024]{2,1,0:T(8,128)(2,1)S(1)} %get-tuple-element.22.grad, bf16[4,8,1024]{2,1,0:T(8,128)(2,1)S(1)} %get-tuple-element.23.pre, bf16[4,8,1024]{2,1,0:T(8,128)(2,1)S(1)} %get-tuple-element.24.inp, ...), custom_call_target="tpu_custom_call" | custom-call | flops 1800000000 | bytes 8000000 | tf_op jit(solution)/shard_map/pallas_call | solution.py:27
  44.3 2.1 %collective-permute-start.6 = (bf16[16,4,1728]{2,1,0:T(4,128)(2,1)S(1)}, bf16[16,4,1728]{2,1,0:T(4,128)(2,1)S(1)}, u32[]{:S(2)}, u32[]{:S(2)}) collective-permute-start(bf16[16,4,1728]{2,1,0:T(4,128)(2,1)S(1)} %get-tuple-element.33), channel_id=1, source_target_pairs={{0,1},{1,0},{2,3},{3,2},{4,5},{5,4},{6,7},{7,6},{8,9},{9,8},{10,11... | collective-permute-start | bytes 663560 | tf_op jit(solution)/shard_map/ppermute | solution.py:369
  46.3 1.1 %shard_map.90 = bf16[4,8,1024]{2,1,0:T(8,128)(2,1)} custom-call(bf16[144,1408]{1,0:T(8,128)(2,1)S(1)} %get-tuple-element.34.pre_grad, bf16[4,8,1024]{2,1,0:T(8,128)(2,1)S(1)} %get-tuple-element.22.grad, bf16[2304,128]{1,0:T(8,128)(2,1)S(1)} %get-tuple-element.35.band), custom_call_target="tpu_custom_call" | custom-call | flops 500000000 | bytes 4000000 | tf_op jit(solution)/shard_map/pallas_call | solution.py:27
  47.5 0.2 collective-permute-done.6.came
  47.6 0.1 shard_map.91
  47.7 17.1 %all_to_all.15.parts = bf16[16,4,1728]{2,1,0:T(4,128)(2,1)S(1)} all-to-all(bf16[16,4,1728]{2,1,0:T(4,128)(2,1)S(1)} %shard_map.91), channel_id=1, replica_groups=mesh['gx'=16,'gy'=8,'gz'=4] {'gx'}, dimensions={0} | all-to-all | bytes 442368 | tf_op jit(solution)/shard_map/all_to_all | solution.py:372
  64.9 11.6 %all_to_all.16.parts = bf16[8,4,1728]{2,1,0:T(4,128)(2,1)S(1)} all-to-all(bf16[8,4,1728]{2,1,0:T(4,128)(2,1)S(1)} %shard_map.92), channel_id=1, replica_groups=mesh['gx'=16,'gy'=8,'gz'=4] {'gy'}, dimensions={0} | all-to-all | bytes 221184 | tf_op jit(solution)/shard_map/all_to_all | solution.py:374
  76.5 9.8 %all-gather.1.parts = f32[4,4,1728]{2,1,0:T(4,128)S(1)} all-gather(f32[1,4,1728]{2,1,0:T(4,128)S(1)} %bitcast.1), channel_id=2, replica_groups=mesh['gx'=16,'gy'=8,'gz'=4] {'gz'}, dimensions={0}, use_global_device_ids=true | all-gather | bytes 138240 | tf_op jit(solution)/shard_map/all_gather | solution.py:376
  86.2 0.6 shard_map.94
  (5 shorter events, 0.1 us)
Async XLA Ops:
  2.4 17.9 %collective-permute-start = (bf16[4,8,1024]{2,1,0:T(8,128)(2,1)S(1)}, bf16[4,8,1024]{2,1,0:T(8,128)(2,1)S(1)}, u32[]{:S(2)}, u32[]{:S(2)}) collective-permute-start(bf16[4,8,1024]{2,1,0:T(8,128)(2,1)S(1)} %get-tuple-element.25), channel_id=1, source_target_pairs={{0,480},{32,64},{64,32},{96,128},{128,96},{160,192},{192,160},{224... | collective-permute-start | bytes 196616 | tf_op jit(solution)/shard_map/ppermute | solution.py:336
  14.9 5.5 %collective-permute-start.1 = (bf16[4,8,1024]{2,1,0:T(8,128)(2,1)S(1)}, bf16[4,8,1024]{2,1,0:T(8,128)(2,1)S(1)}, u32[]{:S(2)}, u32[]{:S(2)}) collective-permute-start(bf16[4,8,1024]{2,1,0:T(8,128)(2,1)S(1)} %get-tuple-element.26), channel_id=1, source_target_pairs={{0,32},{32,0},{64,96},{96,64},{128,160},{160,128},{192,224},{224,1... | collective-permute-start | bytes 196616 | tf_op jit(solution)/shard_map/ppermute | solution.py:337
  16.8 23.2 %all-to-all-start = ((bf16[16,8,1728]{2,1,0:T(8,128)(2,1)}), bf16[16,8,1728]{2,1,0:T(8,128)(2,1)S(1)}, u32[]{:S(2)}, u32[]{:S(2)}) async-start(bf16[16,8,1728]{2,1,0:T(8,128)(2,1)} %get-tuple-element.31), calls=%async_computation | async-start | bytes 917504 | tf_op jit(solution)/shard_map/all_to_all | solution.py:409
  20.6 7.0 %collective-permute-start.2 = (bf16[14,2,1024]{2,1,0:T(2,128)(2,1)S(1)}, bf16[14,2,1024]{2,1,0:T(2,128)(2,1)S(1)}, u32[]{:S(2)}, u32[]{:S(2)}) collective-permute-start(bf16[14,2,1024]{2,1,0:T(2,128)(2,1)S(1)} %get-tuple-element.27), channel_id=1, source_target_pairs={{0,28},{4,8},{8,4},{12,16},{16,12},{20,24},{24,20},{28,0},{1,29},{... | collective-permute-start | bytes 172040 | tf_op jit(solution)/shard_map/ppermute | solution.py:336
  25.7 5.2 %collective-permute-start.3 = (bf16[14,2,1024]{2,1,0:T(2,128)(2,1)S(1)}, bf16[14,2,1024]{2,1,0:T(2,128)(2,1)S(1)}, u32[]{:S(2)}, u32[]{:S(2)}) collective-permute-start(bf16[14,2,1024]{2,1,0:T(2,128)(2,1)S(1)} %get-tuple-element.28), channel_id=1, source_target_pairs={{0,4},{4,0},{8,12},{12,8},{16,20},{20,16},{24,28},{28,24},{1,5},{5... | collective-permute-start | bytes 172040 | tf_op jit(solution)/shard_map/ppermute | solution.py:337
  31.1 9.3 %collective-permute-start.4 = (bf16[168,128]{1,0:T(8,128)(2,1)S(1)}, bf16[168,128]{1,0:T(8,128)(2,1)S(1)}, u32[]{:S(2)}, u32[]{:S(2)}) collective-permute-start(bf16[168,128]{1,0:T(8,128)(2,1)S(1)} %get-tuple-element.29), channel_id=1, source_target_pairs={{0,3},{1,2},{2,1},{3,0},{4,7},{5,6},{6,5},{7,4},{8,11},{9,10},{10,... | collective-permute-start | bytes 129032 | tf_op jit(solution)/shard_map/ppermute | solution.py:336
  38.0 3.1 %collective-permute-start.5 = (bf16[168,128]{1,0:T(8,128)(2,1)S(1)}, bf16[168,128]{1,0:T(8,128)(2,1)S(1)}, u32[]{:S(2)}, u32[]{:S(2)}) collective-permute-start(bf16[168,128]{1,0:T(8,128)(2,1)S(1)} %get-tuple-element.30), channel_id=1, source_target_pairs={{0,1},{1,0},{2,3},{3,2},{4,5},{5,4},{6,7},{7,6},{8,9},{9,8},{10,11... | collective-permute-start | bytes 129032 | tf_op jit(solution)/shard_map/ppermute | solution.py:337
  44.3 3.4 %collective-permute-start.6 = (bf16[16,4,1728]{2,1,0:T(4,128)(2,1)S(1)}, bf16[16,4,1728]{2,1,0:T(4,128)(2,1)S(1)}, u32[]{:S(2)}, u32[]{:S(2)}) collective-permute-start(bf16[16,4,1728]{2,1,0:T(4,128)(2,1)S(1)} %get-tuple-element.33), channel_id=1, source_target_pairs={{0,1},{1,0},{2,3},{3,2},{4,5},{5,4},{6,7},{7,6},{8,9},{9,8},{10,11... | collective-permute-start | bytes 663560 | tf_op jit(solution)/shard_map/ppermute | solution.py:369

commit v12 on v11

--- a/solution.py
+++ b/solution.py
@@ -228,7 +228,7 @@
     return g * (1.0 + v * (1.0 - g))
 
 
-def main_kernel(scale, grad, pre, inp, xfar, xnear, yfar, ynear, zfar, znear, band,
+def main_kernel(scale, grad, pre, inp, xfar, xnear, yfar, ynear, znear, zfar, band,
                 kept, sent, pre_out, fg, fa, fi, moved, picked, evens, odds, columns, many, left, left_f, grads_one, grads_two, held, zlo, zhi):
     wide, acts, inputs = fields_of(grad, pre, inp, *below_above("gx", xfar, xnear))
     ylo, yhi = below_above("gy", yfar, ynear)
@@ -426,7 +426,7 @@
             ((128, DEPTH), F32), ((128, DEPTH), F32), ((MANY, 128), F32), side, side,
         ],
         2 * 900 * 1000 * 1000, 8000000,
-        *fields, yfar, ynear, zfar, znear, band_two,
+        *fields, yfar, ynear, znear, zfar, band_two,
         grant=32,
     )
     (input_grad,) = call(

time: 87.4 us -> 89.2 us (1.021)
  waiting for transfers between devices: 4.22 us -> 5.76 us
    ppermute x3, starting transfers between devices: 5.76 us -> 8.46 us  [swapped(): lax.ppermute(near, axis, [(i, i - step) for i, step in enumerate(steps)])]
    ppermute x3, starting transfers between devices: 24.5 us -> 21.8 us  [swapped(): lax.ppermute(far, axis, [(i, (i + step) % count) for i, step in enumerate...]
    ppermute x3, waiting for transfers between devices: 0.01 us -> 2.14 us  [swapped(): lax.ppermute(far, axis, [(i, (i + step) % count) for i, step in enumerate...]
where the time goes in v12:
time: 89.2 us; the launch traced here: 88.7 us
  blocking collectives  38.9 us (44%)
  starting transfers between devices  35.7 us (40%)
  Pallas kernels  7.58 us (8%)
  waiting for transfers between devices  5.76 us (6%)
    ppermute x3, starting transfers between devices, swapped(): lax.ppermute(far, axis, [(i, (i + step) % count) for i, step in enumerate...  21.8 us
    all_to_all x1, blocking collectives, reduced(): parts = lax.all_to_all(slots, 'gx', 0, 0, tiled=True)  17.5 us
    all_to_all x1, blocking collectives, reduced(): parts = lax.all_to_all(copies, 'gy', 0, 0, tiled=True)  11.6 us
    all_gather x1, blocking collectives, reduced(): parts = lax.all_gather(part, 'gz', axis=0)  9.77 us
    ppermute x3, starting transfers between devices, swapped(): lax.ppermute(near, axis, [(i, i - step) for i, step in enumerate(steps)])  8.46 us
    pallas_call x10, Pallas kernels, call(): pl.pallas_call(kernel, out_shape=[jax.ShapeDtypeStruct(shape, dtype) for...  7.58 us
    all_to_all x1, starting transfers between devices, body(): gathered = lax.all_to_all(copies, 'gx', 0, 0, tiled=True)  3.57 us
    ppermute x3, waiting for transfers between devices, swapped(): lax.ppermute(near, axis, [(i, i - step) for i, step in enumerate(steps)])  3.28 us
  transfers between devices with their start and end apart: 8, of which 3 were waited for; matrix products, arithmetic and copies ran while one was open for 0% of the time, Pallas kernels for 2%

profile of v12, /device:TPU:1, one launch (start us, length us, event | category | flops | bytes accessed | tf_op | source)
XLA Modules:
  0.0 88.7 jit_solution(8837439738892342385)
XLA Ops:
  0.6 1.8 %shard_map.85 = (bf16[4,8,1024]{2,1,0:T(8,128)(2,1)S(1)}, bf16[4,8,1024]{2,1,0:T(8,128)(2,1)S(1)}, bf16[4,8,1024]{2,1,0:T(8,128)(2,1)S(1)}, bf16[4,8,1024]{2,1,0...) custom-call(bf16[4,8,1024]{2,1,0:T(8,128)(2,1)} %skip_in.1, ...), custom_call_target="tpu_custom_call" | custom-call | flops 100000 | bytes 400000 | tf_op jit(solution)/shard_map/pallas_call | solution.py:27
  2.4 12.4 %collective-permute-start = (bf16[4,8,1024]{2,1,0:T(8,128)(2,1)S(1)}, bf16[4,8,1024]{2,1,0:T(8,128)(2,1)S(1)}, u32[]{:S(2)}, u32[]{:S(2)}) collective-permute-start(bf16[4,8,1024]{2,1,0:T(8,128)(2,1)S(1)} %get-tuple-element.25), channel_id=1, source_target_pairs={{0,480},{32,64},{64,32},{96,128},{128,96},{160,192},{192,160},{224... | collective-permute-start | bytes 196616 | tf_op jit(solution)/shard_map/ppermute | solution.py:336
  14.9 1.9 %collective-permute-start.1 = (bf16[4,8,1024]{2,1,0:T(8,128)(2,1)S(1)}, bf16[4,8,1024]{2,1,0:T(8,128)(2,1)S(1)}, u32[]{:S(2)}, u32[]{:S(2)}) collective-permute-start(bf16[4,8,1024]{2,1,0:T(8,128)(2,1)S(1)} %get-tuple-element.26), channel_id=1, source_target_pairs={{0,32},{32,0},{64,96},{96,64},{128,160},{160,128},{192,224},{224,1... | collective-permute-start | bytes 196616 | tf_op jit(solution)/shard_map/ppermute | solution.py:337
  16.8 3.6 %all-to-all-start = ((bf16[16,8,1728]{2,1,0:T(8,128)(2,1)}), bf16[16,8,1728]{2,1,0:T(8,128)(2,1)S(1)}, u32[]{:S(2)}, u32[]{:S(2)}) async-start(bf16[16,8,1728]{2,1,0:T(8,128)(2,1)} %get-tuple-element.31), calls=%async_computation | async-start | bytes 917504 | tf_op jit(solution)/shard_map/all_to_all | solution.py:409
  20.4 0.0 collective-permute-done.1.xnear
  20.4 0.2 shard_map.86
  20.6 5.1 %collective-permute-start.2 = (bf16[14,2,1024]{2,1,0:T(2,128)(2,1)S(1)}, bf16[14,2,1024]{2,1,0:T(2,128)(2,1)S(1)}, u32[]{:S(2)}, u32[]{:S(2)}) collective-permute-start(bf16[14,2,1024]{2,1,0:T(2,128)(2,1)S(1)} %get-tuple-element.27), channel_id=1, source_target_pairs={{0,28},{4,8},{8,4},{12,16},{16,12},{20,24},{24,20},{28,0},{1,29},{... | collective-permute-start | bytes 172040 | tf_op jit(solution)/shard_map/ppermute | solution.py:336
  25.7 1.9 %collective-permute-start.3 = (bf16[14,2,1024]{2,1,0:T(2,128)(2,1)S(1)}, bf16[14,2,1024]{2,1,0:T(2,128)(2,1)S(1)}, u32[]{:S(2)}, u32[]{:S(2)}) collective-permute-start(bf16[14,2,1024]{2,1,0:T(2,128)(2,1)S(1)} %get-tuple-element.28), channel_id=1, source_target_pairs={{0,4},{4,0},{8,12},{12,8},{16,20},{20,16},{24,28},{28,24},{1,5},{5... | collective-permute-start | bytes 172040 | tf_op jit(solution)/shard_map/ppermute | solution.py:337
  27.7 3.3 %collective-permute-done.3.ynear = bf16[14,2,1024]{2,1,0:T(2,128)(2,1)S(1)} collective-permute-done((bf16[14,2,1024]{2,1,0:T(2,128)(2,1)S(1)}, bf16[14,2,1024]{2,1,0:T(2,128)(2,1)S(1)}, u32[]{:S(2)}, u32[]{:S(2)}) %collective-permute-start.3) | collective-permute-done | bytes 57376 | tf_op jit(solution)/shard_map/ppermute | solution.py:337
  30.9 0.1 shard_map.87
  31.1 4.6 %collective-permute-start.4 = (bf16[168,128]{1,0:T(8,128)(2,1)S(1)}, bf16[168,128]{1,0:T(8,128)(2,1)S(1)}, u32[]{:S(2)}, u32[]{:S(2)}) collective-permute-start(bf16[168,128]{1,0:T(8,128)(2,1)S(1)} %get-tuple-element.29), channel_id=1, source_target_pairs={{0,1},{1,0},{2,3},{3,2},{4,5},{5,4},{6,7},{7,6},{8,9},{9,8},{10,11... | collective-permute-start | bytes 129032 | tf_op jit(solution)/shard_map/ppermute | solution.py:337
  35.7 4.3 %collective-permute-start.5 = (bf16[168,128]{1,0:T(8,128)(2,1)S(1)}, bf16[168,128]{1,0:T(8,128)(2,1)S(1)}, u32[]{:S(2)}, u32[]{:S(2)}) collective-permute-start(bf16[168,128]{1,0:T(8,128)(2,1)S(1)} %get-tuple-element.30), channel_id=1, source_target_pairs={{0,3},{1,2},{2,1},{3,0},{4,7},{5,6},{6,5},{7,4},{8,11},{9,10},{10,... | collective-permute-start | bytes 129032 | tf_op jit(solution)/shard_map/ppermute | solution.py:336
  40.0 0.4 shard_map.88
  40.4 0.0 collective-permute-done.4.znear
  40.4 2.1 %collective-permute-done.5.zfar = bf16[168,128]{1,0:T(8,128)(2,1)S(1)} collective-permute-done((bf16[168,128]{1,0:T(8,128)(2,1)S(1)}, bf16[168,128]{1,0:T(8,128)(2,1)S(1)}, u32[]{:S(2)}, u32[]{:S(2)}) %collective-permute-start.5) | collective-permute-done | bytes 43040 | tf_op jit(solution)/shard_map/ppermute | solution.py:336
  42.5 3.1 %shard_map.89 = (f32[16,4,1728]{2,1,0:T(4,128)S(1)}, bf16[16,4,1728]{2,1,0:T(4,128)(2,1)S(1)}, bf16[144,1408]{1,0:T(8,128)(2,1)S(1)}) custom-call(bf16[4,8,1024]{2,1,0:T(8,128)(2,1)S(1)} %get-tuple-element.22.grad, bf16[4,8,1024]{2,1,0:T(8,128)(2,1)S(1)} %get-tuple-element.23.pre, bf16[4,8,1024]{2,1,0:T(8,128)(2,1)S(1)} %get-tuple-element.24.inp, ...), custom_call_target="tpu_custom_call" | custom-call | flops 1800000000 | bytes 8000000 | tf_op jit(solution)/shard_map/pallas_call | solution.py:27
  45.7 1.9 %collective-permute-start.6 = (bf16[16,4,1728]{2,1,0:T(4,128)(2,1)S(1)}, bf16[16,4,1728]{2,1,0:T(4,128)(2,1)S(1)}, u32[]{:S(2)}, u32[]{:S(2)}) collective-permute-start(bf16[16,4,1728]{2,1,0:T(4,128)(2,1)S(1)} %get-tuple-element.33), channel_id=1, source_target_pairs={{0,1},{1,0},{2,3},{3,2},{4,5},{5,4},{6,7},{7,6},{8,9},{9,8},{10,11... | collective-permute-start | bytes 663560 | tf_op jit(solution)/shard_map/ppermute | solution.py:369
  47.6 1.1 %shard_map.90 = bf16[4,8,1024]{2,1,0:T(8,128)(2,1)} custom-call(bf16[144,1408]{1,0:T(8,128)(2,1)S(1)} %get-tuple-element.34.pre_grad, bf16[4,8,1024]{2,1,0:T(8,128)(2,1)S(1)} %get-tuple-element.22.grad, bf16[2304,128]{1,0:T(8,128)(2,1)S(1)} %get-tuple-element.35.band), custom_call_target="tpu_custom_call" | custom-call | flops 500000000 | bytes 4000000 | tf_op jit(solution)/shard_map/pallas_call | solution.py:27
  48.7 0.3 collective-permute-done.6.came
  49.0 0.1 shard_map.91
  49.1 17.5 %all_to_all.15.parts = bf16[16,4,1728]{2,1,0:T(4,128)(2,1)S(1)} all-to-all(bf16[16,4,1728]{2,1,0:T(4,128)(2,1)S(1)} %shard_map.91), channel_id=1, replica_groups=mesh['gx'=16,'gy'=8,'gz'=4] {'gx'}, dimensions={0} | all-to-all | bytes 442368 | tf_op jit(solution)/shard_map/all_to_all | solution.py:372
  66.7 11.6 %all_to_all.16.parts = bf16[8,4,1728]{2,1,0:T(4,128)(2,1)S(1)} all-to-all(bf16[8,4,1728]{2,1,0:T(4,128)(2,1)S(1)} %shard_map.92), channel_id=1, replica_groups=mesh['gx'=16,'gy'=8,'gz'=4] {'gy'}, dimensions={0} | all-to-all | bytes 221184 | tf_op jit(solution)/shard_map/all_to_all | solution.py:374
  78.3 9.8 %all-gather.1.parts = f32[4,4,1728]{2,1,0:T(4,128)S(1)} all-gather(f32[1,4,1728]{2,1,0:T(4,128)S(1)} %bitcast.1), channel_id=2, replica_groups=mesh['gx'=16,'gy'=8,'gz'=4] {'gz'}, dimensions={0}, use_global_device_ids=true | all-gather | bytes 138240 | tf_op jit(solution)/shard_map/all_gather | solution.py:376
  88.1 0.6 shard_map.94
  (5 shorter events, 0.1 us)
Async XLA Ops:
  2.4 17.9 %collective-permute-start = (bf16[4,8,1024]{2,1,0:T(8,128)(2,1)S(1)}, bf16[4,8,1024]{2,1,0:T(8,128)(2,1)S(1)}, u32[]{:S(2)}, u32[]{:S(2)}) collective-permute-start(bf16[4,8,1024]{2,1,0:T(8,128)(2,1)S(1)} %get-tuple-element.25), channel_id=1, source_target_pairs={{0,480},{32,64},{64,32},{96,128},{128,96},{160,192},{192,160},{224... | collective-permute-start | bytes 196616 | tf_op jit(solution)/shard_map/ppermute | solution.py:336
  14.9 5.5 %collective-permute-start.1 = (bf16[4,8,1024]{2,1,0:T(8,128)(2,1)S(1)}, bf16[4,8,1024]{2,1,0:T(8,128)(2,1)S(1)}, u32[]{:S(2)}, u32[]{:S(2)}) collective-permute-start(bf16[4,8,1024]{2,1,0:T(8,128)(2,1)S(1)} %get-tuple-element.26), channel_id=1, source_target_pairs={{0,32},{32,0},{64,96},{96,64},{128,160},{160,128},{192,224},{224,1... | collective-permute-start | bytes 196616 | tf_op jit(solution)/shard_map/ppermute | solution.py:337
  16.8 23.2 %all-to-all-start = ((bf16[16,8,1728]{2,1,0:T(8,128)(2,1)}), bf16[16,8,1728]{2,1,0:T(8,128)(2,1)S(1)}, u32[]{:S(2)}, u32[]{:S(2)}) async-start(bf16[16,8,1728]{2,1,0:T(8,128)(2,1)} %get-tuple-element.31), calls=%async_computation | async-start | bytes 917504 | tf_op jit(solution)/shard_map/all_to_all | solution.py:409
  20.6 7.0 %collective-permute-start.2 = (bf16[14,2,1024]{2,1,0:T(2,128)(2,1)S(1)}, bf16[14,2,1024]{2,1,0:T(2,128)(2,1)S(1)}, u32[]{:S(2)}, u32[]{:S(2)}) collective-permute-start(bf16[14,2,1024]{2,1,0:T(2,128)(2,1)S(1)} %get-tuple-element.27), channel_id=1, source_target_pairs={{0,28},{4,8},{8,4},{12,16},{16,12},{20,24},{24,20},{28,0},{1,29},{... | collective-permute-start | bytes 172040 | tf_op jit(solution)/shard_map/ppermute | solution.py:336
  25.7 5.2 %collective-permute-start.3 = (bf16[14,2,1024]{2,1,0:T(2,128)(2,1)S(1)}, bf16[14,2,1024]{2,1,0:T(2,128)(2,1)S(1)}, u32[]{:S(2)}, u32[]{:S(2)}) collective-permute-start(bf16[14,2,1024]{2,1,0:T(2,128)(2,1)S(1)} %get-tuple-element.28), channel_id=1, source_target_pairs={{0,4},{4,0},{8,12},{12,8},{16,20},{20,16},{24,28},{28,24},{1,5},{5... | collective-permute-start | bytes 172040 | tf_op jit(solution)/shard_map/ppermute | solution.py:337
  31.1 9.3 %collective-permute-start.4 = (bf16[168,128]{1,0:T(8,128)(2,1)S(1)}, bf16[168,128]{1,0:T(8,128)(2,1)S(1)}, u32[]{:S(2)}, u32[]{:S(2)}) collective-permute-start(bf16[168,128]{1,0:T(8,128)(2,1)S(1)} %get-tuple-element.29), channel_id=1, source_target_pairs={{0,1},{1,0},{2,3},{3,2},{4,5},{5,4},{6,7},{7,6},{8,9},{9,8},{10,11... | collective-permute-start | bytes 129032 | tf_op jit(solution)/shard_map/ppermute | solution.py:337
  35.7 6.8 %collective-permute-start.5 = (bf16[168,128]{1,0:T(8,128)(2,1)S(1)}, bf16[168,128]{1,0:T(8,128)(2,1)S(1)}, u32[]{:S(2)}, u32[]{:S(2)}) collective-permute-start(bf16[168,128]{1,0:T(8,128)(2,1)S(1)} %get-tuple-element.30), channel_id=1, source_target_pairs={{0,3},{1,2},{2,1},{3,0},{4,7},{5,6},{6,5},{7,4},{8,11},{9,10},{10,... | collective-permute-start | bytes 129032 | tf_op jit(solution)/shard_map/ppermute | solution.py:336
  45.7 3.4 %collective-permute-start.6 = (bf16[16,4,1728]{2,1,0:T(4,128)(2,1)S(1)}, bf16[16,4,1728]{2,1,0:T(4,128)(2,1)S(1)}, u32[]{:S(2)}, u32[]{:S(2)}) collective-permute-start(bf16[16,4,1728]{2,1,0:T(4,128)(2,1)S(1)} %get-tuple-element.33), channel_id=1, source_target_pairs={{0,1},{1,0},{2,3},{3,2},{4,5},{5,4},{6,7},{7,6},{8,9},{9,8},{10,11... | collective-permute-start | bytes 663560 | tf_op jit(solution)/shard_map/ppermute | solution.py:369

commit v13 on v11

--- a/solution.py
+++ b/solution.py
@@ -372,8 +372,8 @@
     parts = lax.all_to_all(slots, "gx", 0, 0, tiled=True)
     (copies,) = call(total_kernel, [((gy, rows, columns), B16)], [], 1000, 500000, parts)
     parts = lax.all_to_all(copies, "gy", 0, 0, tiled=True)
-    (part,) = call(total_kernel, [((rows, columns), F32)], [], 1000, 500000, parts)
-    parts = lax.all_gather(part, "gz", axis=0)
+    (copies,) = call(total_kernel, [((gz, rows, columns), F32)], [], 1000, 500000, parts)
+    parts = lax.all_to_all(copies, "gz", 0, 0, tiled=True)
     grads = ((rows, columns), F32)
     one, two = call(last_total_kernel, [grads, grads], [], 1000, 500000, parts)
     return other, one, two

time: 87.4 us -> 89.2 us (1.021)
  blocking collectives: 38.4 us -> 40.2 us
    all_to_all x0 -> x1, blocking collectives: none -> 11.6 us  [reduced(): parts = lax.all_to_all(copies, 'gz', 0, 0, tiled=True)]
    all_gather x1 -> x0, blocking collectives: 9.77 us -> none  [reduced(): parts = lax.all_gather(part, 'gz', axis=0)]
where the time goes in v13:
time: 89.2 us; the launch traced here: 88.7 us
  blocking collectives  40.2 us (45%)
  starting transfers between devices  35.9 us (40%)
  Pallas kernels  7.57 us (8%)
  waiting for transfers between devices  4.22 us (5%)
    ppermute x3, starting transfers between devices, swapped(): lax.ppermute(far, axis, [(i, (i + step) % count) for i, step in enumerate...  24.5 us
    all_to_all x1, blocking collectives, reduced(): parts = lax.all_to_all(slots, 'gx', 0, 0, tiled=True)  17.1 us
    all_to_all x1, blocking collectives, reduced(): parts = lax.all_to_all(copies, 'gy', 0, 0, tiled=True)  11.6 us
    all_to_all x1, blocking collectives, reduced(): parts = lax.all_to_all(copies, 'gz', 0, 0, tiled=True)  11.6 us
    pallas_call x10, Pallas kernels, call(): pl.pallas_call(kernel, out_shape=[jax.ShapeDtypeStruct(shape, dtype) for...  7.57 us
    ppermute x3, starting transfers between devices, swapped(): lax.ppermute(near, axis, [(i, i - step) for i, step in enumerate(steps)])  5.76 us
    ppermute x3, waiting for transfers between devices, swapped(): lax.ppermute(near, axis, [(i, i - step) for i, step in enumerate(steps)])  4.02 us
    all_to_all x1, starting transfers between devices, body(): gathered = lax.all_to_all(copies, 'gx', 0, 0, tiled=True)  3.57 us
  transfers between devices with their start and end apart: 8, of which 3 were waited for; matrix products, arithmetic and copies ran while one was open for 0% of the time, Pallas kernels for 2%

profile of v13, /device:TPU:1, one launch (start us, length us, event | category | flops | bytes accessed | tf_op | source)
XLA Modules:
  0.0 88.7 jit_solution(9016511555993161697)
XLA Ops:
  0.6 1.8 %shard_map.85 = (bf16[4,8,1024]{2,1,0:T(8,128)(2,1)S(1)}, bf16[4,8,1024]{2,1,0:T(8,128)(2,1)S(1)}, bf16[4,8,1024]{2,1,0:T(8,128)(2,1)S(1)}, bf16[4,8,1024]{2,1,0...) custom-call(bf16[4,8,1024]{2,1,0:T(8,128)(2,1)} %skip_in.1, ...), custom_call_target="tpu_custom_call" | custom-call | flops 100000 | bytes 400000 | tf_op jit(solution)/shard_map/pallas_call | solution.py:27
  2.4 12.4 %collective-permute-start = (bf16[4,8,1024]{2,1,0:T(8,128)(2,1)S(1)}, bf16[4,8,1024]{2,1,0:T(8,128)(2,1)S(1)}, u32[]{:S(2)}, u32[]{:S(2)}) collective-permute-start(bf16[4,8,1024]{2,1,0:T(8,128)(2,1)S(1)} %get-tuple-element.25), channel_id=1, source_target_pairs={{0,480},{32,64},{64,32},{96,128},{128,96},{160,192},{192,160},{224... | collective-permute-start | bytes 196616 | tf_op jit(solution)/shard_map/ppermute | solution.py:336
  14.9 1.9 %collective-permute-start.1 = (bf16[4,8,1024]{2,1,0:T(8,128)(2,1)S(1)}, bf16[4,8,1024]{2,1,0:T(8,128)(2,1)S(1)}, u32[]{:S(2)}, u32[]{:S(2)}) collective-permute-start(bf16[4,8,1024]{2,1,0:T(8,128)(2,1)S(1)} %get-tuple-element.26), channel_id=1, source_target_pairs={{0,32},{32,0},{64,96},{96,64},{128,160},{160,128},{192,224},{224,1... | collective-permute-start | bytes 196616 | tf_op jit(solution)/shard_map/ppermute | solution.py:337
  16.8 3.6 %all-to-all-start = ((bf16[16,8,1728]{2,1,0:T(8,128)(2,1)}), bf16[16,8,1728]{2,1,0:T(8,128)(2,1)S(1)}, u32[]{:S(2)}, u32[]{:S(2)}) async-start(bf16[16,8,1728]{2,1,0:T(8,128)(2,1)} %get-tuple-element.31), calls=%async_computation | async-start | bytes 917504 | tf_op jit(solution)/shard_map/all_to_all | solution.py:409
  20.4 0.0 collective-permute-done.1.xnear
  20.4 0.2 shard_map.86
  20.6 5.1 %collective-permute-start.2 = (bf16[14,2,1024]{2,1,0:T(2,128)(2,1)S(1)}, bf16[14,2,1024]{2,1,0:T(2,128)(2,1)S(1)}, u32[]{:S(2)}, u32[]{:S(2)}) collective-permute-start(bf16[14,2,1024]{2,1,0:T(2,128)(2,1)S(1)} %get-tuple-element.27), channel_id=1, source_target_pairs={{0,28},{4,8},{8,4},{12,16},{16,12},{20,24},{24,20},{28,0},{1,29},{... | collective-permute-start | bytes 172040 | tf_op jit(solution)/shard_map/ppermute | solution.py:336
  25.7 1.9 %collective-permute-start.3 = (bf16[14,2,1024]{2,1,0:T(2,128)(2,1)S(1)}, bf16[14,2,1024]{2,1,0:T(2,128)(2,1)S(1)}, u32[]{:S(2)}, u32[]{:S(2)}) collective-permute-start(bf16[14,2,1024]{2,1,0:T(2,128)(2,1)S(1)} %get-tuple-element.28), channel_id=1, source_target_pairs={{0,4},{4,0},{8,12},{12,8},{16,20},{20,16},{24,28},{28,24},{1,5},{5... | collective-permute-start | bytes 172040 | tf_op jit(solution)/shard_map/ppermute | solution.py:337
  27.7 3.3 %collective-permute-done.3.ynear = bf16[14,2,1024]{2,1,0:T(2,128)(2,1)S(1)} collective-permute-done((bf16[14,2,1024]{2,1,0:T(2,128)(2,1)S(1)}, bf16[14,2,1024]{2,1,0:T(2,128)(2,1)S(1)}, u32[]{:S(2)}, u32[]{:S(2)}) %collective-permute-start.3) | collective-permute-done | bytes 57376 | tf_op jit(solution)/shard_map/ppermute | solution.py:337
  30.9 0.1 shard_map.87
  31.1 7.0 %collective-permute-start.4 = (bf16[168,128]{1,0:T(8,128)(2,1)S(1)}, bf16[168,128]{1,0:T(8,128)(2,1)S(1)}, u32[]{:S(2)}, u32[]{:S(2)}) collective-permute-start(bf16[168,128]{1,0:T(8,128)(2,1)S(1)} %get-tuple-element.29), channel_id=1, source_target_pairs={{0,3},{1,2},{2,1},{3,0},{4,7},{5,6},{6,5},{7,4},{8,11},{9,10},{10,... | collective-permute-start | bytes 129032 | tf_op jit(solution)/shard_map/ppermute | solution.py:336
  38.0 1.9 %collective-permute-start.5 = (bf16[168,128]{1,0:T(8,128)(2,1)S(1)}, bf16[168,128]{1,0:T(8,128)(2,1)S(1)}, u32[]{:S(2)}, u32[]{:S(2)}) collective-permute-start(bf16[168,128]{1,0:T(8,128)(2,1)S(1)} %get-tuple-element.30), channel_id=1, source_target_pairs={{0,1},{1,0},{2,3},{3,2},{4,5},{5,4},{6,7},{7,6},{8,9},{9,8},{10,11... | collective-permute-start | bytes 129032 | tf_op jit(solution)/shard_map/ppermute | solution.py:337
  40.0 0.4 shard_map.88
  40.4 0.0 collective-permute-done.4.zfar
  40.4 0.7 collective-permute-done.5.znear
  41.2 3.1 %shard_map.89 = (f32[16,4,1728]{2,1,0:T(4,128)S(1)}, bf16[16,4,1728]{2,1,0:T(4,128)(2,1)S(1)}, bf16[144,1408]{1,0:T(8,128)(2,1)S(1)}) custom-call(bf16[4,8,1024]{2,1,0:T(8,128)(2,1)S(1)} %get-tuple-element.22.grad, bf16[4,8,1024]{2,1,0:T(8,128)(2,1)S(1)} %get-tuple-element.23.pre, bf16[4,8,1024]{2,1,0:T(8,128)(2,1)S(1)} %get-tuple-element.24.inp, ...), custom_call_target="tpu_custom_call" | custom-call | flops 1800000000 | bytes 8000000 | tf_op jit(solution)/shard_map/pallas_call | solution.py:27
  44.3 2.1 %collective-permute-start.6 = (bf16[16,4,1728]{2,1,0:T(4,128)(2,1)S(1)}, bf16[16,4,1728]{2,1,0:T(4,128)(2,1)S(1)}, u32[]{:S(2)}, u32[]{:S(2)}) collective-permute-start(bf16[16,4,1728]{2,1,0:T(4,128)(2,1)S(1)} %get-tuple-element.33), channel_id=1, source_target_pairs={{0,1},{1,0},{2,3},{3,2},{4,5},{5,4},{6,7},{7,6},{8,9},{9,8},{10,11... | collective-permute-start | bytes 663560 | tf_op jit(solution)/shard_map/ppermute | solution.py:369
  46.3 1.1 %shard_map.90 = bf16[4,8,1024]{2,1,0:T(8,128)(2,1)} custom-call(bf16[144,1408]{1,0:T(8,128)(2,1)S(1)} %get-tuple-element.34.pre_grad, bf16[4,8,1024]{2,1,0:T(8,128)(2,1)S(1)} %get-tuple-element.22.grad, bf16[2304,128]{1,0:T(8,128)(2,1)S(1)} %get-tuple-element.35.band), custom_call_target="tpu_custom_call" | custom-call | flops 500000000 | bytes 4000000 | tf_op jit(solution)/shard_map/pallas_call | solution.py:27
  47.5 0.2 collective-permute-done.6.came
  47.6 0.1 shard_map.91
  47.7 17.1 %all_to_all.20.parts = bf16[16,4,1728]{2,1,0:T(4,128)(2,1)S(1)} all-to-all(bf16[16,4,1728]{2,1,0:T(4,128)(2,1)S(1)} %shard_map.91), channel_id=1, replica_groups=mesh['gx'=16,'gy'=8,'gz'=4] {'gx'}, dimensions={0} | all-to-all | bytes 442368 | tf_op jit(solution)/shard_map/all_to_all | solution.py:372
  64.9 11.6 %all_to_all.21.parts = bf16[8,4,1728]{2,1,0:T(4,128)(2,1)S(1)} all-to-all(bf16[8,4,1728]{2,1,0:T(4,128)(2,1)S(1)} %shard_map.92), channel_id=1, replica_groups=mesh['gx'=16,'gy'=8,'gz'=4] {'gy'}, dimensions={0} | all-to-all | bytes 221184 | tf_op jit(solution)/shard_map/all_to_all | solution.py:374
  76.5 11.6 %all_to_all.22.parts = f32[4,4,1728]{2,1,0:T(4,128)S(1)} all-to-all(f32[4,4,1728]{2,1,0:T(4,128)S(1)} %shard_map.93), channel_id=1, replica_groups=mesh['gx'=16,'gy'=8,'gz'=4] {'gz'}, dimensions={0} | all-to-all | bytes 221184 | tf_op jit(solution)/shard_map/all_to_all | solution.py:376
  88.0 0.6 shard_map.94
  (5 shorter events, 0.1 us)
Async XLA Ops:
  2.4 17.9 %collective-permute-start = (bf16[4,8,1024]{2,1,0:T(8,128)(2,1)S(1)}, bf16[4,8,1024]{2,1,0:T(8,128)(2,1)S(1)}, u32[]{:S(2)}, u32[]{:S(2)}) collective-permute-start(bf16[4,8,1024]{2,1,0:T(8,128)(2,1)S(1)} %get-tuple-element.25), channel_id=1, source_target_pairs={{0,480},{32,64},{64,32},{96,128},{128,96},{160,192},{192,160},{224... | collective-permute-start | bytes 196616 | tf_op jit(solution)/shard_map/ppermute | solution.py:336
  14.9 5.5 %collective-permute-start.1 = (bf16[4,8,1024]{2,1,0:T(8,128)(2,1)S(1)}, bf16[4,8,1024]{2,1,0:T(8,128)(2,1)S(1)}, u32[]{:S(2)}, u32[]{:S(2)}) collective-permute-start(bf16[4,8,1024]{2,1,0:T(8,128)(2,1)S(1)} %get-tuple-element.26), channel_id=1, source_target_pairs={{0,32},{32,0},{64,96},{96,64},{128,160},{160,128},{192,224},{224,1... | collective-permute-start | bytes 196616 | tf_op jit(solution)/shard_map/ppermute | solution.py:337
  16.8 23.2 %all-to-all-start = ((bf16[16,8,1728]{2,1,0:T(8,128)(2,1)}), bf16[16,8,1728]{2,1,0:T(8,128)(2,1)S(1)}, u32[]{:S(2)}, u32[]{:S(2)}) async-start(bf16[16,8,1728]{2,1,0:T(8,128)(2,1)} %get-tuple-element.31), calls=%async_computation | async-start | bytes 917504 | tf_op jit(solution)/shard_map/all_to_all | solution.py:409
  20.6 7.0 %collective-permute-start.2 = (bf16[14,2,1024]{2,1,0:T(2,128)(2,1)S(1)}, bf16[14,2,1024]{2,1,0:T(2,128)(2,1)S(1)}, u32[]{:S(2)}, u32[]{:S(2)}) collective-permute-start(bf16[14,2,1024]{2,1,0:T(2,128)(2,1)S(1)} %get-tuple-element.27), channel_id=1, source_target_pairs={{0,28},{4,8},{8,4},{12,16},{16,12},{20,24},{24,20},{28,0},{1,29},{... | collective-permute-start | bytes 172040 | tf_op jit(solution)/shard_map/ppermute | solution.py:336
  25.7 5.2 %collective-permute-start.3 = (bf16[14,2,1024]{2,1,0:T(2,128)(2,1)S(1)}, bf16[14,2,1024]{2,1,0:T(2,128)(2,1)S(1)}, u32[]{:S(2)}, u32[]{:S(2)}) collective-permute-start(bf16[14,2,1024]{2,1,0:T(2,128)(2,1)S(1)} %get-tuple-element.28), channel_id=1, source_target_pairs={{0,4},{4,0},{8,12},{12,8},{16,20},{20,16},{24,28},{28,24},{1,5},{5... | collective-permute-start | bytes 172040 | tf_op jit(solution)/shard_map/ppermute | solution.py:337
  31.1 9.3 %collective-permute-start.4 = (bf16[168,128]{1,0:T(8,128)(2,1)S(1)}, bf16[168,128]{1,0:T(8,128)(2,1)S(1)}, u32[]{:S(2)}, u32[]{:S(2)}) collective-permute-start(bf16[168,128]{1,0:T(8,128)(2,1)S(1)} %get-tuple-element.29), channel_id=1, source_target_pairs={{0,3},{1,2},{2,1},{3,0},{4,7},{5,6},{6,5},{7,4},{8,11},{9,10},{10,... | collective-permute-start | bytes 129032 | tf_op jit(solution)/shard_map/ppermute | solution.py:336
  38.0 3.1 %collective-permute-start.5 = (bf16[168,128]{1,0:T(8,128)(2,1)S(1)}, bf16[168,128]{1,0:T(8,128)(2,1)S(1)}, u32[]{:S(2)}, u32[]{:S(2)}) collective-permute-start(bf16[168,128]{1,0:T(8,128)(2,1)S(1)} %get-tuple-element.30), channel_id=1, source_target_pairs={{0,1},{1,0},{2,3},{3,2},{4,5},{5,4},{6,7},{7,6},{8,9},{9,8},{10,11... | collective-permute-start | bytes 129032 | tf_op jit(solution)/shard_map/ppermute | solution.py:337
  44.3 3.4 %collective-permute-start.6 = (bf16[16,4,1728]{2,1,0:T(4,128)(2,1)S(1)}, bf16[16,4,1728]{2,1,0:T(4,128)(2,1)S(1)}, u32[]{:S(2)}, u32[]{:S(2)}) collective-permute-start(bf16[16,4,1728]{2,1,0:T(4,128)(2,1)S(1)} %get-tuple-element.33), channel_id=1, source_target_pairs={{0,1},{1,0},{2,3},{3,2},{4,5},{5,4},{6,7},{7,6},{8,9},{9,8},{10,11... | collective-permute-start | bytes 663560 | tf_op jit(solution)/shard_map/ppermute | solution.py:369

commit v14 on v11

--- a/solution.py
+++ b/solution.py
@@ -104,7 +104,7 @@
     )
 
 
-def ypack_kernel(grad, pre, inp, xfar, xnear, far, near, held):
+def ypack_kernel(grad, pre, inp, xnear, xfar, far, near, held):
     wide, acts, inputs = fields_of(grad, pre, inp, *below_above("gx", xfar, xnear))
     for at, (ref, x) in enumerate(wide):
         value = ref[x].astype(F32)
@@ -116,7 +116,7 @@
         far[8 + at], near[8 + at] = far_near("gy", held[0:2], held[2:4])
 
 
-def zpack_kernel(grad, pre, inp, xfar, xnear, yfar, ynear, far, near, low, high):
+def zpack_kernel(grad, pre, inp, xnear, xfar, yfar, ynear, far, near, low, high):
     wide, acts, inputs = fields_of(grad, pre, inp, *below_above("gx", xfar, xnear))
     ylo, yhi = below_above("gy", yfar, ynear)
     for held, lane, half in ((low, 0, True), (high, LANES - 128, False)):
@@ -228,7 +228,7 @@
     return g * (1.0 + v * (1.0 - g))
 
 
-def main_kernel(scale, grad, pre, inp, xfar, xnear, yfar, ynear, zfar, znear, band,
+def main_kernel(scale, grad, pre, inp, xnear, xfar, yfar, ynear, zfar, znear, band,
                 kept, sent, pre_out, fg, fa, fi, moved, picked, evens, odds, columns, many, left, left_f, grads_one, grads_two, held, zlo, zhi):
     wide, acts, inputs = fields_of(grad, pre, inp, *below_above("gx", xfar, xnear))
     ylo, yhi = below_above("gy", yfar, ynear)
@@ -400,7 +400,7 @@
         space=pltpu.HBM,
     )
     xfar, xnear = swapped(far, near, "gx")
-    fields = (grad, pre, inp, xfar, xnear)
+    fields = (grad, pre, inp, xnear, xfar)
     message = ((LAYERS, 2, LANES), B16)
     yfar, ynear = swapped(
         *call(ypack_kernel, [message, message], [((4, LANES), F32)], 60000000000, 600000, *fields), "gy"

time: 87.4 us -> 88 us (level)
    ppermute x3, starting transfers between devices: 5.76 us -> 7.79 us  [swapped(): lax.ppermute(near, axis, [(i, i - step) for i, step in enumerate(steps)])]
    ppermute x3, starting transfers between devices: 24.5 us -> 22.6 us  [swapped(): lax.ppermute(far, axis, [(i, (i + step) % count) for i, step in enumerate...]
where the time goes in v14:
time: 88 us; the launch traced here: 87.5 us
  blocking collectives  38.9 us (44%)
  starting transfers between devices  36.1 us (41%)
  Pallas kernels  7.57 us (9%)
  waiting for transfers between devices  4.22 us (5%)
    ppermute x3, starting transfers between devices, swapped(): lax.ppermute(far, axis, [(i, (i + step) % count) for i, step in enumerate...  22.6 us
    all_to_all x1, blocking collectives, reduced(): parts = lax.all_to_all(slots, 'gx', 0, 0, tiled=True)  17.5 us
    all_to_all x1, blocking collectives, reduced(): parts = lax.all_to_all(copies, 'gy', 0, 0, tiled=True)  11.6 us
    all_gather x1, blocking collectives, reduced(): parts = lax.all_gather(part, 'gz', axis=0)  9.77 us
    ppermute x3, starting transfers between devices, swapped(): lax.ppermute(near, axis, [(i, i - step) for i, step in enumerate(steps)])  7.79 us
    pallas_call x10, Pallas kernels, call(): pl.pallas_call(kernel, out_shape=[jax.ShapeDtypeStruct(shape, dtype) for...  7.57 us
    ppermute x3, waiting for transfers between devices, swapped(): lax.ppermute(near, axis, [(i, i - step) for i, step in enumerate(steps)])  4.02 us
    all_to_all x1, starting transfers between devices, body(): gathered = lax.all_to_all(copies, 'gx', 0, 0, tiled=True)  3.57 us
  transfers between devices with their start and end apart: 8, of which 3 were waited for; matrix products, arithmetic and copies ran while one was open for 0% of the time, Pallas kernels for 2%

profile of v14, /device:TPU:1, one launch (start us, length us, event | category | flops | bytes accessed | tf_op | source)
XLA Modules:
  0.0 87.5 jit_solution(11474489428070866776)
XLA Ops:
  0.6 1.8 %shard_map.85 = (bf16[4,8,1024]{2,1,0:T(8,128)(2,1)S(1)}, bf16[4,8,1024]{2,1,0:T(8,128)(2,1)S(1)}, bf16[4,8,1024]{2,1,0:T(8,128)(2,1)S(1)}, bf16[4,8,1024]{2,1,0...) custom-call(bf16[4,8,1024]{2,1,0:T(8,128)(2,1)} %skip_in.1, ...), custom_call_target="tpu_custom_call" | custom-call | flops 100000 | bytes 400000 | tf_op jit(solution)/shard_map/pallas_call | solution.py:27
  2.4 3.9 %collective-permute-start = (bf16[4,8,1024]{2,1,0:T(8,128)(2,1)S(1)}, bf16[4,8,1024]{2,1,0:T(8,128)(2,1)S(1)}, u32[]{:S(2)}, u32[]{:S(2)}) collective-permute-start(bf16[4,8,1024]{2,1,0:T(8,128)(2,1)S(1)} %get-tuple-element.25), channel_id=1, source_target_pairs={{0,32},{32,0},{64,96},{96,64},{128,160},{160,128},{192,224},{224,1... | collective-permute-start | bytes 196616 | tf_op jit(solution)/shard_map/ppermute | solution.py:337
  6.4 10.6 %collective-permute-start.1 = (bf16[4,8,1024]{2,1,0:T(8,128)(2,1)S(1)}, bf16[4,8,1024]{2,1,0:T(8,128)(2,1)S(1)}, u32[]{:S(2)}, u32[]{:S(2)}) collective-permute-start(bf16[4,8,1024]{2,1,0:T(8,128)(2,1)S(1)} %get-tuple-element.26), channel_id=1, source_target_pairs={{0,480},{32,64},{64,32},{96,128},{128,96},{160,192},{192,160},{224... | collective-permute-start | bytes 196616 | tf_op jit(solution)/shard_map/ppermute | solution.py:336
  17.0 3.6 %all-to-all-start = ((bf16[16,8,1728]{2,1,0:T(8,128)(2,1)}), bf16[16,8,1728]{2,1,0:T(8,128)(2,1)S(1)}, u32[]{:S(2)}, u32[]{:S(2)}) async-start(bf16[16,8,1728]{2,1,0:T(8,128)(2,1)} %get-tuple-element.31), calls=%async_computation | async-start | bytes 917504 | tf_op jit(solution)/shard_map/all_to_all | solution.py:409
  20.6 0.0 collective-permute-done.xnear
  20.6 0.0 collective-permute-done.1.xfar
  20.6 0.2 shard_map.86
  20.9 5.1 %collective-permute-start.2 = (bf16[14,2,1024]{2,1,0:T(2,128)(2,1)S(1)}, bf16[14,2,1024]{2,1,0:T(2,128)(2,1)S(1)}, u32[]{:S(2)}, u32[]{:S(2)}) collective-permute-start(bf16[14,2,1024]{2,1,0:T(2,128)(2,1)S(1)} %get-tuple-element.27), channel_id=1, source_target_pairs={{0,28},{4,8},{8,4},{12,16},{16,12},{20,24},{24,20},{28,0},{1,29},{... | collective-permute-start | bytes 172040 | tf_op jit(solution)/shard_map/ppermute | solution.py:336
  26.0 1.9 %collective-permute-start.3 = (bf16[14,2,1024]{2,1,0:T(2,128)(2,1)S(1)}, bf16[14,2,1024]{2,1,0:T(2,128)(2,1)S(1)}, u32[]{:S(2)}, u32[]{:S(2)}) collective-permute-start(bf16[14,2,1024]{2,1,0:T(2,128)(2,1)S(1)} %get-tuple-element.28), channel_id=1, source_target_pairs={{0,4},{4,0},{8,12},{12,8},{16,20},{20,16},{24,28},{28,24},{1,5},{5... | collective-permute-start | bytes 172040 | tf_op jit(solution)/shard_map/ppermute | solution.py:337
  27.9 3.3 %collective-permute-done.3.ynear = bf16[14,2,1024]{2,1,0:T(2,128)(2,1)S(1)} collective-permute-done((bf16[14,2,1024]{2,1,0:T(2,128)(2,1)S(1)}, bf16[14,2,1024]{2,1,0:T(2,128)(2,1)S(1)}, u32[]{:S(2)}, u32[]{:S(2)}) %collective-permute-start.3) | collective-permute-done | bytes 57376 | tf_op jit(solution)/shard_map/ppermute | solution.py:337
  31.2 0.1 shard_map.87
  31.3 6.9 %collective-permute-start.4 = (bf16[168,128]{1,0:T(8,128)(2,1)S(1)}, bf16[168,128]{1,0:T(8,128)(2,1)S(1)}, u32[]{:S(2)}, u32[]{:S(2)}) collective-permute-start(bf16[168,128]{1,0:T(8,128)(2,1)S(1)} %get-tuple-element.29), channel_id=1, source_target_pairs={{0,3},{1,2},{2,1},{3,0},{4,7},{5,6},{6,5},{7,4},{8,11},{9,10},{10,... | collective-permute-start | bytes 129032 | tf_op jit(solution)/shard_map/ppermute | solution.py:336
  38.2 1.9 %collective-permute-start.5 = (bf16[168,128]{1,0:T(8,128)(2,1)S(1)}, bf16[168,128]{1,0:T(8,128)(2,1)S(1)}, u32[]{:S(2)}, u32[]{:S(2)}) collective-permute-start(bf16[168,128]{1,0:T(8,128)(2,1)S(1)} %get-tuple-element.30), channel_id=1, source_target_pairs={{0,1},{1,0},{2,3},{3,2},{4,5},{5,4},{6,7},{7,6},{8,9},{9,8},{10,11... | collective-permute-start | bytes 129032 | tf_op jit(solution)/shard_map/ppermute | solution.py:337
  40.2 0.4 shard_map.88
  40.6 0.7 collective-permute-done.5.znear
  41.3 3.1 %shard_map.89 = (f32[16,4,1728]{2,1,0:T(4,128)S(1)}, bf16[16,4,1728]{2,1,0:T(4,128)(2,1)S(1)}, bf16[144,1408]{1,0:T(8,128)(2,1)S(1)}) custom-call(bf16[4,8,1024]{2,1,0:T(8,128)(2,1)S(1)} %get-tuple-element.22.grad, bf16[4,8,1024]{2,1,0:T(8,128)(2,1)S(1)} %get-tuple-element.23.pre, bf16[4,8,1024]{2,1,0:T(8,128)(2,1)S(1)} %get-tuple-element.24.inp, ...), custom_call_target="tpu_custom_call" | custom-call | flops 1800000000 | bytes 8000000 | tf_op jit(solution)/shard_map/pallas_call | solution.py:27
  44.5 2.1 %collective-permute-start.6 = (bf16[16,4,1728]{2,1,0:T(4,128)(2,1)S(1)}, bf16[16,4,1728]{2,1,0:T(4,128)(2,1)S(1)}, u32[]{:S(2)}, u32[]{:S(2)}) collective-permute-start(bf16[16,4,1728]{2,1,0:T(4,128)(2,1)S(1)} %get-tuple-element.33), channel_id=1, source_target_pairs={{0,1},{1,0},{2,3},{3,2},{4,5},{5,4},{6,7},{7,6},{8,9},{9,8},{10,11... | collective-permute-start | bytes 663560 | tf_op jit(solution)/shard_map/ppermute | solution.py:369
  46.5 1.1 %shard_map.90 = bf16[4,8,1024]{2,1,0:T(8,128)(2,1)} custom-call(bf16[144,1408]{1,0:T(8,128)(2,1)S(1)} %get-tuple-element.34.pre_grad, bf16[4,8,1024]{2,1,0:T(8,128)(2,1)S(1)} %get-tuple-element.22.grad, bf16[2304,128]{1,0:T(8,128)(2,1)S(1)} %get-tuple-element.35.band), custom_call_target="tpu_custom_call" | custom-call | flops 500000000 | bytes 4000000 | tf_op jit(solution)/shard_map/pallas_call | solution.py:27
  47.6 0.2 collective-permute-done.6.came
  47.8 0.1 shard_map.91
  47.9 17.5 %all_to_all.15.parts = bf16[16,4,1728]{2,1,0:T(4,128)(2,1)S(1)} all-to-all(bf16[16,4,1728]{2,1,0:T(4,128)(2,1)S(1)} %shard_map.91), channel_id=1, replica_groups=mesh['gx'=16,'gy'=8,'gz'=4] {'gx'}, dimensions={0} | all-to-all | bytes 442368 | tf_op jit(solution)/shard_map/all_to_all | solution.py:372
  65.5 11.6 %all_to_all.16.parts = bf16[8,4,1728]{2,1,0:T(4,128)(2,1)S(1)} all-to-all(bf16[8,4,1728]{2,1,0:T(4,128)(2,1)S(1)} %shard_map.92), channel_id=1, replica_groups=mesh['gx'=16,'gy'=8,'gz'=4] {'gy'}, dimensions={0} | all-to-all | bytes 221184 | tf_op jit(solution)/shard_map/all_to_all | solution.py:374
  77.1 9.8 %all-gather.1.parts = f32[4,4,1728]{2,1,0:T(4,128)S(1)} all-gather(f32[1,4,1728]{2,1,0:T(4,128)S(1)} %bitcast.1), channel_id=2, replica_groups=mesh['gx'=16,'gy'=8,'gz'=4] {'gz'}, dimensions={0}, use_global_device_ids=true | all-gather | bytes 138240 | tf_op jit(solution)/shard_map/all_gather | solution.py:376
  86.9 0.6 shard_map.94
  (5 shorter events, 0.1 us)
Async XLA Ops:
  2.4 18.2 %collective-permute-start = (bf16[4,8,1024]{2,1,0:T(8,128)(2,1)S(1)}, bf16[4,8,1024]{2,1,0:T(8,128)(2,1)S(1)}, u32[]{:S(2)}, u32[]{:S(2)}) collective-permute-start(bf16[4,8,1024]{2,1,0:T(8,128)(2,1)S(1)} %get-tuple-element.25), channel_id=1, source_target_pairs={{0,32},{32,0},{64,96},{96,64},{128,160},{160,128},{192,224},{224,1... | collective-permute-start | bytes 196616 | tf_op jit(solution)/shard_map/ppermute | solution.py:337
  6.4 14.2 %collective-permute-start.1 = (bf16[4,8,1024]{2,1,0:T(8,128)(2,1)S(1)}, bf16[4,8,1024]{2,1,0:T(8,128)(2,1)S(1)}, u32[]{:S(2)}, u32[]{:S(2)}) collective-permute-start(bf16[4,8,1024]{2,1,0:T(8,128)(2,1)S(1)} %get-tuple-element.26), channel_id=1, source_target_pairs={{0,480},{32,64},{64,32},{96,128},{128,96},{160,192},{192,160},{224... | collective-permute-start | bytes 196616 | tf_op jit(solution)/shard_map/ppermute | solution.py:336
  17.0 23.1 %all-to-all-start = ((bf16[16,8,1728]{2,1,0:T(8,128)(2,1)}), bf16[16,8,1728]{2,1,0:T(8,128)(2,1)S(1)}, u32[]{:S(2)}, u32[]{:S(2)}) async-start(bf16[16,8,1728]{2,1,0:T(8,128)(2,1)} %get-tuple-element.31), calls=%async_computation | async-start | bytes 917504 | tf_op jit(solution)/shard_map/all_to_all | solution.py:409
  20.9 7.0 %collective-permute-start.2 = (bf16[14,2,1024]{2,1,0:T(2,128)(2,1)S(1)}, bf16[14,2,1024]{2,1,0:T(2,128)(2,1)S(1)}, u32[]{:S(2)}, u32[]{:S(2)}) collective-permute-start(bf16[14,2,1024]{2,1,0:T(2,128)(2,1)S(1)} %get-tuple-element.27), channel_id=1, source_target_pairs={{0,28},{4,8},{8,4},{12,16},{16,12},{20,24},{24,20},{28,0},{1,29},{... | collective-permute-start | bytes 172040 | tf_op jit(solution)/shard_map/ppermute | solution.py:336
  26.0 5.2 %collective-permute-start.3 = (bf16[14,2,1024]{2,1,0:T(2,128)(2,1)S(1)}, bf16[14,2,1024]{2,1,0:T(2,128)(2,1)S(1)}, u32[]{:S(2)}, u32[]{:S(2)}) collective-permute-start(bf16[14,2,1024]{2,1,0:T(2,128)(2,1)S(1)} %get-tuple-element.28), channel_id=1, source_target_pairs={{0,4},{4,0},{8,12},{12,8},{16,20},{20,16},{24,28},{28,24},{1,5},{5... | collective-permute-start | bytes 172040 | tf_op jit(solution)/shard_map/ppermute | solution.py:337
  31.3 9.3 %collective-permute-start.4 = (bf16[168,128]{1,0:T(8,128)(2,1)S(1)}, bf16[168,128]{1,0:T(8,128)(2,1)S(1)}, u32[]{:S(2)}, u32[]{:S(2)}) collective-permute-start(bf16[168,128]{1,0:T(8,128)(2,1)S(1)} %get-tuple-element.29), channel_id=1, source_target_pairs={{0,3},{1,2},{2,1},{3,0},{4,7},{5,6},{6,5},{7,4},{8,11},{9,10},{10,... | collective-permute-start | bytes 129032 | tf_op jit(solution)/shard_map/ppermute | solution.py:336
  38.2 3.1 %collective-permute-start.5 = (bf16[168,128]{1,0:T(8,128)(2,1)S(1)}, bf16[168,128]{1,0:T(8,128)(2,1)S(1)}, u32[]{:S(2)}, u32[]{:S(2)}) collective-permute-start(bf16[168,128]{1,0:T(8,128)(2,1)S(1)} %get-tuple-element.30), channel_id=1, source_target_pairs={{0,1},{1,0},{2,3},{3,2},{4,5},{5,4},{6,7},{7,6},{8,9},{9,8},{10,11... | collective-permute-start | bytes 129032 | tf_op jit(solution)/shard_map/ppermute | solution.py:337
  44.5 3.4 %collective-permute-start.6 = (bf16[16,4,1728]{2,1,0:T(4,128)(2,1)S(1)}, bf16[16,4,1728]{2,1,0:T(4,128)(2,1)S(1)}, u32[]{:S(2)}, u32[]{:S(2)}) collective-permute-start(bf16[16,4,1728]{2,1,0:T(4,128)(2,1)S(1)} %get-tuple-element.33), channel_id=1, source_target_pairs={{0,1},{1,0},{2,3},{3,2},{4,5},{5,4},{6,7},{7,6},{8,9},{9,8},{10,11... | collective-permute-start | bytes 663560 | tf_op jit(solution)/shard_map/ppermute | solution.py:369
